TPU v7x, 256 devices: a whole 4x4x8 slice. The times are simulated.
256 devices in a mesh: shot: 8 (over y, z_lo), space: 32 (over x, z_hi, core).
Axes of the slice: x: 4, y: 4, z: 8 (z_hi: 4, z_lo: 2; z = z_hi * 2 + z_lo), core: 2. Of those that a mesh axis runs over, the one named last changes fastest.
Arguments:
- wave_prev: float32 [8, 512, 128, 128], P('shot', 'space'), may hold values from -6 to 6
- wave_now: float32 [8, 512, 128, 128], P('shot', 'space'), may hold values from -6 to 6
- velocity: float32 [512, 128, 128], P('space'), may hold values from 0.05 to 0.2
- probe_panel: float32 [4, 512, 128, 128], P(None, 'space', 'shot'), may hold values from -6 to 6
- source_depth: int32 [8], P('shot'), may hold values from 0 to 511
- source_column: int32 [8], P('shot'), may hold values from 0 to 16383
- source_strength: float32 [8], P('shot'), may hold values from 2 to 6
- receiver_wells: int32 [8, 512], P('shot'), may hold values from 0 to 16383
Outputs:
- hessian_action: float32 [4, 512, 128, 128], P(None, 'space', 'shot')
All inputs are finite; a program needn't handle non-finite values.
Results may differ from a plain program's by a relative error of at most 0.0003.
Values sent between devices are 32-bit elements; how exact they have to be, the bound alone decides.
No kernel may reach another device: no remote copies, remote signals or barrier semaphores. Data moves between devices by JAX's collectives and lax.ppermute only.
A program may use at most 128 MiB of HBM per device.

v0:
```python
import functools

import jax
import jax.numpy as jnp
from jax import lax
from jax.experimental import pallas as pl
from jax.experimental.pallas import tpu as pltpu
from jax.sharding import PartitionSpec as P


CENTER = 3.0 * (-205.0 / 72.0)
WEIGHTS = (8.0 / 5.0, -1.0 / 5.0, 8.0 / 315.0, -1.0 / 560.0)
SCALE = WEIGHTS[0]
RATIOS = tuple(w / SCALE for w in WEIGHTS)
F32 = jnp.float32
BF16 = jnp.bfloat16


def halves(value):
    high = value.astype(BF16)
    low = (value - high.astype(F32)).astype(BF16)
    return high, low


def band(distance):
    out = jnp.zeros(distance.shape, F32)
    for k in range(1, 5):
        out = jnp.where(distance == k, RATIOS[k - 1], out)
    return out


def plane_laplace(planes, z, matrix):
    here = planes(z)
    high, low = halves(here)
    along_y = jnp.dot(
        jnp.concatenate([high, low], axis=1),
        jnp.concatenate([matrix, matrix], axis=0),
        preferred_element_type=F32,
    )
    along_x = jnp.dot(
        jnp.concatenate([matrix, matrix], axis=1),
        jnp.concatenate([high, low], axis=0),
        preferred_element_type=F32,
    )
    total = CENTER * here + SCALE * (along_y + along_x)
    for k in range(1, 5):
        total = total + WEIGHTS[k - 1] * (planes(z - k) + planes(z + k))
    return total


def plane_reader(count, low_ref, ref, high_ref):
    def planes(i):
        if i < 0:
            return low_ref[i + 4]
        if i >= count:
            return high_ref[i - count]
        return ref[i]

    return planes


def stencil_matrix(width):
    rows = lax.broadcasted_iota(jnp.int32, (width, width), 0)
    cols = lax.broadcasted_iota(jnp.int32, (width, width), 1)
    return band(jnp.abs(rows - cols)).astype(BF16)


def step_kernel(count, slab_ref, depth_ref, column_ref, strength_ref, now_ref, low_ref, high_ref, prev_ref, vel_ref, born_ref, lap_ref, next_ref, first_ref, last_ref):
    width = now_ref.shape[1]
    matrix = stencil_matrix(width)
    planes = plane_reader(count, low_ref, now_ref, high_ref)
    rows = lax.broadcasted_iota(jnp.int32, (width, width), 0)
    cols = lax.broadcasted_iota(jnp.int32, (width, width), 1)
    hit = (rows * width + cols) == column_ref[0]
    source_z = depth_ref[0] - slab_ref[0] * count
    spot = jnp.where(hit, strength_ref[0], 0.0)
    for z in range(count):
        lap = plane_laplace(planes, z, matrix)
        born = vel_ref[z] * lap
        upcoming = 2.0 * now_ref[z] - prev_ref[z] + born
        upcoming = upcoming + jnp.where(source_z == z, 1.0, 0.0) * spot
        lap_ref[z] = lap
        born_ref[z] = born
        next_ref[z] = upcoming
        if z < 4:
            first_ref[z] = upcoming
        if z >= count - 4:
            last_ref[z - (count - 4)] = upcoming


def second_kernel(count, strips, wells_ref, next_ref, low_ref, high_ref, born_ref, lap_ref, buf_ref):
    width = next_ref.shape[1]
    matrix = stencil_matrix(width)
    planes = plane_reader(count, low_ref, next_ref, high_ref)
    for z in range(count):
        both = 2.0 * lap_ref[z] + plane_laplace(planes, z, matrix)
        born = born_ref[z]
        for strip in range(strips):
            for half in range(2):
                x = strip * 16 + half * 8
                row = half * count * 8 + z * 8
                buf_ref[strip, row : row + 8, :] = born[x : x + 8]
                buf_ref[strip, 2 * count * 8 + row : 2 * count * 8 + row + 8, :] = both[x : x + 8]
    n_rows = wells_ref.shape[1] // width
    for strip in range(strips):
        for i in range(n_rows):
            row = 4 * count * 8 + i
            buf_ref[strip, row : row + 1, :] = wells_ref[:, i * width : (i + 1) * width].astype(F32)
        buf_ref[strip, 4 * count * 8 + n_rows :, :] = jnp.zeros((buf_ref.shape[1] - 4 * count * 8 - n_rows, width), F32)


def masks_of(wells, width):
    x_row = wells // width
    y_row = wells - x_row * width
    y_ids = lax.broadcasted_iota(jnp.int32, (width, wells.shape[1]), 0)
    spot = jnp.where(y_ids == y_row, 1.0, 0.0).astype(BF16)
    side = jnp.dot(stencil_matrix(width), spot, preferred_element_type=F32).astype(BF16)
    return x_row, spot, side


def fill(x_row, spot, side, x, spot_ref, lap_ref, row):
    width = spot.shape[0]
    distance = jnp.abs(x_row - x)
    at = jnp.where(distance == 0, 1.0, 0.0).astype(BF16)
    near = band(distance).astype(BF16)
    spot_ref[row : row + width, :] = spot * at
    lap_ref[row : row + width, :] = spot * near + side * at


def strip_of(me, rounds, plan, i):
    shift = plan[1] + plan[2] * i
    flip = plan[3] + plan[4] * i
    row = me // 2
    return lax.rem(row - shift + rounds, rounds) * 2 + ((me - 2 * row) ^ flip)


def gather_kernel(count, probes, rounds, plans, counts, started, me_ref, wells_ref, vel_ref, buf_ref, *refs):
    n_in = len(plans)
    m_refs = refs[:n_in]
    refs = refs[n_in:]
    if started:
        start_refs, refs = refs[:3], refs[3:]
    first_ref, sigma_ref, v_ref = refs[:3]
    spot_ref, lap_ref, left_ref = refs[-3:]
    width = buf_ref.shape[2]
    rows = probes * count
    x_row, spot, side = masks_of(wells_ref[...], width)
    if started:
        for ref, start_ref in zip((first_ref, sigma_ref, v_ref), start_refs):
            ref[...] = start_ref[...]
    else:
        for ref in (first_ref, sigma_ref, v_ref):
            ref[...] = jnp.zeros_like(ref)
    for m_ref, plan, pieces in zip(m_refs, plans, counts):

        def body(i, carry, m_ref=m_ref, plan=plan):
            half = plan[0]
            strip = strip_of(me_ref[0], rounds, plan, i)
            for x in range(8):
                fill(x_row, spot, side, strip * 16 + half * 8 + x, spot_ref, lap_ref, x * width)
                m = m_ref[i, pl.ds(x, rows, stride=8), :]
                born = buf_ref[strip, pl.ds(half * count * 8 + x, count, stride=8), :]
                both = buf_ref[strip, pl.ds((2 + half) * count * 8 + x, count, stride=8), :]
                vel = vel_ref[pl.ds(strip * 16 + half * 8 + x, count, stride=width), :]
                centre = (both + CENTER * born) * (1.0 / SCALE)
                first = m * jnp.concatenate([born] * probes, axis=0)
                other = m * jnp.concatenate([centre] * probes, axis=0)
                columns = slice(x * width, (x + 1) * width)
                for j, value in enumerate((first, other)):
                    high, low = halves(value)
                    left_ref[2 * j * rows : (2 * j + 1) * rows, columns] = high
                    left_ref[(2 * j + 1) * rows : (2 * j + 2) * rows, columns] = low
                high, low = halves(vel)
                left_ref[4 * rows : 4 * rows + count, columns] = high
                left_ref[4 * rows + count :, columns] = low
            out = jnp.dot(left_ref[...], spot_ref[...], preferred_element_type=F32)
            lap = jnp.dot(left_ref[: 2 * rows, :], lap_ref[...], preferred_element_type=F32)
            first_ref[...] += out[:rows] + out[rows : 2 * rows]
            sigma_ref[...] += (out[2 * rows : 3 * rows] + out[3 * rows : 4 * rows]) + (lap[:rows] + lap[rows:])
            v_ref[...] += out[4 * rows : 4 * rows + count] + out[4 * rows + count :]
            return carry

        lax.fori_loop(0, pieces, body, 0)
    if started:
        for send_ref, top in ((refs[3], False), (refs[4], True)):
            for p in range(probes):
                z = p * count + (count - 8 if top else 0)
                send_ref[8 * p : 8 * p + 8, :] = first_ref[z : z + 8, :]
                z = p * count + (count - 4 if top else 0)
                send_ref[8 * probes + 4 * p : 8 * probes + 4 * p + 4, :] = sigma_ref[z : z + 4, :]
            z = count - 4 if top else 0
            send_ref[12 * probes : 12 * probes + 4, :] = v_ref[z : z + 4, :]
            send_ref[12 * probes + 4 :, :] = jnp.zeros((4, send_ref.shape[1]), F32)


def late_kernel(count, probes, first_ref, sigma_ref, v_ref, low_ref, high_ref, late_ref, f_ref, s_ref, w_ref):
    deep = count + 8
    top = 12 * probes
    w_ref[:4, :] = low_ref[top : top + 4, :]
    w_ref[4 : 4 + count, :] = v_ref[...]
    w_ref[4 + count :, :] = high_ref[top : top + 4, :]
    w = w_ref[...]
    w = w * w
    for p in range(probes):
        f_ref[:8, :] = low_ref[8 * p : 8 * p + 8, :]
        f_ref[8 : 8 + count, :] = first_ref[p * count : (p + 1) * count, :]
        f_ref[8 + count :, :] = high_ref[8 * p : 8 * p + 8, :]
        z = 8 * probes + 4 * p
        s_ref[:4, :] = low_ref[z : z + 4, :]
        s_ref[4 : 4 + count, :] = sigma_ref[p * count : (p + 1) * count, :]
        s_ref[4 + count :, :] = high_ref[z : z + 4, :]
        sigma = SCALE * s_ref[...]
        for k in range(1, 5):
            sigma = sigma + WEIGHTS[k - 1] * (f_ref[4 - k : 4 - k + deep, :] + f_ref[4 + k : 4 + k + deep, :])
        late_ref[p * deep : (p + 1) * deep, :] = w * sigma


def image_kernel(count, probes, flips, scale, started, me_ref, buf_ref, m_ref, *refs):
    n = len(flips)
    late_refs, refs = refs[:n], refs[n:]
    if started:
        start_ref, refs = refs[0], refs[1:]
    out_ref, late_ref, spot_ref, lap_ref, left_ref, side_ref = refs
    width = m_ref.shape[1]
    rows = probes * count
    step = pl.program_id(0)
    n_wells = late_ref.shape[1]

    @pl.when(step == 0)
    def _():
        out_ref[...] = start_ref[...] if started else jnp.zeros_like(out_ref)

    for i in range(n):

        @pl.when(step == i)
        def _(i=i):
            late_ref[...] = late_refs[i][...]

    top = 4 * count * 8
    wells = jnp.concatenate([buf_ref[0, top + i : top + i + 1, :] for i in range(n_wells // width)], axis=1)
    x_row, spot, side = masks_of(wells.astype(jnp.int32), width)
    for p in range(probes):
        top = p * (count + 8)
        here = late_ref[top + 4 : top + 4 + count, :]
        along_z = CENTER * here
        for k in range(1, 5):
            along_z = along_z + WEIGHTS[k - 1] * (
                late_ref[top + 4 - k : top + 4 - k + count, :] + late_ref[top + 4 + k : top + 4 + k + count, :]
            )
        for j, value in enumerate((along_z, here)):
            high, low = halves(value)
            left_ref[2 * j * rows + p * count : 2 * j * rows + (p + 1) * count, :] = high
            left_ref[(2 * j + 1) * rows + p * count : (2 * j + 1) * rows + (p + 1) * count, :] = low
        high, low = halves(SCALE * here)
        side_ref[p * count : (p + 1) * count, :] = high
        side_ref[rows + p * count : rows + (p + 1) * count, :] = low
    left_ref[4 * rows :, :] = jnp.ones((count, n_wells), BF16)
    contract = (((1,), (1,)), ((), ()))
    for half in range(2):
        for pair in range(4):
            slot = pair % 2
            for j in range(2):
                x = half * 8 + pair * 2 + j
                fill(x_row, spot, side, me_ref[0] * 16 + x, spot_ref.at[slot], lap_ref.at[slot], j * width)
            out = lax.dot_general(left_ref[...], spot_ref[slot], contract, preferred_element_type=F32)
            lap = lax.dot_general(side_ref[...], lap_ref[slot], contract, preferred_element_type=F32)
            field = (out[:rows] + out[rows : 2 * rows]) + (lap[:rows] + lap[rows:])
            late = out[2 * rows : 3 * rows] + out[3 * rows : 4 * rows]
            hits = out[4 * rows :]
            for j in range(2):
                x = pair * 2 + j
                columns = slice(j * width, (j + 1) * width)
                born = buf_ref[0, pl.ds(half * count * 8 + x, count, stride=8), :]
                both = buf_ref[0, pl.ds((2 + half) * count * 8 + x, count, stride=8), :]
                seen = hits[:, columns] * born
                m_rows = pl.ds(half * 8 + x, rows, stride=16)
                tile = lambda value: jnp.concatenate([value] * probes, axis=0)
                out_ref[m_rows, :] += (
                    tile(born) * (field[:, columns] + tile(seen) * m_ref[m_rows, :]) + tile(both) * late[:, columns]
                )

    if scale != 1.0:

        @pl.when(step == n - 1)
        def _():
            out_ref[...] = out_ref[...] * scale


VMEM = pl.BlockSpec(memory_space=pltpu.VMEM)
SMEM = pl.BlockSpec(memory_space=pltpu.SMEM)


def spread(low_layers, high_layers, axis="space"):
    count = lax.axis_size(axis)
    forward = [(i, i + 1) for i in range(count - 1)]
    backward = [(i + 1, i) for i in range(count - 1)]
    return lax.ppermute(high_layers, axis, forward), lax.ppermute(low_layers, axis, backward)


def slab(wave_prev, wave_now, velocity, probe_panel, source_depth, source_column, source_strength, receiver_wells):
    count, width = wave_now.shape[1], wave_now.shape[2]
    probes = probe_panel.shape[0]
    strips = lax.axis_size("shot")
    n_wells = receiver_wells.shape[1]
    rows = probes * count
    me = lax.axis_index("shot").reshape(1).astype(jnp.int32)
    params = pltpu.CompilerParams(vmem_limit_bytes=60 * 1024 * 1024)

    rounds = strips // 2
    swap = [(i, i ^ 1) for i in range(strips)]

    def sent(value, pairs):
        return lax.ppermute(value, "shot", pairs)

    def ring(shift):
        return [(i, (i + 2 * shift) % strips) for i in range(strips)]

    part_a, part_b = probe_panel[:, :, :8], probe_panel[:, :, 8:]
    now_low, now_high = spread(wave_now[0, :4], wave_now[0, count - 4 :])
    a_swapped = sent(part_a, swap)
    b_ring = [sent(part_b, ring(s)) for s in range(1, rounds)]
    a_pair = jnp.stack([part_a, a_swapped])
    b_all = jnp.stack([part_b] + b_ring)
    a_ring = [sent(a_pair, ring(s)) for s in range(1, rounds)]
    b_other = sent(b_all, swap)

    slab_id = lax.axis_index("space").reshape(1).astype(jnp.int32)
    plane = jax.ShapeDtypeStruct((count, width, width), F32)
    edge = jax.ShapeDtypeStruct((4, width, width), F32)
    born, lap, upcoming, up_first, up_last = pl.pallas_call(
        functools.partial(step_kernel, count),
        out_shape=(plane, plane, plane, edge, edge),
        in_specs=[SMEM] * 4 + [VMEM] * 5,
        out_specs=(VMEM,) * 5,
        compiler_params=params,
        name="step_kernel",
    )(slab_id, source_depth, source_column, source_strength, wave_now[0], now_low, now_high, wave_prev[0], velocity)
    up_low, up_high = spread(up_first, up_last)

    buf_rows = 4 * count * 8 + 8
    buf = pl.pallas_call(
        functools.partial(second_kernel, count, strips),
        out_shape=jax.ShapeDtypeStruct((strips, buf_rows, width), F32),
        in_specs=[VMEM] * 6,
        out_specs=VMEM,
        compiler_params=params,
        name="second_kernel",
    )(receiver_wells, upcoming, up_low, up_high, born, lap)
    shared = lax.all_to_all(buf, "shot", 0, 0, tiled=True)

    compact = jax.ShapeDtypeStruct((rows, n_wells), F32)
    compact_v = jax.ShapeDtypeStruct((count, n_wells), F32)
    edge_rows = 12 * probes + 8

    def gather(parts, plans, start=()):
        parts = [part.reshape(-1, rows * 8, width) for part in parts]
        counts = tuple(part.shape[0] for part in parts)
        out_shape = (compact, compact, compact_v)
        if start:
            out_shape += (jax.ShapeDtypeStruct((edge_rows, n_wells), F32),) * 2
        return pl.pallas_call(
            functools.partial(gather_kernel, count, probes, rounds, plans, counts, bool(start)),
            out_shape=out_shape,
            in_specs=[SMEM] + [VMEM] * (3 + len(parts) + len(start)),
            out_specs=(VMEM,) * len(out_shape),
            scratch_shapes=[
                pltpu.VMEM((8 * width, n_wells), BF16),
                pltpu.VMEM((8 * width, n_wells), BF16),
                pltpu.VMEM((4 * rows + 2 * count, 8 * width), BF16),
            ],
            compiler_params=params,
        )(me, receiver_wells, velocity.reshape(count * width, width), buf, *parts, *start)

    own_plans = ((0, 0, 0, 0, 0), (0, 0, 0, 1, 0)) + tuple((1, s, 0, 0, 0) for s in range(rounds))
    own = gather([part_a, a_swapped, part_b] + b_ring, own_plans)
    far_plans = tuple((0, s, 0, 0, 1) for s in range(1, rounds)) + ((1, 0, 1, 1, 0),)
    first, sigma, vel, send_low, send_high = gather(a_ring + [b_other], far_plans, own)
    low, high = spread(send_low, send_high)
    deep = count + 8
    late = pl.pallas_call(
        functools.partial(late_kernel, count, probes),
        out_shape=jax.ShapeDtypeStruct((probes * deep, n_wells), F32),
        in_specs=[VMEM] * 5,
        out_specs=VMEM,
        scratch_shapes=[
            pltpu.VMEM((count + 16, n_wells), F32),
            pltpu.VMEM((deep, n_wells), F32),
            pltpu.VMEM((deep, n_wells), F32),
        ],
        compiler_params=params,
        name="late_kernel",
    )(first, sigma, vel, low, high)

    late_from = {0: late}
    for flip in NEAR + FAR:
        late_from[flip] = sent(late, [(i, i ^ flip) for i in range(strips)])
    panel = probe_panel.reshape(rows * 16, width)

    def image(source, flips, scale, start=()):
        whole = pl.BlockSpec((rows * 16, width), lambda s, me: (0, 0))

        def shot_block(s, me):
            flip = flips[-1]
            for i in range(len(flips) - 2, -1, -1):
                flip = jnp.where(s == i, flips[i], flip)
            return (me[0] ^ flip, 0, 0)

        return pl.pallas_call(
            functools.partial(image_kernel, count, probes, flips, scale, bool(start)),
            out_shape=jax.ShapeDtypeStruct((rows * 16, width), F32),
            grid_spec=pltpu.PrefetchScalarGridSpec(
                num_scalar_prefetch=1,
                grid=(len(flips),),
                in_specs=[pl.BlockSpec((1, buf_rows, width), shot_block), whole]
                + [pl.BlockSpec((probes * deep, n_wells), lambda s, me: (0, 0))] * len(flips)
                + [whole] * len(start),
                out_specs=whole,
                scratch_shapes=[
                    pltpu.VMEM((probes * deep, n_wells), F32),
                    pltpu.VMEM((2, 2 * width, n_wells), BF16),
                    pltpu.VMEM((2, 2 * width, n_wells), BF16),
                    pltpu.VMEM((4 * rows + count, n_wells), BF16),
                    pltpu.VMEM((2 * rows, n_wells), BF16),
                ],
            ),
            compiler_params=params,
        )(me, source, panel, *[late_from[flip] for flip in flips], *start)

    total = image(buf, (0,), 1.0)
    total = image(shared, NEAR, 1.0, (total,))
    total = image(shared, FAR, 1.0 / strips, (total,))
    return total.reshape(probe_panel.shape)


NEAR = (1, 2, 6)
FAR = (3, 7, 4, 5)


def solution(mesh):
    return jax.shard_map(
        slab,
        mesh=mesh,
        in_specs=(
            P("shot", "space", None, None),
            P("shot", "space", None, None),
            P("space", None, None),
            P(None, "space", "shot", None),
            P("shot"),
            P("shot"),
            P("shot"),
            P("shot", None),
        ),
        out_specs=P(None, "space", "shot", None),
        check_vma=False,
    )
```

profile of v0, /device:TPU:1, one launch (start us, length us, event | category | flops | bytes accessed | tf_op | source)
XLA Modules:
  0.0 211.3 jit_solution(17420943370030722362)
XLA Ops:
  0.0 1.1 slice_bitcast_fusion
  1.1 6.3 %collective-permute-start = (f32[4,128,128]{2,1,0:T(8,128)S(1)}, f32[4,128,128]{2,1,0:T(8,128)S(1)}, u32[]{:S(2)}, u32[]{:S(2)}) collective-permute-start(f32[4,128,128]{2,1,0:T(8,128)S(1)} %get-tuple-element.32), channel_id=1, source_target_pairs={{0,1},{1,2},{2,3},{3,4},{4,5},{5,6},{6,7},{7,8},{8,9},{9,10},{10,1... | collective-permute-start | bytes 786440 | tf_op jit(solution)/shard_map/ppermute | solution.py:297
  7.4 1.9 collective-permute-start.1
  11.3 7.5 %collective-permute-done.1.high_ref = f32[4,128,128]{2,1,0:T(8,128)S(1)} collective-permute-done((f32[4,128,128]{2,1,0:T(8,128)S(1)}, f32[4,128,128]{2,1,0:T(8,128)S(1)}, u32[]{:S(2)}, u32[]{:S(2)}) %collective-permute-start.1) | collective-permute-done | bytes 262176 | tf_op jit(solution)/shard_map/ppermute | solution.py:297
  18.8 0.7 copy-done.9
  19.5 5.0 %step_kernel.1 = (f32[16,128,128]{2,1,0:T(8,128)}, f32[16,128,128]{2,1,0:T(8,128)}, f32[16,128,128]{2,1,0:T(8,128)}, f32[4,128,128]{2,1,0:T(8,128)}, f32[4,128,128]{2,1,0:T(8,128)}) custom-call(s32[1]{0:T(128)} %bitcast.1.slab_ref, s32[1]{0:T(128)S(6)} %copy.9.depth_ref, s32[1]{0:T(128)S(6)} %copy.10.column_ref, f32[1]{0:T(128)S(6)} %copy.11.strength_ref, ...), custom_call_target="tpu_custom_call" | custom-call | tf_op jit(solution)/shard_map/step_kernel/pallas_call | solution.py:330
  24.4 1.9 collective-permute-start.2
  26.3 2.4 %collective-permute-start.3 = (f32[4,128,128]{2,1,0:T(8,128)}, f32[4,128,128]{2,1,0:T(8,128)S(1)}, u32[]{:S(2)}, u32[]{:S(2)}) collective-permute-start(f32[4,128,128]{2,1,0:T(8,128)} %get-tuple-element.20), channel_id=1, source_target_pairs={{1,0},{2,1},{3,2},{4,3},{5,4},{6,5},{7,6},{8,7},{9,8},{10,9},{11,1... | collective-permute-start | bytes 786440 | tf_op jit(solution)/shard_map/ppermute | solution.py:297
  28.8 4.0 %collective-permute-done.2.low_ref = f32[4,128,128]{2,1,0:T(8,128)S(1)} collective-permute-done((f32[4,128,128]{2,1,0:T(8,128)}, f32[4,128,128]{2,1,0:T(8,128)S(1)}, u32[]{:S(2)}, u32[]{:S(2)}) %collective-permute-start.2) | collective-permute-done | bytes 262176 | tf_op jit(solution)/shard_map/ppermute | solution.py:297
  32.8 8.2 %collective-permute-done.3.high_ref = f32[4,128,128]{2,1,0:T(8,128)S(1)} collective-permute-done((f32[4,128,128]{2,1,0:T(8,128)}, f32[4,128,128]{2,1,0:T(8,128)S(1)}, u32[]{:S(2)}, u32[]{:S(2)}) %collective-permute-start.3) | collective-permute-done | bytes 262176 | tf_op jit(solution)/shard_map/ppermute | solution.py:297
  41.0 0.7 copy-done.11
  41.7 4.5 %second_kernel.1.buf_ref = f32[8,520,128]{2,1,0:T(8,128)} custom-call(s32[1,512]{1,0:T(1,128)} %wells_ref.5, f32[16,128,128]{2,1,0:T(8,128)} %get-tuple-element.18.next_ref, f32[4,128,128]{2,1,0:T(8,128)} %copy-done.10, f32[4,128,128]{2,1,0:T(8,128)} %copy-done.11, f32[16,128,128]{2,1,0:T(8,128)} %get-tuple-element.21.born_ref, ...), custom_call_target="tpu_custom_call" | custom-call | tf_op jit(solution)/shard_map/second_kernel/pallas_call | solution.py:341
  46.2 4.3 %all-to-all-start = ((f32[8,520,128]{2,1,0:T(8,128)}), f32[8,520,128]{2,1,0:T(8,128)S(1)}, u32[]{:S(2)}, u32[]{:S(2)}) async-start(f32[8,520,128]{2,1,0:T(8,128)} %second_kernel.1.buf_ref), calls=%async_computation | async-start | bytes 4259840 | tf_op jit(solution)/shard_map/all_to_all | solution.py:349
  50.7 1.5 collective-permute-start.8
  52.2 2.4 %collective-permute-start.9 = (f32[4,16,8,128]{3,2,1,0:T(8,128)S(1)}, f32[4,16,8,128]{3,2,1,0:T(8,128)S(1)}, u32[]{:S(2)}, u32[]{:S(2)}) collective-permute-start(f32[4,16,8,128]{3,2,1,0:T(8,128)S(1)} %get-tuple-element.35), channel_id=1, source_target_pairs={{0,128},{32,160},{64,192},{96,224},{128,0},{160,32},{192,64},{224,... | collective-permute-start | bytes 786440 | tf_op jit(solution)/shard_map/ppermute | solution.py:313
  54.6 1.2 collective-permute-start.10
  55.8 20.1 %collective-permute-done.8 = f32[4,16,8,128]{3,2,1,0:T(8,128)S(1)} collective-permute-done((f32[4,16,8,128]{3,2,1,0:T(8,128)S(1)}, f32[4,16,8,128]{3,2,1,0:T(8,128)S(1)}, u32[]{:S(2)}, u32[]{:S(2)}) %collective-permute-start.8) | collective-permute-done | bytes 262176 | tf_op jit(solution)/shard_map/ppermute | solution.py:313
  75.9 3.2 %collective-permute-done.9 = f32[4,16,8,128]{3,2,1,0:T(8,128)S(1)} collective-permute-done((f32[4,16,8,128]{3,2,1,0:T(8,128)S(1)}, f32[4,16,8,128]{3,2,1,0:T(8,128)S(1)}, u32[]{:S(2)}, u32[]{:S(2)}) %collective-permute-start.9) | collective-permute-done | bytes 262176 | tf_op jit(solution)/shard_map/ppermute | solution.py:313
  79.1 1.2 collective-permute-start.11
  80.7 25.5 %collective-permute-done.4 = f32[4,16,8,128]{3,2,1,0:T(8,128)S(1)} collective-permute-done((f32[4,16,8,128]{3,2,1,0:T(8,128)S(1)}, f32[4,16,8,128]{3,2,1,0:T(8,128)S(1)}, u32[]{:S(2)}, u32[]{:S(2)}) %collective-permute-start.4) | collective-permute-done | bytes 262176 | tf_op jit(solution)/shard_map/ppermute | solution.py:313
  106.2 0.7 copy-done.4
  106.9 0.8 pad_maximum_fusion.1
  107.7 2.3 %collective-permute-start.6 = (f32[2,4,16,8,128]{4,3,2,1,0:T(8,128)}, f32[2,4,16,8,128]{4,3,2,1,0:T(8,128)}, u32[]{:S(2)}, u32[]{:S(2)}) collective-permute-start(f32[2,4,16,8,128]{4,3,2,1,0:T(8,128)} %pad_maximum_fusion.1), channel_id=1, source_target_pairs={{0,128},{32,160},{64,192},{96,224},{128,0},{160,32},{192,64},{224,... | collective-permute-start | bytes 1572872 | tf_op jit(solution)/shard_map/ppermute | solution.py:313
  110.1 1.3 collective-permute-start.7
  111.3 6.4 %shard_map.82 = (f32[64,512]{1,0:T(8,128)}, f32[64,512]{1,0:T(8,128)}, f32[16,512]{1,0:T(8,128)}) custom-call(s32[1]{0:T(128)} %bitcast.me_ref, s32[1,512]{1,0:T(1,128)} %wells_ref.5, f32[2048,128]{1,0:T(8,128)} %bitcast.29, f32[8,520,128]{2,1,0:T(8,128)} %second_kernel.1.buf_ref, f32[1,512,128]{2,1,0:T(8,128)} %bitcast.37, f32[1,512,128]{2,1,0:T(8,128)} %bitcast.39, ...), custom_call_target="tpu_custom_call" | custom-call | tf_op jit(solution)/shard_map/pallas_call | solution.py:361
  117.8 14.1 %collective-permute-done.5 = f32[2,4,16,8,128]{4,3,2,1,0:T(8,128)} collective-permute-done((f32[2,4,16,8,128]{4,3,2,1,0:T(8,128)}, f32[2,4,16,8,128]{4,3,2,1,0:T(8,128)}, u32[]{:S(2)}, u32[]{:S(2)}) %collective-permute-start.5) | collective-permute-done | bytes 524320 | tf_op jit(solution)/shard_map/ppermute | solution.py:313
  131.9 0.9 collective-permute-done.7
  132.8 11.4 %shard_map.83 = (f32[64,512]{1,0:T(8,128)}, f32[64,512]{1,0:T(8,128)}, f32[16,512]{1,0:T(8,128)}, f32[56,512]{1,0:T(8,128)}, f32[56,512]{1,0:T(8,128)}) custom-call(s32[1]{0:T(128)} %bitcast.me_ref, s32[1,512]{1,0:T(1,128)} %wells_ref.5, f32[2048,128]{1,0:T(8,128)} %bitcast.30, f32[8,520,128]{2,1,0:T(8,128)} %second_kernel.1.buf_ref, ...), custom_call_target="tpu_custom_call" | custom-call | tf_op jit(solution)/shard_map/pallas_call | solution.py:361
  144.2 17.4 %collective-permute-start.12 = (f32[56,512]{1,0:T(8,128)}, f32[56,512]{1,0:T(8,128)S(1)}, u32[]{:S(2)}, u32[]{:S(2)}) collective-permute-start(f32[56,512]{1,0:T(8,128)} %get-tuple-element.29), channel_id=1, source_target_pairs={{0,1},{1,2},{2,3},{3,4},{4,5},{5,6},{6,7},{7,8},{8,9},{9,10},{10,1... | collective-permute-start | bytes 344072 | tf_op jit(solution)/shard_map/ppermute | solution.py:297
  161.6 1.9 collective-permute-start.13
  163.7 5.1 %collective-permute-done.13.high_ref = f32[56,512]{1,0:T(8,128)S(1)} collective-permute-done((f32[56,512]{1,0:T(8,128)}, f32[56,512]{1,0:T(8,128)S(1)}, u32[]{:S(2)}, u32[]{:S(2)}) %collective-permute-start.13) | collective-permute-done | bytes 114720 | tf_op jit(solution)/shard_map/ppermute | solution.py:297
  168.8 0.6 copy-done.20
  169.5 2.0 late_kernel.1.refs_0_
  171.5 1.8 collective-permute-start.18
  173.3 1.0 collective-permute-start.19
  174.3 1.7 collective-permute-start.20
  175.9 0.6 collective-permute-start.14
  176.5 1.8 collective-permute-start.15
  178.3 3.0 %collective-permute-start.16 = (f32[96,512]{1,0:T(8,128)}, f32[96,512]{1,0:T(8,128)S(1)}, u32[]{:S(2)}, u32[]{:S(2)}) collective-permute-start(f32[96,512]{1,0:T(8,128)} %late_kernel.1.refs_0_), channel_id=1, source_target_pairs={{0,128},{32,160},{64,192},{96,224},{128,0},{160,32},{192,64},{224,... | collective-permute-start | bytes 589832 | tf_op jit(solution)/shard_map/ppermute | solution.py:313
  181.3 0.6 collective-permute-done.19.refs_1_
  181.9 2.8 %collective-permute-start.17 = (f32[96,512]{1,0:T(8,128)}, f32[96,512]{1,0:T(8,128)S(1)}, u32[]{:S(2)}, u32[]{:S(2)}) collective-permute-start(f32[96,512]{1,0:T(8,128)} %late_kernel.1.refs_0_), channel_id=1, source_target_pairs={{0,160},{32,128},{64,224},{96,192},{128,32},{160,0},{192,96},{224,... | collective-permute-start | bytes 589832 | tf_op jit(solution)/shard_map/ppermute | solution.py:313
  184.7 4.0 %shard_map.84.refs_3_ = f32[1024,128]{1,0:T(8,128)} custom-call(s32[1]{0:T(128)} %bitcast.me_ref, f32[8,520,128]{2,1,0:T(8,128)} %second_kernel.1.buf_ref, f32[1024,128]{1,0:T(8,128)} %bitcast.31, f32[96,512]{1,0:T(8,128)} %late_kernel.1.refs_0_), custom_call_target="tpu_custom_call" | custom-call | tf_op jit(solution)/shard_map/pallas_call | solution.py:408
  188.7 0.7 copy-done.17
  189.3 1.4 copy-done
  190.7 8.5 %shard_map.85.refs_4_ = f32[1024,128]{1,0:T(8,128)} custom-call(s32[1]{0:T(128)} %bitcast.me_ref, f32[8,520,128]{2,1,0:T(8,128)} %copy-done, f32[1024,128]{1,0:T(8,128)} %bitcast.32, f32[96,512]{1,0:T(8,128)} %copy-done.14, f32[96,512]{1,0:T(8,128)} %copy-done.16, f32[96,512]{1,0:T(8,128)} %copy-done.17, f32[1024,128]{1,0:T(8,128)} %shard_map.84.refs_3_), custom_call_target="tpu_custom_call" | custom-call | tf_op jit(solution)/shard_map/pallas_call | solution.py:408
  199.2 0.6 copy-done.12
  200.0 0.7 copy-done.18
  200.7 10.6 %shard_map.86 = f32[1024,128]{1,0:T(8,128)} custom-call(s32[1]{0:T(128)} %bitcast.me_ref, f32[8,520,128]{2,1,0:T(8,128)} %copy-done, f32[1024,128]{1,0:T(8,128)} %bitcast.33, f32[96,512]{1,0:T(8,128)} %copy-done.12, f32[96,512]{1,0:T(8,128)} %copy-done.13, f32[96,512]{1,0:T(8,128)} %copy-done.15, f32[96,512]{1,0:T(8,128)} %copy-done.18, ...), custom_call_target="tpu_custom_call" | custom-call | tf_op jit(solution)/shard_map/pallas_call | solution.py:408
  (50 shorter events, 0.9 us)
Async XLA Ops:
  1.1 10.2 %collective-permute-start = (f32[4,128,128]{2,1,0:T(8,128)S(1)}, f32[4,128,128]{2,1,0:T(8,128)S(1)}, u32[]{:S(2)}, u32[]{:S(2)}) collective-permute-start(f32[4,128,128]{2,1,0:T(8,128)S(1)} %get-tuple-element.32), channel_id=1, source_target_pairs={{0,1},{1,2},{2,3},{3,4},{4,5},{5,6},{6,7},{7,8},{8,9},{9,10},{10,1... | collective-permute-start | bytes 786440 | tf_op jit(solution)/shard_map/ppermute | solution.py:297
  7.4 11.4 %collective-permute-start.1 = (f32[4,128,128]{2,1,0:T(8,128)S(1)}, f32[4,128,128]{2,1,0:T(8,128)S(1)}, u32[]{:S(2)}, u32[]{:S(2)}) collective-permute-start(f32[4,128,128]{2,1,0:T(8,128)S(1)} %get-tuple-element.31), channel_id=1, source_target_pairs={{1,0},{2,1},{3,2},{4,3},{5,4},{6,5},{7,6},{8,7},{9,8},{10,9},{11,1... | collective-permute-start | bytes 786440 | tf_op jit(solution)/shard_map/ppermute | solution.py:297
  11.2 7.5 %copy-start.8 = (f32[4,128,128]{2,1,0:T(8,128)}, f32[4,128,128]{2,1,0:T(8,128)S(1)}, u32[]{:S(2)}) copy-start(f32[4,128,128]{2,1,0:T(8,128)S(1)} %collective-permute-done.low_ref) | copy-start | bytes 786436
  18.8 0.7 copy-start.9
  24.4 8.4 %collective-permute-start.2 = (f32[4,128,128]{2,1,0:T(8,128)}, f32[4,128,128]{2,1,0:T(8,128)S(1)}, u32[]{:S(2)}, u32[]{:S(2)}) collective-permute-start(f32[4,128,128]{2,1,0:T(8,128)} %get-tuple-element.19), channel_id=1, source_target_pairs={{0,1},{1,2},{2,3},{3,4},{4,5},{5,6},{6,7},{7,8},{8,9},{9,10},{10,1... | collective-permute-start | bytes 786440 | tf_op jit(solution)/shard_map/ppermute | solution.py:297
  26.3 14.6 %collective-permute-start.3 = (f32[4,128,128]{2,1,0:T(8,128)}, f32[4,128,128]{2,1,0:T(8,128)S(1)}, u32[]{:S(2)}, u32[]{:S(2)}) collective-permute-start(f32[4,128,128]{2,1,0:T(8,128)} %get-tuple-element.20), channel_id=1, source_target_pairs={{1,0},{2,1},{3,2},{4,3},{5,4},{6,5},{7,6},{8,7},{9,8},{10,9},{11,1... | collective-permute-start | bytes 786440 | tf_op jit(solution)/shard_map/ppermute | solution.py:297
  32.8 8.2 %copy-start.10 = (f32[4,128,128]{2,1,0:T(8,128)}, f32[4,128,128]{2,1,0:T(8,128)S(1)}, u32[]{:S(2)}) copy-start(f32[4,128,128]{2,1,0:T(8,128)S(1)} %collective-permute-done.2.low_ref) | copy-start | bytes 786436
  41.0 0.7 copy-start.11
  46.2 4.3 %copy-start.1 = (f32[4,16,16,128]{3,2,1,0:T(8,128)S(1)}, f32[4,16,16,128]{3,2,1,0:T(8,128)}, u32[]{:S(2)}) copy-start(f32[4,16,16,128]{3,2,1,0:T(8,128)} %param.11) | copy-start | bytes 1572868
  46.2 142.5 %all-to-all-start = ((f32[8,520,128]{2,1,0:T(8,128)}), f32[8,520,128]{2,1,0:T(8,128)S(1)}, u32[]{:S(2)}, u32[]{:S(2)}) async-start(f32[8,520,128]{2,1,0:T(8,128)} %second_kernel.1.buf_ref), calls=%async_computation | async-start | bytes 4259840 | tf_op jit(solution)/shard_map/all_to_all | solution.py:349
  50.6 29.7 %copy-start.3 = (f32[4,16,8,128]{3,2,1,0:T(8,128)}, f32[4,16,8,128]{3,2,1,0:T(8,128)S(1)}, u32[]{:S(2)}) copy-start(f32[4,16,8,128]{3,2,1,0:T(8,128)S(1)} %get-tuple-element.36) | copy-start | bytes 786436
  50.7 60.7 %copy-start.2 = (f32[4,16,8,128]{3,2,1,0:T(8,128)}, f32[4,16,8,128]{3,2,1,0:T(8,128)S(1)}, u32[]{:S(2)}) copy-start(f32[4,16,8,128]{3,2,1,0:T(8,128)S(1)} %get-tuple-element.35) | copy-start | bytes 786436
  50.7 25.2 %collective-permute-start.8 = (f32[4,16,8,128]{3,2,1,0:T(8,128)S(1)}, f32[4,16,8,128]{3,2,1,0:T(8,128)S(1)}, u32[]{:S(2)}, u32[]{:S(2)}) collective-permute-start(f32[4,16,8,128]{3,2,1,0:T(8,128)S(1)} %get-tuple-element.35), channel_id=1, source_target_pairs={{0,64},{32,96},{64,128},{96,160},{128,192},{160,224},{192,0},{224,... | collective-permute-start | bytes 786440 | tf_op jit(solution)/shard_map/ppermute | solution.py:313
  52.2 26.8 %collective-permute-start.9 = (f32[4,16,8,128]{3,2,1,0:T(8,128)S(1)}, f32[4,16,8,128]{3,2,1,0:T(8,128)S(1)}, u32[]{:S(2)}, u32[]{:S(2)}) collective-permute-start(f32[4,16,8,128]{3,2,1,0:T(8,128)S(1)} %get-tuple-element.35), channel_id=1, source_target_pairs={{0,128},{32,160},{64,192},{96,224},{128,0},{160,32},{192,64},{224,... | collective-permute-start | bytes 786440 | tf_op jit(solution)/shard_map/ppermute | solution.py:313
  54.6 24.4 %collective-permute-start.10 = (f32[4,16,8,128]{3,2,1,0:T(8,128)S(1)}, f32[4,16,8,128]{3,2,1,0:T(8,128)S(1)}, u32[]{:S(2)}, u32[]{:S(2)}) collective-permute-start(f32[4,16,8,128]{3,2,1,0:T(8,128)S(1)} %get-tuple-element.35), channel_id=1, source_target_pairs={{0,192},{32,224},{64,0},{96,32},{128,64},{160,96},{192,128},{224,1... | collective-permute-start | bytes 786440 | tf_op jit(solution)/shard_map/ppermute | solution.py:313
  75.9 31.9 %copy-start.5 = (f32[4,16,8,128]{3,2,1,0:T(8,128)}, f32[4,16,8,128]{3,2,1,0:T(8,128)S(1)}, u32[]{:S(2)}) copy-start(f32[4,16,8,128]{3,2,1,0:T(8,128)S(1)} %collective-permute-done.8) | copy-start | bytes 786436
  79.0 28.7 %copy-start.6 = (f32[4,16,8,128]{3,2,1,0:T(8,128)}, f32[4,16,8,128]{3,2,1,0:T(8,128)S(1)}, u32[]{:S(2)}) copy-start(f32[4,16,8,128]{3,2,1,0:T(8,128)S(1)} %collective-permute-done.9) | copy-start | bytes 786436
  79.0 31.0 %copy-start.7 = (f32[4,16,8,128]{3,2,1,0:T(8,128)}, f32[4,16,8,128]{3,2,1,0:T(8,128)S(1)}, u32[]{:S(2)}) copy-start(f32[4,16,8,128]{3,2,1,0:T(8,128)S(1)} %collective-permute-done.10) | copy-start | bytes 786436
  79.1 53.7 %collective-permute-start.11 = (f32[4,4,16,8,128]{4,3,2,1,0:T(8,128)S(1)}, f32[4,4,16,8,128]{4,3,2,1,0:T(8,128)}, u32[]{:S(2)}, u32[]{:S(2)}) collective-permute-start(f32[4,4,16,8,128]{4,3,2,1,0:T(8,128)S(1)} %pad_maximum_fusion), channel_id=1, source_target_pairs={{0,32},{32,0},{64,96},{96,64},{128,160},{160,128},{192,224},{224,1... | collective-permute-start | bytes 3145736 | tf_op jit(solution)/shard_map/ppermute | solution.py:313
  80.3 25.9 %collective-permute-start.4 = (f32[4,16,8,128]{3,2,1,0:T(8,128)S(1)}, f32[4,16,8,128]{3,2,1,0:T(8,128)S(1)}, u32[]{:S(2)}, u32[]{:S(2)}) collective-permute-start(f32[4,16,8,128]{3,2,1,0:T(8,128)S(1)} %get-tuple-element.36), channel_id=1, source_target_pairs={{0,32},{32,0},{64,96},{96,64},{128,160},{160,128},{192,224},{224,1... | collective-permute-start | bytes 786440 | tf_op jit(solution)/shard_map/ppermute | solution.py:313
  106.2 0.7 copy-start.4
  107.7 24.2 %collective-permute-start.5 = (f32[2,4,16,8,128]{4,3,2,1,0:T(8,128)}, f32[2,4,16,8,128]{4,3,2,1,0:T(8,128)}, u32[]{:S(2)}, u32[]{:S(2)}) collective-permute-start(f32[2,4,16,8,128]{4,3,2,1,0:T(8,128)} %pad_maximum_fusion.1), channel_id=1, source_target_pairs={{0,64},{32,96},{64,128},{96,160},{128,192},{160,224},{192,0},{224,... | collective-permute-start | bytes 1572872 | tf_op jit(solution)/shard_map/ppermute | solution.py:313
  107.7 24.2 %collective-permute-start.6 = (f32[2,4,16,8,128]{4,3,2,1,0:T(8,128)}, f32[2,4,16,8,128]{4,3,2,1,0:T(8,128)}, u32[]{:S(2)}, u32[]{:S(2)}) collective-permute-start(f32[2,4,16,8,128]{4,3,2,1,0:T(8,128)} %pad_maximum_fusion.1), channel_id=1, source_target_pairs={{0,128},{32,160},{64,192},{96,224},{128,0},{160,32},{192,64},{224,... | collective-permute-start | bytes 1572872 | tf_op jit(solution)/shard_map/ppermute | solution.py:313
  110.1 22.8 %collective-permute-start.7 = (f32[2,4,16,8,128]{4,3,2,1,0:T(8,128)}, f32[2,4,16,8,128]{4,3,2,1,0:T(8,128)}, u32[]{:S(2)}, u32[]{:S(2)}) collective-permute-start(f32[2,4,16,8,128]{4,3,2,1,0:T(8,128)} %pad_maximum_fusion.1), channel_id=1, source_target_pairs={{0,192},{32,224},{64,0},{96,32},{128,64},{160,96},{192,128},{224,1... | collective-permute-start | bytes 1572872 | tf_op jit(solution)/shard_map/ppermute | solution.py:313
  144.2 19.5 %collective-permute-start.12 = (f32[56,512]{1,0:T(8,128)}, f32[56,512]{1,0:T(8,128)S(1)}, u32[]{:S(2)}, u32[]{:S(2)}) collective-permute-start(f32[56,512]{1,0:T(8,128)} %get-tuple-element.29), channel_id=1, source_target_pairs={{0,1},{1,2},{2,3},{3,4},{4,5},{5,6},{6,7},{7,8},{8,9},{9,10},{10,1... | collective-permute-start | bytes 344072 | tf_op jit(solution)/shard_map/ppermute | solution.py:297
  161.6 7.2 %collective-permute-start.13 = (f32[56,512]{1,0:T(8,128)}, f32[56,512]{1,0:T(8,128)S(1)}, u32[]{:S(2)}, u32[]{:S(2)}) collective-permute-start(f32[56,512]{1,0:T(8,128)} %get-tuple-element.30), channel_id=1, source_target_pairs={{1,0},{2,1},{3,2},{4,3},{5,4},{6,5},{7,6},{8,7},{9,8},{10,9},{11,1... | collective-permute-start | bytes 344072 | tf_op jit(solution)/shard_map/ppermute | solution.py:297
  163.7 5.1 %copy-start.19 = (f32[56,512]{1,0:T(8,128)}, f32[56,512]{1,0:T(8,128)S(1)}, u32[]{:S(2)}) copy-start(f32[56,512]{1,0:T(8,128)S(1)} %collective-permute-done.12.low_ref) | copy-start | bytes 344068
  168.8 0.7 copy-start.20
  171.5 6.8 %collective-permute-start.18 = (f32[96,512]{1,0:T(8,128)}, f32[96,512]{1,0:T(8,128)S(1)}, u32[]{:S(2)}, u32[]{:S(2)}) collective-permute-start(f32[96,512]{1,0:T(8,128)} %late_kernel.1.refs_0_), channel_id=1, source_target_pairs={{0,32},{32,0},{64,96},{96,64},{128,160},{160,128},{192,224},{224,1... | collective-permute-start | bytes 589832 | tf_op jit(solution)/shard_map/ppermute | solution.py:313
  173.3 8.6 %collective-permute-start.19 = (f32[96,512]{1,0:T(8,128)}, f32[96,512]{1,0:T(8,128)S(1)}, u32[]{:S(2)}, u32[]{:S(2)}) collective-permute-start(f32[96,512]{1,0:T(8,128)} %late_kernel.1.refs_0_), channel_id=1, source_target_pairs={{0,64},{32,96},{64,0},{96,32},{128,192},{160,224},{192,128},{224,1... | collective-permute-start | bytes 589832 | tf_op jit(solution)/shard_map/ppermute | solution.py:313
  174.3 14.4 %collective-permute-start.20 = (f32[96,512]{1,0:T(8,128)}, f32[96,512]{1,0:T(8,128)S(1)}, u32[]{:S(2)}, u32[]{:S(2)}) collective-permute-start(f32[96,512]{1,0:T(8,128)} %late_kernel.1.refs_0_), channel_id=1, source_target_pairs={{0,192},{32,224},{64,128},{96,160},{128,64},{160,96},{192,0},{224,... | collective-permute-start | bytes 589832 | tf_op jit(solution)/shard_map/ppermute | solution.py:313
  175.9 23.2 %collective-permute-start.14 = (f32[96,512]{1,0:T(8,128)}, f32[96,512]{1,0:T(8,128)S(1)}, u32[]{:S(2)}, u32[]{:S(2)}) collective-permute-start(f32[96,512]{1,0:T(8,128)} %late_kernel.1.refs_0_), channel_id=1, source_target_pairs={{0,96},{32,64},{64,32},{96,0},{128,224},{160,192},{192,160},{224,1... | collective-permute-start | bytes 589832 | tf_op jit(solution)/shard_map/ppermute | solution.py:313
  176.5 22.6 %collective-permute-start.15 = (f32[96,512]{1,0:T(8,128)}, f32[96,512]{1,0:T(8,128)S(1)}, u32[]{:S(2)}, u32[]{:S(2)}) collective-permute-start(f32[96,512]{1,0:T(8,128)} %late_kernel.1.refs_0_), channel_id=1, source_target_pairs={{0,224},{32,192},{64,160},{96,128},{128,96},{160,64},{192,32},{224... | collective-permute-start | bytes 589832 | tf_op jit(solution)/shard_map/ppermute | solution.py:313
  178.3 10.4 %copy-start.14 = (f32[96,512]{1,0:T(8,128)}, f32[96,512]{1,0:T(8,128)S(1)}, u32[]{:S(2)}) copy-start(f32[96,512]{1,0:T(8,128)S(1)} %collective-permute-done.18.refs_0_) | copy-start | bytes 589828
  178.3 20.9 %collective-permute-start.16 = (f32[96,512]{1,0:T(8,128)}, f32[96,512]{1,0:T(8,128)S(1)}, u32[]{:S(2)}, u32[]{:S(2)}) collective-permute-start(f32[96,512]{1,0:T(8,128)} %late_kernel.1.refs_0_), channel_id=1, source_target_pairs={{0,128},{32,160},{64,192},{96,224},{128,0},{160,32},{192,64},{224,... | collective-permute-start | bytes 589832 | tf_op jit(solution)/shard_map/ppermute | solution.py:313
  181.9 6.8 %copy-start.16 = (f32[96,512]{1,0:T(8,128)}, f32[96,512]{1,0:T(8,128)S(1)}, u32[]{:S(2)}) copy-start(f32[96,512]{1,0:T(8,128)S(1)} %collective-permute-done.19.refs_1_) | copy-start | bytes 589828
  181.9 17.3 %collective-permute-start.17 = (f32[96,512]{1,0:T(8,128)}, f32[96,512]{1,0:T(8,128)S(1)}, u32[]{:S(2)}, u32[]{:S(2)}) collective-permute-start(f32[96,512]{1,0:T(8,128)} %late_kernel.1.refs_0_), channel_id=1, source_target_pairs={{0,160},{32,128},{64,224},{96,192},{128,32},{160,0},{192,96},{224,... | collective-permute-start | bytes 589832 | tf_op jit(solution)/shard_map/ppermute | solution.py:313
  188.7 0.7 copy-start.17
  189.3 1.4 copy-start
  199.2 0.7 copy-start.12
  199.2 0.8 copy-start.13
  199.2 0.8 copy-start.15
  200.0 0.7 copy-start.18
where the time goes:
time: 215 us; the launch traced here: 211 us
  waiting for transfers between devices  89.4 us (42%)
  starting transfers between devices  59 us (27%)
  Pallas kernels  52.3 us (24%)
  local copies, waits for them, and re-layouts  7.44 us (3%)
    ppermute x15, waiting for transfers between devices, sent(): return lax.ppermute(value, 'shot', pairs)  64.4 us
    ppermute x3, starting transfers between devices, spread(): lax.ppermute(high_layers, axis, forward)  25.6 us
    pallas_call x3, Pallas kernels, image(): pl.pallas_call(functools.partial(image_kernel, count, probes, flips, scal...  23 us
    ppermute x15, starting transfers between devices, sent(): return lax.ppermute(value, 'shot', pairs)  22.9 us
    ppermute x3, waiting for transfers between devices, spread(): lax.ppermute(low_layers, axis, backward)  20.8 us
    pallas_call x2, Pallas kernels, gather(): pl.pallas_call(functools.partial(gather_kernel, count, probes, rounds, pl...  17.8 us
    unnamed x42, local copies, waits for them, and re-layouts  6.28 us
    ppermute x3, starting transfers between devices, spread(): lax.ppermute(low_layers, axis, backward)  6.26 us
  transfers between devices with their start and end apart: 22, of which 11 were waited for; matrix products, arithmetic and copies ran while one was open for 0% of the time, Pallas kernels for 15%

commit v1 on v0

--- a/solution.py
+++ b/solution.py
@@ -109,22 +109,28 @@
         buf_ref[strip, 4 * count * 8 + n_rows :, :] = jnp.zeros((buf_ref.shape[1] - 4 * count * 8 - n_rows, width), F32)
 
 
-def masks_of(wells, width):
+def masks_of(wells, width, matrix):
     x_row = wells // width
     y_row = wells - x_row * width
     y_ids = lax.broadcasted_iota(jnp.int32, (width, wells.shape[1]), 0)
     spot = jnp.where(y_ids == y_row, 1.0, 0.0).astype(BF16)
-    side = jnp.dot(stencil_matrix(width), spot, preferred_element_type=F32).astype(BF16)
+    side = jnp.dot(matrix, spot, preferred_element_type=F32).astype(BF16)
     return x_row, spot, side
 
 
-def fill(x_row, spot, side, x, spot_ref, lap_ref, row):
-    width = spot.shape[0]
-    distance = jnp.abs(x_row - x)
-    at = jnp.where(distance == 0, 1.0, 0.0).astype(BF16)
-    near = band(distance).astype(BF16)
-    spot_ref[row : row + width, :] = spot * at
-    lap_ref[row : row + width, :] = spot * near + side * at
+def rows_of(x_row, base, count):
+    ids = base + lax.broadcasted_iota(jnp.int32, (count, x_row.shape[1]), 0)
+    distance = jnp.abs(x_row - ids)
+    return jnp.where(distance == 0, 1.0, 0.0), band(distance)
+
+
+def fill(rows, spot, side, x, spot_ref, lap_ref, row):
+    width, n = spot.shape
+    at, near = (jnp.broadcast_to(value[x : x + 1], (16, n)).astype(BF16)[None] for value in rows)
+    spot = spot.reshape(width // 16, 16, n)
+    side = side.reshape(width // 16, 16, n)
+    spot_ref[row : row + width, :] = (spot * at).reshape(width, n)
+    lap_ref[row : row + width, :] = (spot * near + side * at).reshape(width, n)
 
 
 def strip_of(me, rounds, plan, i):
@@ -144,7 +150,7 @@
     spot_ref, lap_ref, left_ref = refs[-3:]
     width = buf_ref.shape[2]
     rows = probes * count
-    x_row, spot, side = masks_of(wells_ref[...], width)
+    x_row, spot, side = masks_of(wells_ref[...], width, stencil_matrix(width))
     if started:
         for ref, start_ref in zip((first_ref, sigma_ref, v_ref), start_refs):
             ref[...] = start_ref[...]
@@ -156,8 +162,9 @@
         def body(i, carry, m_ref=m_ref, plan=plan):
             half = plan[0]
             strip = strip_of(me_ref[0], rounds, plan, i)
+            x_rows = rows_of(x_row, strip * 16 + half * 8, 8)
             for x in range(8):
-                fill(x_row, spot, side, strip * 16 + half * 8 + x, spot_ref, lap_ref, x * width)
+                fill(x_rows, spot, side, x, spot_ref, lap_ref, x * width)
                 m = m_ref[i, pl.ds(x, rows, stride=8), :]
                 born = buf_ref[strip, pl.ds(half * count * 8 + x, count, stride=8), :]
                 both = buf_ref[strip, pl.ds((2 + half) * count * 8 + x, count, stride=8), :]
@@ -220,7 +227,7 @@
     late_refs, refs = refs[:n], refs[n:]
     if started:
         start_ref, refs = refs[0], refs[1:]
-    out_ref, late_ref, spot_ref, lap_ref, left_ref, side_ref = refs
+    out_ref, late_ref, spot_ref, lap_ref, left_ref, matrix_ref = refs
     width = m_ref.shape[1]
     rows = probes * count
     step = pl.program_id(0)
@@ -229,6 +236,7 @@
     @pl.when(step == 0)
     def _():
         out_ref[...] = start_ref[...] if started else jnp.zeros_like(out_ref)
+        matrix_ref[...] = stencil_matrix(width)
 
     for i in range(n):
 
@@ -238,7 +246,8 @@
 
     top = 4 * count * 8
     wells = jnp.concatenate([buf_ref[0, top + i : top + i + 1, :] for i in range(n_wells // width)], axis=1)
-    x_row, spot, side = masks_of(wells.astype(jnp.int32), width)
+    x_row, spot, side = masks_of(wells.astype(jnp.int32), width, matrix_ref[...])
+    x_rows = rows_of(x_row, me_ref[0] * 16, 16)
     for p in range(probes):
         top = p * (count + 8)
         here = late_ref[top + 4 : top + 4 + count, :]
@@ -251,9 +260,6 @@
             high, low = halves(value)
             left_ref[2 * j * rows + p * count : 2 * j * rows + (p + 1) * count, :] = high
             left_ref[(2 * j + 1) * rows + p * count : (2 * j + 1) * rows + (p + 1) * count, :] = low
-        high, low = halves(SCALE * here)
-        side_ref[p * count : (p + 1) * count, :] = high
-        side_ref[rows + p * count : rows + (p + 1) * count, :] = low
     left_ref[4 * rows :, :] = jnp.ones((count, n_wells), BF16)
     contract = (((1,), (1,)), ((), ()))
     for half in range(2):
@@ -261,10 +267,10 @@
             slot = pair % 2
             for j in range(2):
                 x = half * 8 + pair * 2 + j
-                fill(x_row, spot, side, me_ref[0] * 16 + x, spot_ref.at[slot], lap_ref.at[slot], j * width)
+                fill(x_rows, spot, side, x, spot_ref.at[slot], lap_ref.at[slot], j * width)
             out = lax.dot_general(left_ref[...], spot_ref[slot], contract, preferred_element_type=F32)
-            lap = lax.dot_general(side_ref[...], lap_ref[slot], contract, preferred_element_type=F32)
-            field = (out[:rows] + out[rows : 2 * rows]) + (lap[:rows] + lap[rows:])
+            lap = lax.dot_general(left_ref[2 * rows : 4 * rows, :], lap_ref[slot], contract, preferred_element_type=F32)
+            field = (out[:rows] + out[rows : 2 * rows]) + SCALE * (lap[:rows] + lap[rows:])
             late = out[2 * rows : 3 * rows] + out[3 * rows : 4 * rows]
             hits = out[4 * rows :]
             for j in range(2):
@@ -304,7 +310,9 @@
     n_wells = receiver_wells.shape[1]
     rows = probes * count
     me = lax.axis_index("shot").reshape(1).astype(jnp.int32)
-    params = pltpu.CompilerParams(vmem_limit_bytes=60 * 1024 * 1024)
+    params = pltpu.CompilerParams(vmem_limit_bytes=32 * 1024 * 1024)
+    gather_params = pltpu.CompilerParams(vmem_limit_bytes=32 * 1024 * 1024)
+    image_params = pltpu.CompilerParams(vmem_limit_bytes=67043328)
 
     rounds = strips // 2
     swap = [(i, i ^ 1) for i in range(strips)]
@@ -368,7 +376,7 @@
                 pltpu.VMEM((8 * width, n_wells), BF16),
                 pltpu.VMEM((4 * rows + 2 * count, 8 * width), BF16),
             ],
-            compiler_params=params,
+            compiler_params=gather_params,
         )(me, receiver_wells, velocity.reshape(count * width, width), buf, *parts, *start)
 
     own_plans = ((0, 0, 0, 0, 0), (0, 0, 0, 1, 0)) + tuple((1, s, 0, 0, 0) for s in range(rounds))
@@ -420,10 +428,10 @@
                     pltpu.VMEM((2, 2 * width, n_wells), BF16),
                     pltpu.VMEM((2, 2 * width, n_wells), BF16),
                     pltpu.VMEM((4 * rows + count, n_wells), BF16),
-                    pltpu.VMEM((2 * rows, n_wells), BF16),
+                    pltpu.VMEM((width, width), BF16),
                 ],
             ),
-            compiler_params=params,
+            compiler_params=image_params,
         )(me, source, panel, *[late_from[flip] for flip in flips], *start)
 
     total = image(buf, (0,), 1.0)

time: 215 us -> 203 us (0.944)
  Pallas kernels: 52.3 us -> 42.1 us
  starting transfers between devices: 59 us -> 55.5 us
  waiting for transfers between devices: 89.4 us -> 92.9 us
    ppermute x15, starting transfers between devices: 22.9 us -> 18.8 us  [sent(): return lax.ppermute(value, 'shot', pairs)]
    ppermute x15, waiting for transfers between devices: 64.4 us -> 68.2 us  [sent(): return lax.ppermute(value, 'shot', pairs)]
    pallas_call x1, Pallas kernels: 4.96 us -> 1.38 us  [slab(): pl.pallas_call(functools.partial(step_kernel, count), out_shape=(plane, p...]
    pallas_call x2, Pallas kernels: 17.8 us -> 14.5 us  [gather(): pl.pallas_call(functools.partial(gather_kernel, count, probes, rounds, pl...]
    unnamed x42 -> x16, local copies, waits for them, and re-layouts: 6.28 us -> 4.64 us
  transfers between devices with their start and end apart: 22 -> 22, of which waited for: 11 -> 10; matrix products, arithmetic and copies ran while one was open for 0% -> 1% of each run, Pallas kernels for 15% -> 14%
where the time goes in v1:
time: 203 us; the launch traced here: 200 us
  waiting for transfers between devices  92.9 us (46%)
  starting transfers between devices  55.5 us (27%)
  Pallas kernels  42.1 us (21%)
  local copies, waits for them, and re-layouts  5.82 us (3%)
  between operations  2.1 us (1%)
    ppermute x15, waiting for transfers between devices, sent(): return lax.ppermute(value, 'shot', pairs)  68.2 us
    ppermute x3, starting transfers between devices, spread(): lax.ppermute(high_layers, axis, forward)  25.9 us
    pallas_call x3, Pallas kernels, image(): pl.pallas_call(functools.partial(image_kernel, count, probes, flips, scal...  22.6 us
    ppermute x3, waiting for transfers between devices, spread(): lax.ppermute(low_layers, axis, backward)  20.9 us
    ppermute x15, starting transfers between devices, sent(): return lax.ppermute(value, 'shot', pairs)  18.8 us
    pallas_call x2, Pallas kernels, gather(): pl.pallas_call(functools.partial(gather_kernel, count, probes, rounds, pl...  14.5 us
    ppermute x3, starting transfers between devices, spread(): lax.ppermute(low_layers, axis, backward)  6.26 us
    unnamed x16, local copies, waits for them, and re-layouts  4.64 us
  transfers between devices with their start and end apart: 22, of which 10 were waited for; matrix products, arithmetic and copies ran while one was open for 1% of the time, Pallas kernels for 14%

profile of v1, /device:TPU:1, one launch (start us, length us, event | category | flops | bytes accessed | tf_op | source)
XLA Modules:
  0.0 200.3 jit_solution(13259771641947357371)
XLA Ops:
  0.0 1.1 slice_bitcast_fusion
  1.1 6.3 %collective-permute-start = (f32[4,128,128]{2,1,0:T(8,128)S(1)}, f32[4,128,128]{2,1,0:T(8,128)S(1)}, u32[]{:S(2)}, u32[]{:S(2)}) collective-permute-start(f32[4,128,128]{2,1,0:T(8,128)S(1)} %get-tuple-element.32), channel_id=1, source_target_pairs={{0,1},{1,2},{2,3},{3,4},{4,5},{5,6},{6,7},{7,8},{8,9},{9,10},{10,1... | collective-permute-start | bytes 786440 | tf_op jit(solution)/shard_map/ppermute | solution.py:303
  7.4 1.9 collective-permute-start.1
  11.3 7.5 %collective-permute-done.1.high_ref = f32[4,128,128]{2,1,0:T(8,128)S(1)} collective-permute-done((f32[4,128,128]{2,1,0:T(8,128)S(1)}, f32[4,128,128]{2,1,0:T(8,128)S(1)}, u32[]{:S(2)}, u32[]{:S(2)}) %collective-permute-start.1) | collective-permute-done | bytes 262176 | tf_op jit(solution)/shard_map/ppermute | solution.py:303
  18.8 1.2 copy-done
  20.0 1.2 copy-done.2
  21.2 1.2 copy-done.3
  22.4 1.4 step_kernel.1
  23.8 1.9 collective-permute-start.2
  25.8 2.4 %collective-permute-start.3 = (f32[4,128,128]{2,1,0:T(8,128)S(1)}, f32[4,128,128]{2,1,0:T(8,128)S(1)}, u32[]{:S(2)}, u32[]{:S(2)}) collective-permute-start(f32[4,128,128]{2,1,0:T(8,128)S(1)} %get-tuple-element.20), channel_id=1, source_target_pairs={{1,0},{2,1},{3,2},{4,3},{5,4},{6,5},{7,6},{8,7},{9,8},{10,9},{11,1... | collective-permute-start | bytes 786440 | tf_op jit(solution)/shard_map/ppermute | solution.py:303
  28.2 3.7 %collective-permute-done.2.low_ref = f32[4,128,128]{2,1,0:T(8,128)S(1)} collective-permute-done((f32[4,128,128]{2,1,0:T(8,128)S(1)}, f32[4,128,128]{2,1,0:T(8,128)S(1)}, u32[]{:S(2)}, u32[]{:S(2)}) %collective-permute-start.2) | collective-permute-done | bytes 262176 | tf_op jit(solution)/shard_map/ppermute | solution.py:303
  31.9 8.3 %collective-permute-done.3.high_ref = f32[4,128,128]{2,1,0:T(8,128)S(1)} collective-permute-done((f32[4,128,128]{2,1,0:T(8,128)S(1)}, f32[4,128,128]{2,1,0:T(8,128)S(1)}, u32[]{:S(2)}, u32[]{:S(2)}) %collective-permute-start.3) | collective-permute-done | bytes 262176 | tf_op jit(solution)/shard_map/ppermute | solution.py:303
  40.2 2.6 %second_kernel.1.buf_ref = f32[8,520,128]{2,1,0:T(8,128)} custom-call(s32[1,512]{1,0:T(1,128)S(1)} %copy-done.6, f32[16,128,128]{2,1,0:T(8,128)S(1)} %get-tuple-element.18.next_ref, f32[4,128,128]{2,1,0:T(8,128)S(1)} %collective-permute-done.2.low_ref, f32[4,128,128]{2,1,0:T(8,128)S(1)} %collective-permute-done.3.high_ref, ...), custom_call_target="tpu_custom_call" | custom-call | tf_op jit(solution)/shard_map/second_kernel/pallas_call | solution.py:349
  42.8 4.5 %all-to-all-start = ((f32[8,520,128]{2,1,0:T(8,128)}), f32[8,520,128]{2,1,0:T(8,128)}, u32[]{:S(2)}, u32[]{:S(2)}) async-start(f32[8,520,128]{2,1,0:T(8,128)} %second_kernel.1.buf_ref), calls=%async_computation | async-start | bytes 4259840 | tf_op jit(solution)/shard_map/all_to_all | solution.py:357
  47.4 0.0 copy-start.1
  47.4 0.1 slice_bitcast_fusion.2
  47.5 1.5 collective-permute-start.8
  49.0 2.8 %collective-permute-start.9 = (f32[4,16,8,128]{3,2,1,0:T(8,128)S(1)}, f32[4,16,8,128]{3,2,1,0:T(8,128)S(1)}, u32[]{:S(2)}, u32[]{:S(2)}) collective-permute-start(f32[4,16,8,128]{3,2,1,0:T(8,128)S(1)} %get-tuple-element.35), channel_id=1, source_target_pairs={{0,128},{32,160},{64,192},{96,224},{128,0},{160,32},{192,64},{224,... | collective-permute-start | bytes 786440 | tf_op jit(solution)/shard_map/ppermute | solution.py:321
  51.8 0.8 collective-permute-start.10
  52.6 19.9 %collective-permute-done.8 = f32[4,16,8,128]{3,2,1,0:T(8,128)S(1)} collective-permute-done((f32[4,16,8,128]{3,2,1,0:T(8,128)S(1)}, f32[4,16,8,128]{3,2,1,0:T(8,128)S(1)}, u32[]{:S(2)}, u32[]{:S(2)}) %collective-permute-start.8) | collective-permute-done | bytes 262176 | tf_op jit(solution)/shard_map/ppermute | solution.py:321
  72.5 3.1 %collective-permute-done.9 = f32[4,16,8,128]{3,2,1,0:T(8,128)S(1)} collective-permute-done((f32[4,16,8,128]{3,2,1,0:T(8,128)S(1)}, f32[4,16,8,128]{3,2,1,0:T(8,128)S(1)}, u32[]{:S(2)}, u32[]{:S(2)}) %collective-permute-start.9) | collective-permute-done | bytes 262176 | tf_op jit(solution)/shard_map/ppermute | solution.py:321
  75.6 1.1 pad_maximum_fusion
  76.7 1.2 collective-permute-start.11
  77.9 0.3 collective-permute-start.4
  78.2 25.6 %collective-permute-done.4 = f32[4,16,8,128]{3,2,1,0:T(8,128)S(1)} collective-permute-done((f32[4,16,8,128]{3,2,1,0:T(8,128)S(1)}, f32[4,16,8,128]{3,2,1,0:T(8,128)S(1)}, u32[]{:S(2)}, u32[]{:S(2)}) %collective-permute-start.4) | collective-permute-done | bytes 262176 | tf_op jit(solution)/shard_map/ppermute | solution.py:321
  103.7 0.8 pad_maximum_fusion.1
  104.6 2.3 %collective-permute-start.6 = (f32[2,4,16,8,128]{4,3,2,1,0:T(8,128)}, f32[2,4,16,8,128]{4,3,2,1,0:T(8,128)}, u32[]{:S(2)}, u32[]{:S(2)}) collective-permute-start(f32[2,4,16,8,128]{4,3,2,1,0:T(8,128)} %pad_maximum_fusion.1), channel_id=1, source_target_pairs={{0,128},{32,160},{64,192},{96,224},{128,0},{160,32},{192,64},{224,... | collective-permute-start | bytes 1572872 | tf_op jit(solution)/shard_map/ppermute | solution.py:321
  106.8 1.0 collective-permute-start.7
  107.8 0.9 copy-done.5
  108.8 4.9 %shard_map.82 = (f32[64,512]{1,0:T(8,128)S(1)}, f32[64,512]{1,0:T(8,128)S(1)}, f32[16,512]{1,0:T(8,128)S(1)}) custom-call(s32[1]{0:T(128)} %bitcast.me_ref, s32[1,512]{1,0:T(1,128)S(1)} %copy-done.6, f32[2048,128]{1,0:T(8,128)S(1)} %bitcast.29, f32[8,520,128]{2,1,0:T(8,128)} %second_kernel.1.buf_ref, f32[1,512,128]{2,1,0:T(8,128)S(1)} %bitcast.34, ...), custom_call_target="tpu_custom_call" | custom-call | tf_op jit(solution)/shard_map/pallas_call | solution.py:369
  113.7 14.8 %collective-permute-done.5 = f32[2,4,16,8,128]{4,3,2,1,0:T(8,128)} collective-permute-done((f32[2,4,16,8,128]{4,3,2,1,0:T(8,128)}, f32[2,4,16,8,128]{4,3,2,1,0:T(8,128)}, u32[]{:S(2)}, u32[]{:S(2)}) %collective-permute-start.5) | collective-permute-done | bytes 524320 | tf_op jit(solution)/shard_map/ppermute | solution.py:321
  128.6 0.9 collective-permute-done.7
  129.5 9.6 %shard_map.83 = (f32[64,512]{1,0:T(8,128)S(1)}, f32[64,512]{1,0:T(8,128)S(1)}, f32[16,512]{1,0:T(8,128)S(1)}, f32[56,512]{1,0:T(8,128)S(1)}, f32[56,512]{1,0:T(8,128)S(1)}) custom-call(s32[1]{0:T(128)} %bitcast.me_ref, s32[1,512]{1,0:T(1,128)S(1)} %copy-done.6, f32[2048,128]{1,0:T(8,128)S(1)} %bitcast.30, f32[8,520,128]{2,1,0:T(8,128)} %second_kernel.1.buf_ref, ...), custom_call_target="tpu_custom_call" | custom-call | tf_op jit(solution)/shard_map/pallas_call | solution.py:369
  139.0 17.7 %collective-permute-start.12 = (f32[56,512]{1,0:T(8,128)S(1)}, f32[56,512]{1,0:T(8,128)S(1)}, u32[]{:S(2)}, u32[]{:S(2)}) collective-permute-start(f32[56,512]{1,0:T(8,128)S(1)} %get-tuple-element.29), channel_id=1, source_target_pairs={{0,1},{1,2},{2,3},{3,4},{4,5},{5,6},{6,7},{7,8},{8,9},{9,10},{10,1... | collective-permute-start | bytes 344072 | tf_op jit(solution)/shard_map/ppermute | solution.py:303
  156.7 1.9 collective-permute-start.13
  158.7 5.1 %collective-permute-done.13.high_ref = f32[56,512]{1,0:T(8,128)S(1)} collective-permute-done((f32[56,512]{1,0:T(8,128)S(1)}, f32[56,512]{1,0:T(8,128)S(1)}, u32[]{:S(2)}, u32[]{:S(2)}) %collective-permute-start.13) | collective-permute-done | bytes 114720 | tf_op jit(solution)/shard_map/ppermute | solution.py:303
  163.7 0.9 late_kernel.1.refs_0_
  164.7 1.7 collective-permute-start.18
  166.4 1.4 collective-permute-start.19
  167.8 1.3 collective-permute-start.20
  169.1 0.6 collective-permute-start.14
  169.7 1.8 collective-permute-start.15
  171.5 1.8 collective-permute-start.16
  173.3 3.9 %collective-permute-done.19.refs_1_ = f32[96,512]{1,0:T(8,128)} collective-permute-done((f32[96,512]{1,0:T(8,128)}, f32[96,512]{1,0:T(8,128)}, u32[]{:S(2)}, u32[]{:S(2)}) %collective-permute-start.19) | collective-permute-done | bytes 196640 | tf_op jit(solution)/shard_map/ppermute | solution.py:321
  177.2 0.4 collective-permute-start.17
  177.6 3.9 %shard_map.84.refs_3_ = f32[1024,128]{1,0:T(8,128)} custom-call(s32[1]{0:T(128)} %bitcast.me_ref, f32[8,520,128]{2,1,0:T(8,128)} %second_kernel.1.buf_ref, f32[1024,128]{1,0:T(8,128)} %bitcast.44, f32[96,512]{1,0:T(8,128)} %late_kernel.1.refs_0_), custom_call_target="tpu_custom_call" | custom-call | tf_op jit(solution)/shard_map/pallas_call | solution.py:416
  181.5 8.3 %shard_map.85.refs_4_ = f32[1024,128]{1,0:T(8,128)} custom-call(s32[1]{0:T(128)} %bitcast.me_ref, f32[8,520,128]{2,1,0:T(8,128)} %all-to-all-done.buf_ref, f32[1024,128]{1,0:T(8,128)} %bitcast.45, f32[96,512]{1,0:T(8,128)} %collective-permute-done.18.refs_0_, f32[96,512]{1,0:T(8,128)} %collective-permute-done.19.refs_1_, ...), custom_call_target="tpu_custom_call" | custom-call | tf_op jit(solution)/shard_map/pallas_call | solution.py:416
  189.8 10.4 %shard_map.86 = f32[1024,128]{1,0:T(8,128)} custom-call(s32[1]{0:T(128)} %bitcast.me_ref, f32[8,520,128]{2,1,0:T(8,128)} %all-to-all-done.buf_ref, f32[1024,128]{1,0:T(8,128)} %bitcast.46, f32[96,512]{1,0:T(8,128)} %collective-permute-done.14.refs_0_, f32[96,512]{1,0:T(8,128)} %collective-permute-done.15.refs_1_, f32[96,512]{1,0:T(8,128)} %collective-permute-done.16.refs_2_, ...), custom_call_target="tpu_custom_call" | custom-call | tf_op jit(solution)/shard_map/pallas_call | solution.py:416
  (24 shorter events, 0.1 us)
Async XLA Ops:
  0.0 40.2 %copy-start.6 = (s32[1,512]{1,0:T(1,128)S(1)}, s32[1,512]{1,0:T(1,128)}, u32[]{:S(2)}) copy-start(s32[1,512]{1,0:T(1,128)} %wells_ref.5) | copy-start | bytes 6148
  1.1 10.2 %collective-permute-start = (f32[4,128,128]{2,1,0:T(8,128)S(1)}, f32[4,128,128]{2,1,0:T(8,128)S(1)}, u32[]{:S(2)}, u32[]{:S(2)}) collective-permute-start(f32[4,128,128]{2,1,0:T(8,128)S(1)} %get-tuple-element.32), channel_id=1, source_target_pairs={{0,1},{1,2},{2,3},{3,4},{4,5},{5,6},{6,7},{7,8},{8,9},{9,10},{10,1... | collective-permute-start | bytes 786440 | tf_op jit(solution)/shard_map/ppermute | solution.py:303
  7.4 11.4 %collective-permute-start.1 = (f32[4,128,128]{2,1,0:T(8,128)S(1)}, f32[4,128,128]{2,1,0:T(8,128)S(1)}, u32[]{:S(2)}, u32[]{:S(2)}) collective-permute-start(f32[4,128,128]{2,1,0:T(8,128)S(1)} %get-tuple-element.31), channel_id=1, source_target_pairs={{1,0},{2,1},{3,2},{4,3},{5,4},{6,5},{7,6},{8,7},{9,8},{10,9},{11,1... | collective-permute-start | bytes 786440 | tf_op jit(solution)/shard_map/ppermute | solution.py:303
  18.8 1.2 copy-start
  20.0 1.2 copy-start.2
  21.2 1.2 copy-start.3
  23.8 8.1 %collective-permute-start.2 = (f32[4,128,128]{2,1,0:T(8,128)S(1)}, f32[4,128,128]{2,1,0:T(8,128)S(1)}, u32[]{:S(2)}, u32[]{:S(2)}) collective-permute-start(f32[4,128,128]{2,1,0:T(8,128)S(1)} %get-tuple-element.19), channel_id=1, source_target_pairs={{0,1},{1,2},{2,3},{3,4},{4,5},{5,6},{6,7},{7,8},{8,9},{9,10},{10,1... | collective-permute-start | bytes 786440 | tf_op jit(solution)/shard_map/ppermute | solution.py:303
  25.8 14.4 %collective-permute-start.3 = (f32[4,128,128]{2,1,0:T(8,128)S(1)}, f32[4,128,128]{2,1,0:T(8,128)S(1)}, u32[]{:S(2)}, u32[]{:S(2)}) collective-permute-start(f32[4,128,128]{2,1,0:T(8,128)S(1)} %get-tuple-element.20), channel_id=1, source_target_pairs={{1,0},{2,1},{3,2},{4,3},{5,4},{6,5},{7,6},{8,7},{9,8},{10,9},{11,1... | collective-permute-start | bytes 786440 | tf_op jit(solution)/shard_map/ppermute | solution.py:303
  42.8 4.5 %copy-start.7 = (f32[4,16,16,128]{3,2,1,0:T(8,128)S(1)}, f32[4,16,16,128]{3,2,1,0:T(8,128)}, u32[]{:S(2)}) copy-start(f32[4,16,16,128]{3,2,1,0:T(8,128)} %param.11) | copy-start | bytes 1572868
  42.8 138.7 %all-to-all-start = ((f32[8,520,128]{2,1,0:T(8,128)}), f32[8,520,128]{2,1,0:T(8,128)}, u32[]{:S(2)}, u32[]{:S(2)}) async-start(f32[8,520,128]{2,1,0:T(8,128)} %second_kernel.1.buf_ref), calls=%async_computation | async-start | bytes 4259840 | tf_op jit(solution)/shard_map/all_to_all | solution.py:357
  47.4 60.5 %copy-start.1 = (f32[16,128,128]{2,1,0:T(8,128)S(1)}, f32[16,128,128]{2,1,0:T(8,128)}, u32[]{:S(2)}) copy-start(f32[16,128,128]{2,1,0:T(8,128)} %vel_ref.1) | copy-start | bytes 3145732
  47.5 25.0 %collective-permute-start.8 = (f32[4,16,8,128]{3,2,1,0:T(8,128)S(1)}, f32[4,16,8,128]{3,2,1,0:T(8,128)S(1)}, u32[]{:S(2)}, u32[]{:S(2)}) collective-permute-start(f32[4,16,8,128]{3,2,1,0:T(8,128)S(1)} %get-tuple-element.35), channel_id=1, source_target_pairs={{0,64},{32,96},{64,128},{96,160},{128,192},{160,224},{192,0},{224,... | collective-permute-start | bytes 786440 | tf_op jit(solution)/shard_map/ppermute | solution.py:321
  49.0 26.6 %collective-permute-start.9 = (f32[4,16,8,128]{3,2,1,0:T(8,128)S(1)}, f32[4,16,8,128]{3,2,1,0:T(8,128)S(1)}, u32[]{:S(2)}, u32[]{:S(2)}) collective-permute-start(f32[4,16,8,128]{3,2,1,0:T(8,128)S(1)} %get-tuple-element.35), channel_id=1, source_target_pairs={{0,128},{32,160},{64,192},{96,224},{128,0},{160,32},{192,64},{224,... | collective-permute-start | bytes 786440 | tf_op jit(solution)/shard_map/ppermute | solution.py:321
  51.8 23.8 %collective-permute-start.10 = (f32[4,16,8,128]{3,2,1,0:T(8,128)S(1)}, f32[4,16,8,128]{3,2,1,0:T(8,128)S(1)}, u32[]{:S(2)}, u32[]{:S(2)}) collective-permute-start(f32[4,16,8,128]{3,2,1,0:T(8,128)S(1)} %get-tuple-element.35), channel_id=1, source_target_pairs={{0,192},{32,224},{64,0},{96,32},{128,64},{160,96},{192,128},{224,1... | collective-permute-start | bytes 786440 | tf_op jit(solution)/shard_map/ppermute | solution.py:321
  75.6 2.3 %copy-start.4 = (f32[4,16,8,128]{3,2,1,0:T(8,128)}, f32[4,16,8,128]{3,2,1,0:T(8,128)S(1)}, u32[]{:S(2)}) copy-start(f32[4,16,8,128]{3,2,1,0:T(8,128)S(1)} %collective-permute-done.10) | copy-start | bytes 786436
  76.7 52.7 %collective-permute-start.11 = (f32[4,4,16,8,128]{4,3,2,1,0:T(8,128)}, f32[4,4,16,8,128]{4,3,2,1,0:T(8,128)S(1)}, u32[]{:S(2)}, u32[]{:S(2)}) collective-permute-start(f32[4,4,16,8,128]{4,3,2,1,0:T(8,128)} %pad_maximum_fusion), channel_id=1, source_target_pairs={{0,32},{32,0},{64,96},{96,64},{128,160},{160,128},{192,224},{224,1... | collective-permute-start | bytes 3145736 | tf_op jit(solution)/shard_map/ppermute | solution.py:321
  77.9 25.8 %collective-permute-start.4 = (f32[4,16,8,128]{3,2,1,0:T(8,128)S(1)}, f32[4,16,8,128]{3,2,1,0:T(8,128)S(1)}, u32[]{:S(2)}, u32[]{:S(2)}) collective-permute-start(f32[4,16,8,128]{3,2,1,0:T(8,128)S(1)} %get-tuple-element.36), channel_id=1, source_target_pairs={{0,32},{32,0},{64,96},{96,64},{128,160},{160,128},{192,224},{224,1... | collective-permute-start | bytes 786440 | tf_op jit(solution)/shard_map/ppermute | solution.py:321
  104.6 24.0 %collective-permute-start.5 = (f32[2,4,16,8,128]{4,3,2,1,0:T(8,128)}, f32[2,4,16,8,128]{4,3,2,1,0:T(8,128)}, u32[]{:S(2)}, u32[]{:S(2)}) collective-permute-start(f32[2,4,16,8,128]{4,3,2,1,0:T(8,128)} %pad_maximum_fusion.1), channel_id=1, source_target_pairs={{0,64},{32,96},{64,128},{96,160},{128,192},{160,224},{192,0},{224,... | collective-permute-start | bytes 1572872 | tf_op jit(solution)/shard_map/ppermute | solution.py:321
  104.6 24.0 %collective-permute-start.6 = (f32[2,4,16,8,128]{4,3,2,1,0:T(8,128)}, f32[2,4,16,8,128]{4,3,2,1,0:T(8,128)}, u32[]{:S(2)}, u32[]{:S(2)}) collective-permute-start(f32[2,4,16,8,128]{4,3,2,1,0:T(8,128)} %pad_maximum_fusion.1), channel_id=1, source_target_pairs={{0,128},{32,160},{64,192},{96,224},{128,0},{160,32},{192,64},{224,... | collective-permute-start | bytes 1572872 | tf_op jit(solution)/shard_map/ppermute | solution.py:321
  106.8 22.6 %collective-permute-start.7 = (f32[2,4,16,8,128]{4,3,2,1,0:T(8,128)}, f32[2,4,16,8,128]{4,3,2,1,0:T(8,128)}, u32[]{:S(2)}, u32[]{:S(2)}) collective-permute-start(f32[2,4,16,8,128]{4,3,2,1,0:T(8,128)} %pad_maximum_fusion.1), channel_id=1, source_target_pairs={{0,192},{32,224},{64,0},{96,32},{128,64},{160,96},{192,128},{224,1... | collective-permute-start | bytes 1572872 | tf_op jit(solution)/shard_map/ppermute | solution.py:321
  107.8 1.0 copy-start.5
  139.0 19.6 %collective-permute-start.12 = (f32[56,512]{1,0:T(8,128)S(1)}, f32[56,512]{1,0:T(8,128)S(1)}, u32[]{:S(2)}, u32[]{:S(2)}) collective-permute-start(f32[56,512]{1,0:T(8,128)S(1)} %get-tuple-element.29), channel_id=1, source_target_pairs={{0,1},{1,2},{2,3},{3,4},{4,5},{5,6},{6,7},{7,8},{8,9},{9,10},{10,1... | collective-permute-start | bytes 344072 | tf_op jit(solution)/shard_map/ppermute | solution.py:303
  156.7 7.0 %collective-permute-start.13 = (f32[56,512]{1,0:T(8,128)S(1)}, f32[56,512]{1,0:T(8,128)S(1)}, u32[]{:S(2)}, u32[]{:S(2)}) collective-permute-start(f32[56,512]{1,0:T(8,128)S(1)} %get-tuple-element.30), channel_id=1, source_target_pairs={{1,0},{2,1},{3,2},{4,3},{5,4},{6,5},{7,6},{8,7},{9,8},{10,9},{11,1... | collective-permute-start | bytes 344072 | tf_op jit(solution)/shard_map/ppermute | solution.py:303
  164.7 6.8 %collective-permute-start.18 = (f32[96,512]{1,0:T(8,128)}, f32[96,512]{1,0:T(8,128)}, u32[]{:S(2)}, u32[]{:S(2)}) collective-permute-start(f32[96,512]{1,0:T(8,128)} %late_kernel.1.refs_0_), channel_id=1, source_target_pairs={{0,32},{32,0},{64,96},{96,64},{128,160},{160,128},{192,224},{224,1... | collective-permute-start | bytes 589832 | tf_op jit(solution)/shard_map/ppermute | solution.py:321
  166.4 10.8 %collective-permute-start.19 = (f32[96,512]{1,0:T(8,128)}, f32[96,512]{1,0:T(8,128)}, u32[]{:S(2)}, u32[]{:S(2)}) collective-permute-start(f32[96,512]{1,0:T(8,128)} %late_kernel.1.refs_0_), channel_id=1, source_target_pairs={{0,64},{32,96},{64,0},{96,32},{128,192},{160,224},{192,128},{224,1... | collective-permute-start | bytes 589832 | tf_op jit(solution)/shard_map/ppermute | solution.py:321
  167.8 13.6 %collective-permute-start.20 = (f32[96,512]{1,0:T(8,128)}, f32[96,512]{1,0:T(8,128)}, u32[]{:S(2)}, u32[]{:S(2)}) collective-permute-start(f32[96,512]{1,0:T(8,128)} %late_kernel.1.refs_0_), channel_id=1, source_target_pairs={{0,192},{32,224},{64,128},{96,160},{128,64},{160,96},{192,0},{224,... | collective-permute-start | bytes 589832 | tf_op jit(solution)/shard_map/ppermute | solution.py:321
  169.1 20.7 %collective-permute-start.14 = (f32[96,512]{1,0:T(8,128)}, f32[96,512]{1,0:T(8,128)}, u32[]{:S(2)}, u32[]{:S(2)}) collective-permute-start(f32[96,512]{1,0:T(8,128)} %late_kernel.1.refs_0_), channel_id=1, source_target_pairs={{0,96},{32,64},{64,32},{96,0},{128,224},{160,192},{192,160},{224,1... | collective-permute-start | bytes 589832 | tf_op jit(solution)/shard_map/ppermute | solution.py:321
  169.7 20.1 %collective-permute-start.15 = (f32[96,512]{1,0:T(8,128)}, f32[96,512]{1,0:T(8,128)}, u32[]{:S(2)}, u32[]{:S(2)}) collective-permute-start(f32[96,512]{1,0:T(8,128)} %late_kernel.1.refs_0_), channel_id=1, source_target_pairs={{0,224},{32,192},{64,160},{96,128},{128,96},{160,64},{192,32},{224... | collective-permute-start | bytes 589832 | tf_op jit(solution)/shard_map/ppermute | solution.py:321
  171.5 18.3 %collective-permute-start.16 = (f32[96,512]{1,0:T(8,128)}, f32[96,512]{1,0:T(8,128)}, u32[]{:S(2)}, u32[]{:S(2)}) collective-permute-start(f32[96,512]{1,0:T(8,128)} %late_kernel.1.refs_0_), channel_id=1, source_target_pairs={{0,128},{32,160},{64,192},{96,224},{128,0},{160,32},{192,64},{224,... | collective-permute-start | bytes 589832 | tf_op jit(solution)/shard_map/ppermute | solution.py:321
  177.2 12.7 %collective-permute-start.17 = (f32[96,512]{1,0:T(8,128)}, f32[96,512]{1,0:T(8,128)}, u32[]{:S(2)}, u32[]{:S(2)}) collective-permute-start(f32[96,512]{1,0:T(8,128)} %late_kernel.1.refs_0_), channel_id=1, source_target_pairs={{0,160},{32,128},{64,224},{96,192},{128,32},{160,0},{192,96},{224,... | collective-permute-start | bytes 589832 | tf_op jit(solution)/shard_map/ppermute | solution.py:321

commit v2 on v1

--- a/solution.py
+++ b/solution.py
@@ -157,15 +157,20 @@
     else:
         for ref in (first_ref, sigma_ref, v_ref):
             ref[...] = jnp.zeros_like(ref)
+    jobs = []
     for m_ref, plan, pieces in zip(m_refs, plans, counts):
-
-        def body(i, carry, m_ref=m_ref, plan=plan):
-            half = plan[0]
+        if plan[0] is None:
+            jobs += [(m_ref, plan, 1, 0), (m_ref, plan, 1, 1)]
+        else:
+            jobs += [(m_ref, plan, pieces, plan[0])]
+    for m_ref, plan, pieces, half in jobs:
+
+        def body(i, carry, m_ref=m_ref, plan=plan, half=half):
             strip = strip_of(me_ref[0], rounds, plan, i)
             x_rows = rows_of(x_row, strip * 16 + half * 8, 8)
             for x in range(8):
                 fill(x_rows, spot, side, x, spot_ref, lap_ref, x * width)
-                m = m_ref[i, pl.ds(x, rows, stride=8), :]
+                m = m_ref[0, pl.ds(half * 8 + x, rows, stride=16), :] if plan[0] is None else m_ref[i, pl.ds(x, rows, stride=8), :]
                 born = buf_ref[strip, pl.ds(half * count * 8 + x, count, stride=8), :]
                 both = buf_ref[strip, pl.ds((2 + half) * count * 8 + x, count, stride=8), :]
                 vel = vel_ref[pl.ds(strip * 16 + half * 8 + x, count, stride=width), :]
@@ -310,8 +315,8 @@
     n_wells = receiver_wells.shape[1]
     rows = probes * count
     me = lax.axis_index("shot").reshape(1).astype(jnp.int32)
-    params = pltpu.CompilerParams(vmem_limit_bytes=32 * 1024 * 1024)
-    gather_params = pltpu.CompilerParams(vmem_limit_bytes=32 * 1024 * 1024)
+    params = pltpu.CompilerParams(vmem_limit_bytes=52 * 1024 * 1024)
+    gather_params = pltpu.CompilerParams(vmem_limit_bytes=40 * 1024 * 1024)
     image_params = pltpu.CompilerParams(vmem_limit_bytes=67043328)
 
     rounds = strips // 2
@@ -323,14 +328,13 @@
     def ring(shift):
         return [(i, (i + 2 * shift) % strips) for i in range(strips)]
 
-    part_a, part_b = probe_panel[:, :, :8], probe_panel[:, :, 8:]
     now_low, now_high = spread(wave_now[0, :4], wave_now[0, count - 4 :])
-    a_swapped = sent(part_a, swap)
+    swapped = sent(probe_panel, swap)
+    part_b = probe_panel[:, :, 8:]
     b_ring = [sent(part_b, ring(s)) for s in range(1, rounds)]
-    a_pair = jnp.stack([part_a, a_swapped])
-    b_all = jnp.stack([part_b] + b_ring)
+    a_pair = jnp.stack([probe_panel[:, :, :8], swapped[:, :, :8]])
     a_ring = [sent(a_pair, ring(s)) for s in range(1, rounds)]
-    b_other = sent(b_all, swap)
+    b_other = sent(jnp.stack(b_ring), swap)
 
     slab_id = lax.axis_index("space").reshape(1).astype(jnp.int32)
     plane = jax.ShapeDtypeStruct((count, width, width), F32)
@@ -361,7 +365,7 @@
     edge_rows = 12 * probes + 8
 
     def gather(parts, plans, start=()):
-        parts = [part.reshape(-1, rows * 8, width) for part in parts]
+        parts = [part.reshape(-1, rows * (16 if plan[0] is None else 8), width) for part, plan in zip(parts, plans)]
         counts = tuple(part.shape[0] for part in parts)
         out_shape = (compact, compact, compact_v)
         if start:
@@ -379,9 +383,9 @@
             compiler_params=gather_params,
         )(me, receiver_wells, velocity.reshape(count * width, width), buf, *parts, *start)
 
-    own_plans = ((0, 0, 0, 0, 0), (0, 0, 0, 1, 0)) + tuple((1, s, 0, 0, 0) for s in range(rounds))
-    own = gather([part_a, a_swapped, part_b] + b_ring, own_plans)
-    far_plans = tuple((0, s, 0, 0, 1) for s in range(1, rounds)) + ((1, 0, 1, 1, 0),)
+    own_plans = ((None, 0, 0, 0, 0), (None, 0, 0, 1, 0)) + tuple((1, s, 0, 0, 0) for s in range(1, rounds))
+    own = gather([probe_panel, swapped] + b_ring, own_plans)
+    far_plans = tuple((0, s, 0, 0, 1) for s in range(1, rounds)) + ((1, 1, 1, 1, 0),)
     first, sigma, vel, send_low, send_high = gather(a_ring + [b_other], far_plans, own)
     low, high = spread(send_low, send_high)
     deep = count + 8

time: 203 us -> 182 us (0.90)
  the two profiles are of different devices: /device:TPU:1 before, /device:TPU:10 now
where the time goes in v2:
time: 182 us; the launch traced here: 181 us
  starting transfers between devices  64.4 us (35%)
  waiting for transfers between devices  62.7 us (34%)
  Pallas kernels  44.7 us (25%)
  local copies, waits for them, and re-layouts  5.49 us (3%)
  between operations  2.08 us (1%)
  other arithmetic  1.94 us (1%)
    ppermute x15, waiting for transfers between devices, sent(): return lax.ppermute(value, 'shot', pairs)  49.3 us
    ppermute x15, starting transfers between devices, sent(): return lax.ppermute(value, 'shot', pairs)  32.4 us
    pallas_call x3, Pallas kernels, image(): pl.pallas_call(functools.partial(image_kernel, count, probes, flips, scal...  22.7 us
    ppermute x3, starting transfers between devices, spread(): lax.ppermute(low_layers, axis, backward)  20.6 us
    pallas_call x2, Pallas kernels, gather(): pl.pallas_call(functools.partial(gather_kernel, count, probes, rounds, pl...  12.4 us
    ppermute x3, waiting for transfers between devices, spread(): lax.ppermute(low_layers, axis, backward)  9.07 us
    ppermute x3, starting transfers between devices, spread(): lax.ppermute(high_layers, axis, forward)  6.26 us
    all_to_all x1, starting transfers between devices, slab(): shared = lax.all_to_all(buf, 'shot', 0, 0, tiled=True)  5.05 us
  transfers between devices with their start and end apart: 22, of which 13 were waited for; matrix products, arithmetic and copies ran while one was open for 1% of the time, Pallas kernels for 14%

profile of v2, /device:TPU:10, one launch (start us, length us, event | category | flops | bytes accessed | tf_op | source)
XLA Modules:
  0.0 181.3 jit_solution(6404322093655730677)
XLA Ops:
  0.0 1.1 slice_bitcast_fusion.2
  1.1 1.9 %collective-permute-start = (f32[4,128,128]{2,1,0:T(8,128)S(1)}, f32[4,128,128]{2,1,0:T(8,128)S(1)}, u32[]{:S(2)}, u32[]{:S(2)}) collective-permute-start(f32[4,128,128]{2,1,0:T(8,128)S(1)} %get-tuple-element.32), channel_id=1, source_target_pairs={{0,1},{1,2},{2,3},{3,4},{4,5},{5,6},{6,7},{7,8},{8,9},{9,10},{10,1... | collective-permute-start | bytes 786440 | tf_op jit(solution)/shard_map/ppermute | solution.py:308
  3.0 7.6 %collective-permute-start.1 = (f32[4,128,128]{2,1,0:T(8,128)S(1)}, f32[4,128,128]{2,1,0:T(8,128)S(1)}, u32[]{:S(2)}, u32[]{:S(2)}) collective-permute-start(f32[4,128,128]{2,1,0:T(8,128)S(1)} %get-tuple-element.31), channel_id=1, source_target_pairs={{1,0},{2,1},{3,2},{4,3},{5,4},{6,5},{7,6},{8,7},{9,8},{10,9},{11,1... | collective-permute-start | bytes 786440 | tf_op jit(solution)/shard_map/ppermute | solution.py:308
  12.6 0.8 collective-permute-done.low_ref
  13.3 4.0 %collective-permute-done.1.high_ref = f32[4,128,128]{2,1,0:T(8,128)S(1)} collective-permute-done((f32[4,128,128]{2,1,0:T(8,128)S(1)}, f32[4,128,128]{2,1,0:T(8,128)S(1)}, u32[]{:S(2)}, u32[]{:S(2)}) %collective-permute-start.1) | collective-permute-done | bytes 262176 | tf_op jit(solution)/shard_map/ppermute | solution.py:308
  17.3 4.7 %step_kernel.1 = (f32[16,128,128]{2,1,0:T(8,128)}, f32[16,128,128]{2,1,0:T(8,128)}, f32[16,128,128]{2,1,0:T(8,128)}, f32[4,128,128]{2,1,0:T(8,128)S(1)}, f32[4,128,128]{2,1,0:T(8,128)S(1)}) custom-call(s32[1]{0:T(128)} %bitcast.1.slab_ref, s32[1]{0:T(128)S(6)} %copy.9.depth_ref, s32[1]{0:T(128)S(6)} %copy.10.column_ref, f32[1]{0:T(128)S(6)} %copy.11.strength_ref, ...), custom_call_target="tpu_custom_call" | custom-call | tf_op jit(solution)/shard_map/step_kernel/pallas_call | solution.py:342
  22.0 2.4 %collective-permute-start.2 = (f32[4,128,128]{2,1,0:T(8,128)S(1)}, f32[4,128,128]{2,1,0:T(8,128)S(1)}, u32[]{:S(2)}, u32[]{:S(2)}) collective-permute-start(f32[4,128,128]{2,1,0:T(8,128)S(1)} %get-tuple-element.19), channel_id=1, source_target_pairs={{0,1},{1,2},{2,3},{3,4},{4,5},{5,6},{6,7},{7,8},{8,9},{9,10},{10,1... | collective-permute-start | bytes 786440 | tf_op jit(solution)/shard_map/ppermute | solution.py:308
  24.4 6.4 %collective-permute-start.3 = (f32[4,128,128]{2,1,0:T(8,128)S(1)}, f32[4,128,128]{2,1,0:T(8,128)S(1)}, u32[]{:S(2)}, u32[]{:S(2)}) collective-permute-start(f32[4,128,128]{2,1,0:T(8,128)S(1)} %get-tuple-element.20), channel_id=1, source_target_pairs={{1,0},{2,1},{3,2},{4,3},{5,4},{6,5},{7,6},{8,7},{9,8},{10,9},{11,1... | collective-permute-start | bytes 786440 | tf_op jit(solution)/shard_map/ppermute | solution.py:308
  30.8 3.0 %collective-permute-done.2.low_ref = f32[4,128,128]{2,1,0:T(8,128)S(1)} collective-permute-done((f32[4,128,128]{2,1,0:T(8,128)S(1)}, f32[4,128,128]{2,1,0:T(8,128)S(1)}, u32[]{:S(2)}, u32[]{:S(2)}) %collective-permute-start.2) | collective-permute-done | bytes 262176 | tf_op jit(solution)/shard_map/ppermute | solution.py:308
  33.8 2.2 %collective-permute-done.3.high_ref = f32[4,128,128]{2,1,0:T(8,128)S(1)} collective-permute-done((f32[4,128,128]{2,1,0:T(8,128)S(1)}, f32[4,128,128]{2,1,0:T(8,128)S(1)}, u32[]{:S(2)}, u32[]{:S(2)}) %collective-permute-start.3) | collective-permute-done | bytes 262176 | tf_op jit(solution)/shard_map/ppermute | solution.py:308
  36.0 1.2 copy-done.7
  37.2 4.0 %second_kernel.1.buf_ref = f32[8,520,128]{2,1,0:T(8,128)} custom-call(s32[1,512]{1,0:T(1,128)S(1)} %copy-done.8, f32[16,128,128]{2,1,0:T(8,128)S(1)} %copy-done.7, f32[4,128,128]{2,1,0:T(8,128)S(1)} %collective-permute-done.2.low_ref, f32[4,128,128]{2,1,0:T(8,128)S(1)} %collective-permute-done.3.high_ref, f32[16,128,128]{2,1,0:T(8,128)} %get-tuple-element.21.born_ref, ...), custom_call_target="tpu_custom_call" | custom-call | tf_op jit(solution)/shard_map/second_kernel/pallas_call | solution.py:353
  41.2 5.0 %all-to-all-start = ((f32[8,520,128]{2,1,0:T(8,128)}), f32[8,520,128]{2,1,0:T(8,128)}, u32[]{:S(2)}, u32[]{:S(2)}) async-start(f32[8,520,128]{2,1,0:T(8,128)} %second_kernel.1.buf_ref), calls=%async_computation | async-start | bytes 4259840 | tf_op jit(solution)/shard_map/all_to_all | solution.py:361
  46.3 1.5 collective-permute-start.4
  47.9 1.5 collective-permute-start.8
  49.4 1.2 collective-permute-start.9
  50.6 2.1 %collective-permute-start.10 = (f32[4,16,8,128]{3,2,1,0:T(8,128)S(1)}, f32[4,16,8,128]{3,2,1,0:T(8,128)S(1)}, u32[]{:S(2)}, u32[]{:S(2)}) collective-permute-start(f32[4,16,8,128]{3,2,1,0:T(8,128)S(1)} %get-tuple-element.33), channel_id=1, source_target_pairs={{0,192},{32,224},{64,0},{96,32},{128,64},{160,96},{192,128},{224,1... | collective-permute-start | bytes 786440 | tf_op jit(solution)/shard_map/ppermute | solution.py:326
  52.6 23.3 %collective-permute-done.8 = f32[4,16,8,128]{3,2,1,0:T(8,128)S(1)} collective-permute-done((f32[4,16,8,128]{3,2,1,0:T(8,128)S(1)}, f32[4,16,8,128]{3,2,1,0:T(8,128)S(1)}, u32[]{:S(2)}, u32[]{:S(2)}) %collective-permute-start.8) | collective-permute-done | bytes 262176 | tf_op jit(solution)/shard_map/ppermute | solution.py:326
  75.9 2.1 %collective-permute-done.9 = f32[4,16,8,128]{3,2,1,0:T(8,128)S(1)} collective-permute-done((f32[4,16,8,128]{3,2,1,0:T(8,128)S(1)}, f32[4,16,8,128]{3,2,1,0:T(8,128)S(1)}, u32[]{:S(2)}, u32[]{:S(2)}) %collective-permute-start.9) | collective-permute-done | bytes 262176 | tf_op jit(solution)/shard_map/ppermute | solution.py:326
  78.1 5.0 %collective-permute-done.10 = f32[4,16,8,128]{3,2,1,0:T(8,128)S(1)} collective-permute-done((f32[4,16,8,128]{3,2,1,0:T(8,128)S(1)}, f32[4,16,8,128]{3,2,1,0:T(8,128)S(1)}, u32[]{:S(2)}, u32[]{:S(2)}) %collective-permute-start.10) | collective-permute-done | bytes 262176 | tf_op jit(solution)/shard_map/ppermute | solution.py:326
  83.1 1.1 pad_maximum_fusion
  84.2 1.9 %collective-permute-start.11 = (f32[3,4,16,8,128]{4,3,2,1,0:T(8,128)}, f32[3,4,16,8,128]{4,3,2,1,0:T(8,128)}, u32[]{:S(2)}, u32[]{:S(2)}) collective-permute-start(f32[3,4,16,8,128]{4,3,2,1,0:T(8,128)} %pad_maximum_fusion), channel_id=1, source_target_pairs={{0,32},{32,0},{64,96},{96,64},{128,160},{160,128},{192,224},{224,1... | collective-permute-start | bytes 2359304 | tf_op jit(solution)/shard_map/ppermute | solution.py:326
  86.1 0.8 pad_maximum_fusion.1
  86.9 1.2 collective-permute-start.5
  88.1 2.6 %collective-permute-start.6 = (f32[2,4,16,8,128]{4,3,2,1,0:T(8,128)}, f32[2,4,16,8,128]{4,3,2,1,0:T(8,128)}, u32[]{:S(2)}, u32[]{:S(2)}) collective-permute-start(f32[2,4,16,8,128]{4,3,2,1,0:T(8,128)} %pad_maximum_fusion.1), channel_id=1, source_target_pairs={{0,128},{32,160},{64,192},{96,224},{128,0},{160,32},{192,64},{224,... | collective-permute-start | bytes 1572872 | tf_op jit(solution)/shard_map/ppermute | solution.py:326
  90.7 1.2 copy-done.2
  91.9 0.9 copy-done.4
  92.9 0.9 copy-done.6
  93.8 3.9 %shard_map.82 = (f32[64,512]{1,0:T(8,128)S(1)}, f32[64,512]{1,0:T(8,128)S(1)}, f32[16,512]{1,0:T(8,128)S(1)}) custom-call(s32[1]{0:T(128)} %bitcast.me_ref, s32[1,512]{1,0:T(1,128)S(1)} %copy-done.8, f32[2048,128]{1,0:T(8,128)S(1)} %bitcast.31, f32[8,520,128]{2,1,0:T(8,128)S(1)} %copy-done, f32[1,1024,128]{2,1,0:T(8,128)S(1)} %bitcast.30, ...), custom_call_target="tpu_custom_call" | custom-call | tf_op jit(solution)/shard_map/pallas_call | solution.py:373
  97.8 6.5 %collective-permute-done.11 = f32[3,4,16,8,128]{4,3,2,1,0:T(8,128)} collective-permute-done((f32[3,4,16,8,128]{4,3,2,1,0:T(8,128)}, f32[3,4,16,8,128]{4,3,2,1,0:T(8,128)}, u32[]{:S(2)}, u32[]{:S(2)}) %collective-permute-start.11) | collective-permute-done | bytes 786464 | tf_op jit(solution)/shard_map/ppermute | solution.py:326
  104.2 0.5 collective-permute-done.6
  104.8 9.8 %collective-permute-done.7 = f32[2,4,16,8,128]{4,3,2,1,0:T(8,128)} collective-permute-done((f32[2,4,16,8,128]{4,3,2,1,0:T(8,128)}, f32[2,4,16,8,128]{4,3,2,1,0:T(8,128)}, u32[]{:S(2)}, u32[]{:S(2)}) %collective-permute-start.7) | collective-permute-done | bytes 524320 | tf_op jit(solution)/shard_map/ppermute | solution.py:326
  114.6 8.5 %shard_map.83 = (f32[64,512]{1,0:T(8,128)S(1)}, f32[64,512]{1,0:T(8,128)S(1)}, f32[16,512]{1,0:T(8,128)S(1)}, f32[56,512]{1,0:T(8,128)S(1)}, f32[56,512]{1,0:T(8,128)S(1)}) custom-call(s32[1]{0:T(128)} %bitcast.me_ref, s32[1,512]{1,0:T(1,128)S(1)} %copy-done.8, f32[2048,128]{1,0:T(8,128)S(1)} %bitcast.32, f32[8,520,128]{2,1,0:T(8,128)S(1)} %copy-done, ...), custom_call_target="tpu_custom_call" | custom-call | tf_op jit(solution)/shard_map/pallas_call | solution.py:373
  123.0 1.9 %collective-permute-start.12 = (f32[56,512]{1,0:T(8,128)S(1)}, f32[56,512]{1,0:T(8,128)S(1)}, u32[]{:S(2)}, u32[]{:S(2)}) collective-permute-start(f32[56,512]{1,0:T(8,128)S(1)} %get-tuple-element.29), channel_id=1, source_target_pairs={{0,1},{1,2},{2,3},{3,4},{4,5},{5,6},{6,7},{7,8},{8,9},{9,10},{10,1... | collective-permute-start | bytes 344072 | tf_op jit(solution)/shard_map/ppermute | solution.py:308
  124.9 6.6 %collective-permute-start.13 = (f32[56,512]{1,0:T(8,128)S(1)}, f32[56,512]{1,0:T(8,128)S(1)}, u32[]{:S(2)}, u32[]{:S(2)}) collective-permute-start(f32[56,512]{1,0:T(8,128)S(1)} %get-tuple-element.30), channel_id=1, source_target_pairs={{1,0},{2,1},{3,2},{4,3},{5,4},{6,5},{7,6},{8,7},{9,8},{10,9},{11,1... | collective-permute-start | bytes 344072 | tf_op jit(solution)/shard_map/ppermute | solution.py:308
  131.6 0.6 collective-permute-done.12.low_ref
  132.2 2.9 %collective-permute-done.13.high_ref = f32[56,512]{1,0:T(8,128)S(1)} collective-permute-done((f32[56,512]{1,0:T(8,128)S(1)}, f32[56,512]{1,0:T(8,128)S(1)}, u32[]{:S(2)}, u32[]{:S(2)}) %collective-permute-start.13) | collective-permute-done | bytes 114720 | tf_op jit(solution)/shard_map/ppermute | solution.py:308
  135.1 1.0 late_kernel.1.refs_0_
  136.3 1.1 collective-permute-start.19
  137.4 2.0 %collective-permute-start.20 = (f32[96,512]{1,0:T(8,128)}, f32[96,512]{1,0:T(8,128)}, u32[]{:S(2)}, u32[]{:S(2)}) collective-permute-start(f32[96,512]{1,0:T(8,128)} %late_kernel.1.refs_0_), channel_id=1, source_target_pairs={{0,192},{32,224},{64,128},{96,160},{128,64},{160,96},{192,0},{224,... | collective-permute-start | bytes 589832 | tf_op jit(solution)/shard_map/ppermute | solution.py:326
  139.4 2.1 %collective-permute-start.14 = (f32[96,512]{1,0:T(8,128)}, f32[96,512]{1,0:T(8,128)}, u32[]{:S(2)}, u32[]{:S(2)}) collective-permute-start(f32[96,512]{1,0:T(8,128)} %late_kernel.1.refs_0_), channel_id=1, source_target_pairs={{0,96},{32,64},{64,32},{96,0},{128,224},{160,192},{192,160},{224,1... | collective-permute-start | bytes 589832 | tf_op jit(solution)/shard_map/ppermute | solution.py:326
  141.5 0.4 collective-permute-start.15
  141.9 2.0 %collective-permute-done.18.refs_0_ = f32[96,512]{1,0:T(8,128)} collective-permute-done((f32[96,512]{1,0:T(8,128)}, f32[96,512]{1,0:T(8,128)}, u32[]{:S(2)}, u32[]{:S(2)}) %collective-permute-start.18) | collective-permute-done | bytes 196640 | tf_op jit(solution)/shard_map/ppermute | solution.py:326
  143.9 3.0 %collective-permute-start.16 = (f32[96,512]{1,0:T(8,128)}, f32[96,512]{1,0:T(8,128)}, u32[]{:S(2)}, u32[]{:S(2)}) collective-permute-start(f32[96,512]{1,0:T(8,128)} %late_kernel.1.refs_0_), channel_id=1, source_target_pairs={{0,128},{32,160},{64,192},{96,224},{128,0},{160,32},{192,64},{224,... | collective-permute-start | bytes 589832 | tf_op jit(solution)/shard_map/ppermute | solution.py:326
  147.0 11.7 %collective-permute-start.17 = (f32[96,512]{1,0:T(8,128)}, f32[96,512]{1,0:T(8,128)}, u32[]{:S(2)}, u32[]{:S(2)}) collective-permute-start(f32[96,512]{1,0:T(8,128)} %late_kernel.1.refs_0_), channel_id=1, source_target_pairs={{0,160},{32,128},{64,224},{96,192},{128,32},{160,0},{192,96},{224,... | collective-permute-start | bytes 589832 | tf_op jit(solution)/shard_map/ppermute | solution.py:326
  158.6 3.9 %shard_map.84.refs_3_ = f32[1024,128]{1,0:T(8,128)} custom-call(s32[1]{0:T(128)} %bitcast.me_ref, f32[8,520,128]{2,1,0:T(8,128)} %second_kernel.1.buf_ref, f32[1024,128]{1,0:T(8,128)} %bitcast.27, f32[96,512]{1,0:T(8,128)} %late_kernel.1.refs_0_), custom_call_target="tpu_custom_call" | custom-call | tf_op jit(solution)/shard_map/pallas_call | solution.py:420
  162.5 8.3 %shard_map.85.refs_4_ = f32[1024,128]{1,0:T(8,128)} custom-call(s32[1]{0:T(128)} %bitcast.me_ref, f32[8,520,128]{2,1,0:T(8,128)} %all-to-all-done.buf_ref, f32[1024,128]{1,0:T(8,128)} %bitcast.28, f32[96,512]{1,0:T(8,128)} %collective-permute-done.18.refs_0_, f32[96,512]{1,0:T(8,128)} %collective-permute-done.19.refs_1_, ...), custom_call_target="tpu_custom_call" | custom-call | tf_op jit(solution)/shard_map/pallas_call | solution.py:420
  170.9 10.4 %shard_map.86 = f32[1024,128]{1,0:T(8,128)} custom-call(s32[1]{0:T(128)} %bitcast.me_ref, f32[8,520,128]{2,1,0:T(8,128)} %all-to-all-done.buf_ref, f32[1024,128]{1,0:T(8,128)} %bitcast.29, f32[96,512]{1,0:T(8,128)} %collective-permute-done.14.refs_0_, f32[96,512]{1,0:T(8,128)} %collective-permute-done.15.refs_1_, f32[96,512]{1,0:T(8,128)} %collective-permute-done.16.refs_2_, ...), custom_call_target="tpu_custom_call" | custom-call | tf_op jit(solution)/shard_map/pallas_call | solution.py:420
  (27 shorter events, 0.3 us)
Async XLA Ops:
  0.0 35.9 %copy-start.8 = (s32[1,512]{1,0:T(1,128)S(1)}, s32[1,512]{1,0:T(1,128)}, u32[]{:S(2)}) copy-start(s32[1,512]{1,0:T(1,128)} %wells_ref.5) | copy-start | bytes 6148
  1.1 12.3 %collective-permute-start = (f32[4,128,128]{2,1,0:T(8,128)S(1)}, f32[4,128,128]{2,1,0:T(8,128)S(1)}, u32[]{:S(2)}, u32[]{:S(2)}) collective-permute-start(f32[4,128,128]{2,1,0:T(8,128)S(1)} %get-tuple-element.32), channel_id=1, source_target_pairs={{0,1},{1,2},{2,3},{3,4},{4,5},{5,6},{6,7},{7,8},{8,9},{9,10},{10,1... | collective-permute-start | bytes 786440 | tf_op jit(solution)/shard_map/ppermute | solution.py:308
  3.0 14.3 %collective-permute-start.1 = (f32[4,128,128]{2,1,0:T(8,128)S(1)}, f32[4,128,128]{2,1,0:T(8,128)S(1)}, u32[]{:S(2)}, u32[]{:S(2)}) collective-permute-start(f32[4,128,128]{2,1,0:T(8,128)S(1)} %get-tuple-element.31), channel_id=1, source_target_pairs={{1,0},{2,1},{3,2},{4,3},{5,4},{6,5},{7,6},{8,7},{9,8},{10,9},{11,1... | collective-permute-start | bytes 786440 | tf_op jit(solution)/shard_map/ppermute | solution.py:308
  22.0 11.8 %collective-permute-start.2 = (f32[4,128,128]{2,1,0:T(8,128)S(1)}, f32[4,128,128]{2,1,0:T(8,128)S(1)}, u32[]{:S(2)}, u32[]{:S(2)}) collective-permute-start(f32[4,128,128]{2,1,0:T(8,128)S(1)} %get-tuple-element.19), channel_id=1, source_target_pairs={{0,1},{1,2},{2,3},{3,4},{4,5},{5,6},{6,7},{7,8},{8,9},{9,10},{10,1... | collective-permute-start | bytes 786440 | tf_op jit(solution)/shard_map/ppermute | solution.py:308
  24.4 11.5 %collective-permute-start.3 = (f32[4,128,128]{2,1,0:T(8,128)S(1)}, f32[4,128,128]{2,1,0:T(8,128)S(1)}, u32[]{:S(2)}, u32[]{:S(2)}) collective-permute-start(f32[4,128,128]{2,1,0:T(8,128)S(1)} %get-tuple-element.20), channel_id=1, source_target_pairs={{1,0},{2,1},{3,2},{4,3},{5,4},{6,5},{7,6},{8,7},{9,8},{10,9},{11,1... | collective-permute-start | bytes 786440 | tf_op jit(solution)/shard_map/ppermute | solution.py:308
  35.9 1.2 copy-start.7
  41.2 5.1 %copy-start.1 = (f32[4,16,16,128]{3,2,1,0:T(8,128)S(1)}, f32[4,16,16,128]{3,2,1,0:T(8,128)}, u32[]{:S(2)}) copy-start(f32[4,16,16,128]{3,2,1,0:T(8,128)} %param.11) | copy-start | bytes 1572868
  41.2 121.3 %all-to-all-start = ((f32[8,520,128]{2,1,0:T(8,128)}), f32[8,520,128]{2,1,0:T(8,128)}, u32[]{:S(2)}, u32[]{:S(2)}) async-start(f32[8,520,128]{2,1,0:T(8,128)} %second_kernel.1.buf_ref), calls=%async_computation | async-start | bytes 4259840 | tf_op jit(solution)/shard_map/all_to_all | solution.py:361
  46.3 44.4 %copy-start = (f32[8,520,128]{2,1,0:T(8,128)S(1)}, f32[8,520,128]{2,1,0:T(8,128)}, u32[]{:S(2)}) copy-start(f32[8,520,128]{2,1,0:T(8,128)} %second_kernel.1.buf_ref) | copy-start | bytes 6389764
  46.3 39.8 %collective-permute-start.4 = (f32[4,16,16,128]{3,2,1,0:T(8,128)S(1)}, f32[4,16,16,128]{3,2,1,0:T(8,128)S(1)}, u32[]{:S(2)}, u32[]{:S(2)}) collective-permute-start(f32[4,16,16,128]{3,2,1,0:T(8,128)S(1)} %copy-done.1), channel_id=1, source_target_pairs={{0,32},{32,0},{64,96},{96,64},{128,160},{160,128},{192,224},{224,1... | collective-permute-start | bytes 1572872 | tf_op jit(solution)/shard_map/ppermute | solution.py:326
  47.9 28.1 %collective-permute-start.8 = (f32[4,16,8,128]{3,2,1,0:T(8,128)S(1)}, f32[4,16,8,128]{3,2,1,0:T(8,128)S(1)}, u32[]{:S(2)}, u32[]{:S(2)}) collective-permute-start(f32[4,16,8,128]{3,2,1,0:T(8,128)S(1)} %get-tuple-element.33), channel_id=1, source_target_pairs={{0,64},{32,96},{64,128},{96,160},{128,192},{160,224},{192,0},{224,... | collective-permute-start | bytes 786440 | tf_op jit(solution)/shard_map/ppermute | solution.py:326
  49.4 28.7 %collective-permute-start.9 = (f32[4,16,8,128]{3,2,1,0:T(8,128)S(1)}, f32[4,16,8,128]{3,2,1,0:T(8,128)S(1)}, u32[]{:S(2)}, u32[]{:S(2)}) collective-permute-start(f32[4,16,8,128]{3,2,1,0:T(8,128)S(1)} %get-tuple-element.33), channel_id=1, source_target_pairs={{0,128},{32,160},{64,192},{96,224},{128,0},{160,32},{192,64},{224,... | collective-permute-start | bytes 786440 | tf_op jit(solution)/shard_map/ppermute | solution.py:326
  50.6 32.5 %collective-permute-start.10 = (f32[4,16,8,128]{3,2,1,0:T(8,128)S(1)}, f32[4,16,8,128]{3,2,1,0:T(8,128)S(1)}, u32[]{:S(2)}, u32[]{:S(2)}) collective-permute-start(f32[4,16,8,128]{3,2,1,0:T(8,128)S(1)} %get-tuple-element.33), channel_id=1, source_target_pairs={{0,192},{32,224},{64,0},{96,32},{128,64},{160,96},{192,128},{224,1... | collective-permute-start | bytes 786440 | tf_op jit(solution)/shard_map/ppermute | solution.py:326
  78.1 8.0 %copy-start.3 = (f32[4,16,8,128]{3,2,1,0:T(8,128)}, f32[4,16,8,128]{3,2,1,0:T(8,128)S(1)}, u32[]{:S(2)}) copy-start(f32[4,16,8,128]{3,2,1,0:T(8,128)S(1)} %collective-permute-done.9) | copy-start | bytes 786436
  83.1 3.0 %copy-start.5 = (f32[4,16,8,128]{3,2,1,0:T(8,128)}, f32[4,16,8,128]{3,2,1,0:T(8,128)S(1)}, u32[]{:S(2)}) copy-start(f32[4,16,8,128]{3,2,1,0:T(8,128)S(1)} %collective-permute-done.10) | copy-start | bytes 786436
  84.2 20.0 %collective-permute-start.11 = (f32[3,4,16,8,128]{4,3,2,1,0:T(8,128)}, f32[3,4,16,8,128]{4,3,2,1,0:T(8,128)}, u32[]{:S(2)}, u32[]{:S(2)}) collective-permute-start(f32[3,4,16,8,128]{4,3,2,1,0:T(8,128)} %pad_maximum_fusion), channel_id=1, source_target_pairs={{0,32},{32,0},{64,96},{96,64},{128,160},{160,128},{192,224},{224,1... | collective-permute-start | bytes 2359304 | tf_op jit(solution)/shard_map/ppermute | solution.py:326
  86.9 17.3 %collective-permute-start.5 = (f32[2,4,16,8,128]{4,3,2,1,0:T(8,128)}, f32[2,4,16,8,128]{4,3,2,1,0:T(8,128)}, u32[]{:S(2)}, u32[]{:S(2)}) collective-permute-start(f32[2,4,16,8,128]{4,3,2,1,0:T(8,128)} %pad_maximum_fusion.1), channel_id=1, source_target_pairs={{0,64},{32,96},{64,128},{96,160},{128,192},{160,224},{192,0},{224,... | collective-permute-start | bytes 1572872 | tf_op jit(solution)/shard_map/ppermute | solution.py:326
  88.1 16.7 %collective-permute-start.6 = (f32[2,4,16,8,128]{4,3,2,1,0:T(8,128)}, f32[2,4,16,8,128]{4,3,2,1,0:T(8,128)}, u32[]{:S(2)}, u32[]{:S(2)}) collective-permute-start(f32[2,4,16,8,128]{4,3,2,1,0:T(8,128)} %pad_maximum_fusion.1), channel_id=1, source_target_pairs={{0,128},{32,160},{64,192},{96,224},{128,0},{160,32},{192,64},{224,... | collective-permute-start | bytes 1572872 | tf_op jit(solution)/shard_map/ppermute | solution.py:326
  90.7 23.9 %collective-permute-start.7 = (f32[2,4,16,8,128]{4,3,2,1,0:T(8,128)}, f32[2,4,16,8,128]{4,3,2,1,0:T(8,128)}, u32[]{:S(2)}, u32[]{:S(2)}) collective-permute-start(f32[2,4,16,8,128]{4,3,2,1,0:T(8,128)} %pad_maximum_fusion.1), channel_id=1, source_target_pairs={{0,192},{32,224},{64,0},{96,32},{128,64},{160,96},{192,128},{224,1... | collective-permute-start | bytes 1572872 | tf_op jit(solution)/shard_map/ppermute | solution.py:326
  90.7 1.2 copy-start.2
  91.9 0.9 copy-start.4
  92.9 0.9 copy-start.6
  123.0 9.2 %collective-permute-start.12 = (f32[56,512]{1,0:T(8,128)S(1)}, f32[56,512]{1,0:T(8,128)S(1)}, u32[]{:S(2)}, u32[]{:S(2)}) collective-permute-start(f32[56,512]{1,0:T(8,128)S(1)} %get-tuple-element.29), channel_id=1, source_target_pairs={{0,1},{1,2},{2,3},{3,4},{4,5},{5,6},{6,7},{7,8},{8,9},{9,10},{10,1... | collective-permute-start | bytes 344072 | tf_op jit(solution)/shard_map/ppermute | solution.py:308
  124.9 10.2 %collective-permute-start.13 = (f32[56,512]{1,0:T(8,128)S(1)}, f32[56,512]{1,0:T(8,128)S(1)}, u32[]{:S(2)}, u32[]{:S(2)}) collective-permute-start(f32[56,512]{1,0:T(8,128)S(1)} %get-tuple-element.30), channel_id=1, source_target_pairs={{1,0},{2,1},{3,2},{4,3},{5,4},{6,5},{7,6},{8,7},{9,8},{10,9},{11,1... | collective-permute-start | bytes 344072 | tf_op jit(solution)/shard_map/ppermute | solution.py:308
  136.1 7.8 %collective-permute-start.18 = (f32[96,512]{1,0:T(8,128)}, f32[96,512]{1,0:T(8,128)}, u32[]{:S(2)}, u32[]{:S(2)}) collective-permute-start(f32[96,512]{1,0:T(8,128)} %late_kernel.1.refs_0_), channel_id=1, source_target_pairs={{0,32},{32,0},{64,96},{96,64},{128,160},{160,128},{192,224},{224,1... | collective-permute-start | bytes 589832 | tf_op jit(solution)/shard_map/ppermute | solution.py:326
  136.3 10.6 %collective-permute-start.19 = (f32[96,512]{1,0:T(8,128)}, f32[96,512]{1,0:T(8,128)}, u32[]{:S(2)}, u32[]{:S(2)}) collective-permute-start(f32[96,512]{1,0:T(8,128)} %late_kernel.1.refs_0_), channel_id=1, source_target_pairs={{0,64},{32,96},{64,0},{96,32},{128,192},{160,224},{192,128},{224,1... | collective-permute-start | bytes 589832 | tf_op jit(solution)/shard_map/ppermute | solution.py:326
  137.4 25.1 %collective-permute-start.20 = (f32[96,512]{1,0:T(8,128)}, f32[96,512]{1,0:T(8,128)}, u32[]{:S(2)}, u32[]{:S(2)}) collective-permute-start(f32[96,512]{1,0:T(8,128)} %late_kernel.1.refs_0_), channel_id=1, source_target_pairs={{0,192},{32,224},{64,128},{96,160},{128,64},{160,96},{192,0},{224,... | collective-permute-start | bytes 589832 | tf_op jit(solution)/shard_map/ppermute | solution.py:326
  139.4 31.4 %collective-permute-start.14 = (f32[96,512]{1,0:T(8,128)}, f32[96,512]{1,0:T(8,128)}, u32[]{:S(2)}, u32[]{:S(2)}) collective-permute-start(f32[96,512]{1,0:T(8,128)} %late_kernel.1.refs_0_), channel_id=1, source_target_pairs={{0,96},{32,64},{64,32},{96,0},{128,224},{160,192},{192,160},{224,1... | collective-permute-start | bytes 589832 | tf_op jit(solution)/shard_map/ppermute | solution.py:326
  141.5 29.4 %collective-permute-start.15 = (f32[96,512]{1,0:T(8,128)}, f32[96,512]{1,0:T(8,128)}, u32[]{:S(2)}, u32[]{:S(2)}) collective-permute-start(f32[96,512]{1,0:T(8,128)} %late_kernel.1.refs_0_), channel_id=1, source_target_pairs={{0,224},{32,192},{64,160},{96,128},{128,96},{160,64},{192,32},{224... | collective-permute-start | bytes 589832 | tf_op jit(solution)/shard_map/ppermute | solution.py:326
  143.9 27.0 %collective-permute-start.16 = (f32[96,512]{1,0:T(8,128)}, f32[96,512]{1,0:T(8,128)}, u32[]{:S(2)}, u32[]{:S(2)}) collective-permute-start(f32[96,512]{1,0:T(8,128)} %late_kernel.1.refs_0_), channel_id=1, source_target_pairs={{0,128},{32,160},{64,192},{96,224},{128,0},{160,32},{192,64},{224,... | collective-permute-start | bytes 589832 | tf_op jit(solution)/shard_map/ppermute | solution.py:326
  147.0 23.9 %collective-permute-start.17 = (f32[96,512]{1,0:T(8,128)}, f32[96,512]{1,0:T(8,128)}, u32[]{:S(2)}, u32[]{:S(2)}) collective-permute-start(f32[96,512]{1,0:T(8,128)} %late_kernel.1.refs_0_), channel_id=1, source_target_pairs={{0,160},{32,128},{64,224},{96,192},{128,32},{160,0},{192,96},{224,... | collective-permute-start | bytes 589832 | tf_op jit(solution)/shard_map/ppermute | solution.py:326

commit v3 on v2

--- a/solution.py
+++ b/solution.py
@@ -140,7 +140,7 @@
     return lax.rem(row - shift + rounds, rounds) * 2 + ((me - 2 * row) ^ flip)
 
 
-def gather_kernel(count, probes, rounds, plans, counts, started, me_ref, wells_ref, vel_ref, buf_ref, *refs):
+def gather_kernel(count, probes, rounds, plans, counts, started, ended, me_ref, wells_ref, vel_ref, buf_ref, *refs):
     n_in = len(plans)
     m_refs = refs[:n_in]
     refs = refs[n_in:]
@@ -193,7 +193,7 @@
             return carry
 
         lax.fori_loop(0, pieces, body, 0)
-    if started:
+    if ended:
         for send_ref, top in ((refs[3], False), (refs[4], True)):
             for p in range(probes):
                 z = p * count + (count - 8 if top else 0)
@@ -315,7 +315,7 @@
     n_wells = receiver_wells.shape[1]
     rows = probes * count
     me = lax.axis_index("shot").reshape(1).astype(jnp.int32)
-    params = pltpu.CompilerParams(vmem_limit_bytes=52 * 1024 * 1024)
+    params = pltpu.CompilerParams(vmem_limit_bytes=48 * 1024 * 1024)
     gather_params = pltpu.CompilerParams(vmem_limit_bytes=40 * 1024 * 1024)
     image_params = pltpu.CompilerParams(vmem_limit_bytes=67043328)
 
@@ -334,7 +334,8 @@
     b_ring = [sent(part_b, ring(s)) for s in range(1, rounds)]
     a_pair = jnp.stack([probe_panel[:, :, :8], swapped[:, :, :8]])
     a_ring = [sent(a_pair, ring(s)) for s in range(1, rounds)]
-    b_other = sent(jnp.stack(b_ring), swap)
+    b_stack = jnp.stack(b_ring)
+    b_other = sent(b_stack, swap)
 
     slab_id = lax.axis_index("space").reshape(1).astype(jnp.int32)
     plane = jax.ShapeDtypeStruct((count, width, width), F32)
@@ -364,14 +365,14 @@
     compact_v = jax.ShapeDtypeStruct((count, n_wells), F32)
     edge_rows = 12 * probes + 8
 
-    def gather(parts, plans, start=()):
+    def gather(parts, plans, start=(), ended=False):
         parts = [part.reshape(-1, rows * (16 if plan[0] is None else 8), width) for part, plan in zip(parts, plans)]
         counts = tuple(part.shape[0] for part in parts)
         out_shape = (compact, compact, compact_v)
-        if start:
+        if ended:
             out_shape += (jax.ShapeDtypeStruct((edge_rows, n_wells), F32),) * 2
         return pl.pallas_call(
-            functools.partial(gather_kernel, count, probes, rounds, plans, counts, bool(start)),
+            functools.partial(gather_kernel, count, probes, rounds, plans, counts, bool(start), ended),
             out_shape=out_shape,
             in_specs=[SMEM] + [VMEM] * (3 + len(parts) + len(start)),
             out_specs=(VMEM,) * len(out_shape),
@@ -385,8 +386,10 @@
 
     own_plans = ((None, 0, 0, 0, 0), (None, 0, 0, 1, 0)) + tuple((1, s, 0, 0, 0) for s in range(1, rounds))
     own = gather([probe_panel, swapped] + b_ring, own_plans)
-    far_plans = tuple((0, s, 0, 0, 1) for s in range(1, rounds)) + ((1, 1, 1, 1, 0),)
-    first, sigma, vel, send_low, send_high = gather(a_ring + [b_other], far_plans, own)
+    first_ring, rest = a_ring[0], a_ring[1:]
+    most = gather([first_ring, b_other], ((0, 1, 0, 0, 1), (1, 1, 1, 1, 0)), own)
+    last_plans = tuple((0, s, 0, 0, 1) for s in range(2, rounds))
+    first, sigma, vel, send_low, send_high = gather(rest, last_plans, most, True)
     low, high = spread(send_low, send_high)
     deep = count + 8
     late = pl.pallas_call(

time: 182 us -> 178 us (0.978)
  the two profiles are of different devices: /device:TPU:10 before, /device:TPU:22 now
where the time goes in v3:
time: 178 us
  starting transfers between devices  70.5 us (40%)
  waiting for transfers between devices  55.7 us (31%)
  Pallas kernels  45.3 us (25%)
  local copies, waits for them, and re-layouts  2.36 us (1%)
  between operations  2.08 us (1%)
  other arithmetic  1.79 us (1%)
    ppermute x15, waiting for transfers between devices, sent(): return lax.ppermute(value, 'shot', pairs)  42.6 us
    ppermute x15, starting transfers between devices, sent(): return lax.ppermute(value, 'shot', pairs)  38.4 us
    pallas_call x3, Pallas kernels, image(): pl.pallas_call(functools.partial(image_kernel, count, probes, flips, scal...  22.6 us
    ppermute x3, starting transfers between devices, spread(): lax.ppermute(low_layers, axis, backward)  21.2 us
    pallas_call x3, Pallas kernels, gather(): pl.pallas_call(functools.partial(gather_kernel, count, probes, rounds, pl...  16.2 us
    ppermute x3, waiting for transfers between devices, spread(): lax.ppermute(low_layers, axis, backward)  8.33 us
    ppermute x3, starting transfers between devices, spread(): lax.ppermute(high_layers, axis, forward)  5.97 us
    all_to_all x1, starting transfers between devices, slab(): shared = lax.all_to_all(buf, 'shot', 0, 0, tiled=True)  4.93 us
  transfers between devices with their start and end apart: 22, of which 12 were waited for; matrix products, arithmetic and copies ran while one was open for 1% of the time, Pallas kernels for 17%

profile of v3, /device:TPU:22, one launch (start us, length us, event | category | flops | bytes accessed | tf_op | source)
XLA Modules:
  0.0 177.8 jit_solution(15530247058967517331)
XLA Ops:
  0.0 1.1 slice_bitcast_fusion.2
  1.1 1.9 %collective-permute-start = (f32[4,128,128]{2,1,0:T(8,128)S(1)}, f32[4,128,128]{2,1,0:T(8,128)S(1)}, u32[]{:S(2)}, u32[]{:S(2)}) collective-permute-start(f32[4,128,128]{2,1,0:T(8,128)S(1)} %get-tuple-element.38), channel_id=1, source_target_pairs={{0,1},{1,2},{2,3},{3,4},{4,5},{5,6},{6,7},{7,8},{8,9},{9,10},{10,1... | collective-permute-start | bytes 786440 | tf_op jit(solution)/shard_map/ppermute | solution.py:308
  3.0 7.9 %collective-permute-start.1 = (f32[4,128,128]{2,1,0:T(8,128)S(1)}, f32[4,128,128]{2,1,0:T(8,128)S(1)}, u32[]{:S(2)}, u32[]{:S(2)}) collective-permute-start(f32[4,128,128]{2,1,0:T(8,128)S(1)} %get-tuple-element.37), channel_id=1, source_target_pairs={{1,0},{2,1},{3,2},{4,3},{5,4},{6,5},{7,6},{8,7},{9,8},{10,9},{11,1... | collective-permute-start | bytes 786440 | tf_op jit(solution)/shard_map/ppermute | solution.py:308
  12.9 0.8 collective-permute-done.low_ref
  13.6 4.0 %collective-permute-done.1.high_ref = f32[4,128,128]{2,1,0:T(8,128)S(1)} collective-permute-done((f32[4,128,128]{2,1,0:T(8,128)S(1)}, f32[4,128,128]{2,1,0:T(8,128)S(1)}, u32[]{:S(2)}, u32[]{:S(2)}) %collective-permute-start.1) | collective-permute-done | bytes 262176 | tf_op jit(solution)/shard_map/ppermute | solution.py:308
  17.6 1.2 copy-done.2
  18.8 2.9 %step_kernel.1 = (f32[16,128,128]{2,1,0:T(8,128)S(1)}, f32[16,128,128]{2,1,0:T(8,128)S(1)}, f32[16,128,128]{2,1,0:T(8,128)S(1)}, f32[4,128,128]{2,1,0:T(8,128)S(1)}, f32[4,128,128]{2,1,0:T(8,128)S(1)}) custom-call(s32[1]{0:T(128)} %bitcast.1.slab_ref, s32[1]{0:T(128)S(6)} %copy.9.depth_ref, s32[1]{0:T(128)S(6)} %copy.10.column_ref, f32[1]{0:T(128)S(6)} %copy.11.strength_ref, ...), custom_call_target="tpu_custom_call" | custom-call | tf_op jit(solution)/shard_map/step_kernel/pallas_call | solution.py:343
  21.8 2.1 %collective-permute-start.2 = (f32[4,128,128]{2,1,0:T(8,128)S(1)}, f32[4,128,128]{2,1,0:T(8,128)S(1)}, u32[]{:S(2)}, u32[]{:S(2)}) collective-permute-start(f32[4,128,128]{2,1,0:T(8,128)S(1)} %get-tuple-element.22), channel_id=1, source_target_pairs={{0,1},{1,2},{2,3},{3,4},{4,5},{5,6},{6,7},{7,8},{8,9},{9,10},{10,1... | collective-permute-start | bytes 786440 | tf_op jit(solution)/shard_map/ppermute | solution.py:308
  23.9 6.6 %collective-permute-start.3 = (f32[4,128,128]{2,1,0:T(8,128)S(1)}, f32[4,128,128]{2,1,0:T(8,128)S(1)}, u32[]{:S(2)}, u32[]{:S(2)}) collective-permute-start(f32[4,128,128]{2,1,0:T(8,128)S(1)} %get-tuple-element.23), channel_id=1, source_target_pairs={{1,0},{2,1},{3,2},{4,3},{5,4},{6,5},{7,6},{8,7},{9,8},{10,9},{11,1... | collective-permute-start | bytes 786440 | tf_op jit(solution)/shard_map/ppermute | solution.py:308
  30.5 3.4 %collective-permute-done.2.low_ref = f32[4,128,128]{2,1,0:T(8,128)S(1)} collective-permute-done((f32[4,128,128]{2,1,0:T(8,128)S(1)}, f32[4,128,128]{2,1,0:T(8,128)S(1)}, u32[]{:S(2)}, u32[]{:S(2)}) %collective-permute-start.2) | collective-permute-done | bytes 262176 | tf_op jit(solution)/shard_map/ppermute | solution.py:308
  33.9 1.8 %collective-permute-done.3.high_ref = f32[4,128,128]{2,1,0:T(8,128)S(1)} collective-permute-done((f32[4,128,128]{2,1,0:T(8,128)S(1)}, f32[4,128,128]{2,1,0:T(8,128)S(1)}, u32[]{:S(2)}, u32[]{:S(2)}) %collective-permute-start.3) | collective-permute-done | bytes 262176 | tf_op jit(solution)/shard_map/ppermute | solution.py:308
  35.7 2.6 %second_kernel.1.buf_ref = f32[8,520,128]{2,1,0:T(8,128)} custom-call(s32[1,512]{1,0:T(1,128)S(1)} %copy-done.3, f32[16,128,128]{2,1,0:T(8,128)S(1)} %get-tuple-element.21.next_ref, f32[4,128,128]{2,1,0:T(8,128)S(1)} %collective-permute-done.2.low_ref, f32[4,128,128]{2,1,0:T(8,128)S(1)} %collective-permute-done.3.high_ref, ...), custom_call_target="tpu_custom_call" | custom-call | tf_op jit(solution)/shard_map/second_kernel/pallas_call | solution.py:354
  38.3 4.9 %all-to-all-start = ((f32[8,520,128]{2,1,0:T(8,128)}), f32[8,520,128]{2,1,0:T(8,128)}, u32[]{:S(2)}, u32[]{:S(2)}) async-start(f32[8,520,128]{2,1,0:T(8,128)} %second_kernel.1.buf_ref), calls=%async_computation | async-start | bytes 4259840 | tf_op jit(solution)/shard_map/all_to_all | solution.py:362
  43.3 1.5 collective-permute-start.4
  44.9 1.2 collective-permute-start.8
  46.1 0.9 collective-permute-start.9
  47.0 1.2 collective-permute-start.10
  48.1 25.4 %collective-permute-done.8 = f32[4,16,8,128]{3,2,1,0:T(8,128)S(1)} collective-permute-done((f32[4,16,8,128]{3,2,1,0:T(8,128)S(1)}, f32[4,16,8,128]{3,2,1,0:T(8,128)S(1)}, u32[]{:S(2)}, u32[]{:S(2)}) %collective-permute-start.8) | collective-permute-done | bytes 262176 | tf_op jit(solution)/shard_map/ppermute | solution.py:326
  73.5 3.9 %collective-permute-done.9 = f32[4,16,8,128]{3,2,1,0:T(8,128)S(1)} collective-permute-done((f32[4,16,8,128]{3,2,1,0:T(8,128)S(1)}, f32[4,16,8,128]{3,2,1,0:T(8,128)S(1)}, u32[]{:S(2)}, u32[]{:S(2)}) %collective-permute-start.9) | collective-permute-done | bytes 262176 | tf_op jit(solution)/shard_map/ppermute | solution.py:326
  77.4 1.3 collective-permute-done.10
  78.7 1.0 pad_maximum_fusion
  79.7 2.9 %collective-permute-start.11 = (f32[3,4,16,8,128]{4,3,2,1,0:T(8,128)}, f32[3,4,16,8,128]{4,3,2,1,0:T(8,128)}, u32[]{:S(2)}, u32[]{:S(2)}) collective-permute-start(f32[3,4,16,8,128]{4,3,2,1,0:T(8,128)} %pad_maximum_fusion), channel_id=1, source_target_pairs={{0,32},{32,0},{64,96},{96,64},{128,160},{160,128},{192,224},{224,1... | collective-permute-start | bytes 2359304 | tf_op jit(solution)/shard_map/ppermute | solution.py:326
  82.6 0.0 collective-permute-done.4
  82.6 0.8 pad_maximum_fusion.1
  83.4 2.3 %collective-permute-start.5 = (f32[2,4,16,8,128]{4,3,2,1,0:T(8,128)}, f32[2,4,16,8,128]{4,3,2,1,0:T(8,128)S(1)}, u32[]{:S(2)}, u32[]{:S(2)}) collective-permute-start(f32[2,4,16,8,128]{4,3,2,1,0:T(8,128)} %pad_maximum_fusion.1), channel_id=1, source_target_pairs={{0,128},{32,160},{64,192},{96,224},{128,0},{160,32},{192,64},{224,... | collective-permute-start | bytes 1572872 | tf_op jit(solution)/shard_map/ppermute | solution.py:326
  85.7 1.4 collective-permute-start.6
  87.1 5.5 %shard_map.82 = (f32[64,512]{1,0:T(8,128)S(1)}, f32[64,512]{1,0:T(8,128)S(1)}, f32[16,512]{1,0:T(8,128)S(1)}) custom-call(s32[1]{0:T(128)} %bitcast.me_ref, s32[1,512]{1,0:T(1,128)S(1)} %copy-done.3, f32[2048,128]{1,0:T(8,128)S(1)} %bitcast.27, f32[8,520,128]{2,1,0:T(8,128)} %second_kernel.1.buf_ref, f32[1,1024,128]{2,1,0:T(8,128)S(1)} %bitcast.33, ...), custom_call_target="tpu_custom_call" | custom-call | tf_op jit(solution)/shard_map/pallas_call | solution.py:374
  92.6 8.1 %collective-permute-done.11 = f32[3,4,16,8,128]{4,3,2,1,0:T(8,128)} collective-permute-done((f32[3,4,16,8,128]{4,3,2,1,0:T(8,128)}, f32[3,4,16,8,128]{4,3,2,1,0:T(8,128)}, u32[]{:S(2)}, u32[]{:S(2)}) %collective-permute-start.11) | collective-permute-done | bytes 786464 | tf_op jit(solution)/shard_map/ppermute | solution.py:326
  100.8 5.8 %shard_map.83 = (f32[64,512]{1,0:T(8,128)S(1)}, f32[64,512]{1,0:T(8,128)S(1)}, f32[16,512]{1,0:T(8,128)S(1)}) custom-call(s32[1]{0:T(128)} %bitcast.me_ref, s32[1,512]{1,0:T(1,128)S(1)} %copy-done.3, f32[2048,128]{1,0:T(8,128)S(1)} %bitcast.28, f32[8,520,128]{2,1,0:T(8,128)} %second_kernel.1.buf_ref, f32[2,512,128]{2,1,0:T(8,128)} %bitcast.12.refs_0_, ...), custom_call_target="tpu_custom_call" | custom-call | tf_op jit(solution)/shard_map/pallas_call | solution.py:374
  106.6 2.3 %collective-permute-done.5 = f32[2,4,16,8,128]{4,3,2,1,0:T(8,128)S(1)} collective-permute-done((f32[2,4,16,8,128]{4,3,2,1,0:T(8,128)}, f32[2,4,16,8,128]{4,3,2,1,0:T(8,128)S(1)}, u32[]{:S(2)}, u32[]{:S(2)}) %collective-permute-start.5) | collective-permute-done | bytes 524320 | tf_op jit(solution)/shard_map/ppermute | solution.py:326
  109.0 1.5 collective-permute-done.6
  110.5 4.9 %shard_map.84 = (f32[64,512]{1,0:T(8,128)S(1)}, f32[64,512]{1,0:T(8,128)S(1)}, f32[16,512]{1,0:T(8,128)S(1)}, f32[56,512]{1,0:T(8,128)S(1)}, f32[56,512]{1,0:T(8,128)S(1)}) custom-call(s32[1]{0:T(128)} %bitcast.me_ref, s32[1,512]{1,0:T(1,128)S(1)} %copy-done.3, f32[2048,128]{1,0:T(8,128)S(1)} %bitcast.29, f32[8,520,128]{2,1,0:T(8,128)} %second_kernel.1.buf_ref, ...), custom_call_target="tpu_custom_call" | custom-call | tf_op jit(solution)/shard_map/pallas_call | solution.py:374
  115.4 1.9 %collective-permute-start.12 = (f32[56,512]{1,0:T(8,128)S(1)}, f32[56,512]{1,0:T(8,128)S(1)}, u32[]{:S(2)}, u32[]{:S(2)}) collective-permute-start(f32[56,512]{1,0:T(8,128)S(1)} %get-tuple-element.35), channel_id=1, source_target_pairs={{0,1},{1,2},{2,3},{3,4},{4,5},{5,6},{6,7},{7,8},{8,9},{9,10},{10,1... | collective-permute-start | bytes 344072 | tf_op jit(solution)/shard_map/ppermute | solution.py:308
  117.3 6.7 %collective-permute-start.13 = (f32[56,512]{1,0:T(8,128)S(1)}, f32[56,512]{1,0:T(8,128)S(1)}, u32[]{:S(2)}, u32[]{:S(2)}) collective-permute-start(f32[56,512]{1,0:T(8,128)S(1)} %get-tuple-element.36), channel_id=1, source_target_pairs={{1,0},{2,1},{3,2},{4,3},{5,4},{6,5},{7,6},{8,7},{9,8},{10,9},{11,1... | collective-permute-start | bytes 344072 | tf_op jit(solution)/shard_map/ppermute | solution.py:308
  123.9 0.6 collective-permute-done.12.low_ref
  124.6 2.5 %collective-permute-done.13.high_ref = f32[56,512]{1,0:T(8,128)S(1)} collective-permute-done((f32[56,512]{1,0:T(8,128)S(1)}, f32[56,512]{1,0:T(8,128)S(1)}, u32[]{:S(2)}, u32[]{:S(2)}) %collective-permute-start.13) | collective-permute-done | bytes 114720 | tf_op jit(solution)/shard_map/ppermute | solution.py:308
  127.1 0.9 late_kernel.1.refs_0_
  128.0 0.8 collective-permute-start.18
  128.8 4.5 %collective-permute-start.19 = (f32[96,512]{1,0:T(8,128)}, f32[96,512]{1,0:T(8,128)}, u32[]{:S(2)}, u32[]{:S(2)}) collective-permute-start(f32[96,512]{1,0:T(8,128)} %late_kernel.1.refs_0_), channel_id=1, source_target_pairs={{0,64},{32,96},{64,0},{96,32},{128,192},{160,224},{192,128},{224,1... | collective-permute-start | bytes 589832 | tf_op jit(solution)/shard_map/ppermute | solution.py:326
  133.3 3.1 %collective-permute-start.20 = (f32[96,512]{1,0:T(8,128)}, f32[96,512]{1,0:T(8,128)}, u32[]{:S(2)}, u32[]{:S(2)}) collective-permute-start(f32[96,512]{1,0:T(8,128)} %late_kernel.1.refs_0_), channel_id=1, source_target_pairs={{0,192},{32,224},{64,128},{96,160},{128,64},{160,96},{192,0},{224,... | collective-permute-start | bytes 589832 | tf_op jit(solution)/shard_map/ppermute | solution.py:326
  136.4 2.1 %collective-permute-start.14 = (f32[96,512]{1,0:T(8,128)}, f32[96,512]{1,0:T(8,128)}, u32[]{:S(2)}, u32[]{:S(2)}) collective-permute-start(f32[96,512]{1,0:T(8,128)} %late_kernel.1.refs_0_), channel_id=1, source_target_pairs={{0,96},{32,64},{64,32},{96,0},{128,224},{160,192},{192,160},{224,1... | collective-permute-start | bytes 589832 | tf_op jit(solution)/shard_map/ppermute | solution.py:326
  138.5 0.0 collective-permute-start.15
  138.5 0.0 collective-permute-done.18.refs_0_
  138.5 5.4 %collective-permute-start.16 = (f32[96,512]{1,0:T(8,128)}, f32[96,512]{1,0:T(8,128)}, u32[]{:S(2)}, u32[]{:S(2)}) collective-permute-start(f32[96,512]{1,0:T(8,128)} %late_kernel.1.refs_0_), channel_id=1, source_target_pairs={{0,128},{32,160},{64,192},{96,224},{128,0},{160,32},{192,64},{224,... | collective-permute-start | bytes 589832 | tf_op jit(solution)/shard_map/ppermute | solution.py:326
  143.9 11.2 %collective-permute-start.17 = (f32[96,512]{1,0:T(8,128)}, f32[96,512]{1,0:T(8,128)}, u32[]{:S(2)}, u32[]{:S(2)}) collective-permute-start(f32[96,512]{1,0:T(8,128)} %late_kernel.1.refs_0_), channel_id=1, source_target_pairs={{0,160},{32,128},{64,224},{96,192},{128,32},{160,0},{192,96},{224,... | collective-permute-start | bytes 589832 | tf_op jit(solution)/shard_map/ppermute | solution.py:326
  155.1 3.9 %shard_map.85.refs_3_ = f32[1024,128]{1,0:T(8,128)} custom-call(s32[1]{0:T(128)} %bitcast.me_ref, f32[8,520,128]{2,1,0:T(8,128)} %second_kernel.1.buf_ref, f32[1024,128]{1,0:T(8,128)} %bitcast.30, f32[96,512]{1,0:T(8,128)} %late_kernel.1.refs_0_), custom_call_target="tpu_custom_call" | custom-call | tf_op jit(solution)/shard_map/pallas_call | solution.py:423
  159.0 8.3 %shard_map.86.refs_4_ = f32[1024,128]{1,0:T(8,128)} custom-call(s32[1]{0:T(128)} %bitcast.me_ref, f32[8,520,128]{2,1,0:T(8,128)} %all-to-all-done.buf_ref, f32[1024,128]{1,0:T(8,128)} %bitcast.31, f32[96,512]{1,0:T(8,128)} %collective-permute-done.18.refs_0_, f32[96,512]{1,0:T(8,128)} %collective-permute-done.19.refs_1_, ...), custom_call_target="tpu_custom_call" | custom-call | tf_op jit(solution)/shard_map/pallas_call | solution.py:423
  167.3 10.4 %shard_map.87 = f32[1024,128]{1,0:T(8,128)} custom-call(s32[1]{0:T(128)} %bitcast.me_ref, f32[8,520,128]{2,1,0:T(8,128)} %all-to-all-done.buf_ref, f32[1024,128]{1,0:T(8,128)} %bitcast.32, f32[96,512]{1,0:T(8,128)} %collective-permute-done.14.refs_0_, f32[96,512]{1,0:T(8,128)} %collective-permute-done.15.refs_1_, f32[96,512]{1,0:T(8,128)} %collective-permute-done.16.refs_2_, ...), custom_call_target="tpu_custom_call" | custom-call | tf_op jit(solution)/shard_map/pallas_call | solution.py:423
  (18 shorter events, 0.1 us)
Async XLA Ops:
  0.0 35.7 %copy-start.3 = (s32[1,512]{1,0:T(1,128)S(1)}, s32[1,512]{1,0:T(1,128)}, u32[]{:S(2)}) copy-start(s32[1,512]{1,0:T(1,128)} %wells_ref.7) | copy-start | bytes 6148
  1.1 12.6 %collective-permute-start = (f32[4,128,128]{2,1,0:T(8,128)S(1)}, f32[4,128,128]{2,1,0:T(8,128)S(1)}, u32[]{:S(2)}, u32[]{:S(2)}) collective-permute-start(f32[4,128,128]{2,1,0:T(8,128)S(1)} %get-tuple-element.38), channel_id=1, source_target_pairs={{0,1},{1,2},{2,3},{3,4},{4,5},{5,6},{6,7},{7,8},{8,9},{9,10},{10,1... | collective-permute-start | bytes 786440 | tf_op jit(solution)/shard_map/ppermute | solution.py:308
  3.0 14.6 %collective-permute-start.1 = (f32[4,128,128]{2,1,0:T(8,128)S(1)}, f32[4,128,128]{2,1,0:T(8,128)S(1)}, u32[]{:S(2)}, u32[]{:S(2)}) collective-permute-start(f32[4,128,128]{2,1,0:T(8,128)S(1)} %get-tuple-element.37), channel_id=1, source_target_pairs={{1,0},{2,1},{3,2},{4,3},{5,4},{6,5},{7,6},{8,7},{9,8},{10,9},{11,1... | collective-permute-start | bytes 786440 | tf_op jit(solution)/shard_map/ppermute | solution.py:308
  17.6 1.2 copy-start.2
  21.8 12.1 %collective-permute-start.2 = (f32[4,128,128]{2,1,0:T(8,128)S(1)}, f32[4,128,128]{2,1,0:T(8,128)S(1)}, u32[]{:S(2)}, u32[]{:S(2)}) collective-permute-start(f32[4,128,128]{2,1,0:T(8,128)S(1)} %get-tuple-element.22), channel_id=1, source_target_pairs={{0,1},{1,2},{2,3},{3,4},{4,5},{5,6},{6,7},{7,8},{8,9},{9,10},{10,1... | collective-permute-start | bytes 786440 | tf_op jit(solution)/shard_map/ppermute | solution.py:308
  23.9 11.8 %collective-permute-start.3 = (f32[4,128,128]{2,1,0:T(8,128)S(1)}, f32[4,128,128]{2,1,0:T(8,128)S(1)}, u32[]{:S(2)}, u32[]{:S(2)}) collective-permute-start(f32[4,128,128]{2,1,0:T(8,128)S(1)} %get-tuple-element.23), channel_id=1, source_target_pairs={{1,0},{2,1},{3,2},{4,3},{5,4},{6,5},{7,6},{8,7},{9,8},{10,9},{11,1... | collective-permute-start | bytes 786440 | tf_op jit(solution)/shard_map/ppermute | solution.py:308
  38.3 4.9 %copy-start.1 = (f32[4,16,16,128]{3,2,1,0:T(8,128)S(1)}, f32[4,16,16,128]{3,2,1,0:T(8,128)}, u32[]{:S(2)}) copy-start(f32[4,16,16,128]{3,2,1,0:T(8,128)} %param.11) | copy-start | bytes 1572868
  38.3 120.7 %all-to-all-start = ((f32[8,520,128]{2,1,0:T(8,128)}), f32[8,520,128]{2,1,0:T(8,128)}, u32[]{:S(2)}, u32[]{:S(2)}) async-start(f32[8,520,128]{2,1,0:T(8,128)} %second_kernel.1.buf_ref), calls=%async_computation | async-start | bytes 4259840 | tf_op jit(solution)/shard_map/all_to_all | solution.py:362
  43.3 43.8 %copy-start = (f32[16,128,128]{2,1,0:T(8,128)S(1)}, f32[16,128,128]{2,1,0:T(8,128)}, u32[]{:S(2)}) copy-start(f32[16,128,128]{2,1,0:T(8,128)} %vel_ref.1) | copy-start | bytes 3145732
  43.3 39.3 %collective-permute-start.4 = (f32[4,16,16,128]{3,2,1,0:T(8,128)S(1)}, f32[4,16,16,128]{3,2,1,0:T(8,128)S(1)}, u32[]{:S(2)}, u32[]{:S(2)}) collective-permute-start(f32[4,16,16,128]{3,2,1,0:T(8,128)S(1)} %copy-done.1), channel_id=1, source_target_pairs={{0,32},{32,0},{64,96},{96,64},{128,160},{160,128},{192,224},{224,1... | collective-permute-start | bytes 1572872 | tf_op jit(solution)/shard_map/ppermute | solution.py:326
  44.9 28.7 %collective-permute-start.8 = (f32[4,16,8,128]{3,2,1,0:T(8,128)S(1)}, f32[4,16,8,128]{3,2,1,0:T(8,128)S(1)}, u32[]{:S(2)}, u32[]{:S(2)}) collective-permute-start(f32[4,16,8,128]{3,2,1,0:T(8,128)S(1)} %get-tuple-element.39), channel_id=1, source_target_pairs={{0,64},{32,96},{64,128},{96,160},{128,192},{160,224},{192,0},{224,... | collective-permute-start | bytes 786440 | tf_op jit(solution)/shard_map/ppermute | solution.py:326
  46.1 31.3 %collective-permute-start.9 = (f32[4,16,8,128]{3,2,1,0:T(8,128)S(1)}, f32[4,16,8,128]{3,2,1,0:T(8,128)S(1)}, u32[]{:S(2)}, u32[]{:S(2)}) collective-permute-start(f32[4,16,8,128]{3,2,1,0:T(8,128)S(1)} %get-tuple-element.39), channel_id=1, source_target_pairs={{0,128},{32,160},{64,192},{96,224},{128,0},{160,32},{192,64},{224,... | collective-permute-start | bytes 786440 | tf_op jit(solution)/shard_map/ppermute | solution.py:326
  47.0 31.8 %collective-permute-start.10 = (f32[4,16,8,128]{3,2,1,0:T(8,128)S(1)}, f32[4,16,8,128]{3,2,1,0:T(8,128)S(1)}, u32[]{:S(2)}, u32[]{:S(2)}) collective-permute-start(f32[4,16,8,128]{3,2,1,0:T(8,128)S(1)} %get-tuple-element.39), channel_id=1, source_target_pairs={{0,192},{32,224},{64,0},{96,32},{128,64},{160,96},{192,128},{224,1... | collective-permute-start | bytes 786440 | tf_op jit(solution)/shard_map/ppermute | solution.py:326
  79.7 21.1 %collective-permute-start.11 = (f32[3,4,16,8,128]{4,3,2,1,0:T(8,128)}, f32[3,4,16,8,128]{4,3,2,1,0:T(8,128)}, u32[]{:S(2)}, u32[]{:S(2)}) collective-permute-start(f32[3,4,16,8,128]{4,3,2,1,0:T(8,128)} %pad_maximum_fusion), channel_id=1, source_target_pairs={{0,32},{32,0},{64,96},{96,64},{128,160},{160,128},{192,224},{224,1... | collective-permute-start | bytes 2359304 | tf_op jit(solution)/shard_map/ppermute | solution.py:326
  83.4 17.4 %collective-permute-start.7 = (f32[2,4,16,8,128]{4,3,2,1,0:T(8,128)}, f32[2,4,16,8,128]{4,3,2,1,0:T(8,128)}, u32[]{:S(2)}, u32[]{:S(2)}) collective-permute-start(f32[2,4,16,8,128]{4,3,2,1,0:T(8,128)} %pad_maximum_fusion.1), channel_id=1, source_target_pairs={{0,64},{32,96},{64,128},{96,160},{128,192},{160,224},{192,0},{224,... | collective-permute-start | bytes 1572872 | tf_op jit(solution)/shard_map/ppermute | solution.py:326
  83.4 25.5 %collective-permute-start.5 = (f32[2,4,16,8,128]{4,3,2,1,0:T(8,128)}, f32[2,4,16,8,128]{4,3,2,1,0:T(8,128)S(1)}, u32[]{:S(2)}, u32[]{:S(2)}) collective-permute-start(f32[2,4,16,8,128]{4,3,2,1,0:T(8,128)} %pad_maximum_fusion.1), channel_id=1, source_target_pairs={{0,128},{32,160},{64,192},{96,224},{128,0},{160,32},{192,64},{224,... | collective-permute-start | bytes 1572872 | tf_op jit(solution)/shard_map/ppermute | solution.py:326
  85.7 24.7 %collective-permute-start.6 = (f32[2,4,16,8,128]{4,3,2,1,0:T(8,128)}, f32[2,4,16,8,128]{4,3,2,1,0:T(8,128)}, u32[]{:S(2)}, u32[]{:S(2)}) collective-permute-start(f32[2,4,16,8,128]{4,3,2,1,0:T(8,128)} %pad_maximum_fusion.1), channel_id=1, source_target_pairs={{0,192},{32,224},{64,0},{96,32},{128,64},{160,96},{192,128},{224,1... | collective-permute-start | bytes 1572872 | tf_op jit(solution)/shard_map/ppermute | solution.py:326
  115.4 9.2 %collective-permute-start.12 = (f32[56,512]{1,0:T(8,128)S(1)}, f32[56,512]{1,0:T(8,128)S(1)}, u32[]{:S(2)}, u32[]{:S(2)}) collective-permute-start(f32[56,512]{1,0:T(8,128)S(1)} %get-tuple-element.35), channel_id=1, source_target_pairs={{0,1},{1,2},{2,3},{3,4},{4,5},{5,6},{6,7},{7,8},{8,9},{9,10},{10,1... | collective-permute-start | bytes 344072 | tf_op jit(solution)/shard_map/ppermute | solution.py:308
  117.3 9.8 %collective-permute-start.13 = (f32[56,512]{1,0:T(8,128)S(1)}, f32[56,512]{1,0:T(8,128)S(1)}, u32[]{:S(2)}, u32[]{:S(2)}) collective-permute-start(f32[56,512]{1,0:T(8,128)S(1)} %get-tuple-element.36), channel_id=1, source_target_pairs={{1,0},{2,1},{3,2},{4,3},{5,4},{6,5},{7,6},{8,7},{9,8},{10,9},{11,1... | collective-permute-start | bytes 344072 | tf_op jit(solution)/shard_map/ppermute | solution.py:308
  128.0 10.5 %collective-permute-start.18 = (f32[96,512]{1,0:T(8,128)}, f32[96,512]{1,0:T(8,128)}, u32[]{:S(2)}, u32[]{:S(2)}) collective-permute-start(f32[96,512]{1,0:T(8,128)} %late_kernel.1.refs_0_), channel_id=1, source_target_pairs={{0,32},{32,0},{64,96},{96,64},{128,160},{160,128},{192,224},{224,1... | collective-permute-start | bytes 589832 | tf_op jit(solution)/shard_map/ppermute | solution.py:326
  128.8 15.1 %collective-permute-start.19 = (f32[96,512]{1,0:T(8,128)}, f32[96,512]{1,0:T(8,128)}, u32[]{:S(2)}, u32[]{:S(2)}) collective-permute-start(f32[96,512]{1,0:T(8,128)} %late_kernel.1.refs_0_), channel_id=1, source_target_pairs={{0,64},{32,96},{64,0},{96,32},{128,192},{160,224},{192,128},{224,1... | collective-permute-start | bytes 589832 | tf_op jit(solution)/shard_map/ppermute | solution.py:326
  133.3 25.7 %collective-permute-start.20 = (f32[96,512]{1,0:T(8,128)}, f32[96,512]{1,0:T(8,128)}, u32[]{:S(2)}, u32[]{:S(2)}) collective-permute-start(f32[96,512]{1,0:T(8,128)} %late_kernel.1.refs_0_), channel_id=1, source_target_pairs={{0,192},{32,224},{64,128},{96,160},{128,64},{160,96},{192,0},{224,... | collective-permute-start | bytes 589832 | tf_op jit(solution)/shard_map/ppermute | solution.py:326
  136.4 30.9 %collective-permute-start.14 = (f32[96,512]{1,0:T(8,128)}, f32[96,512]{1,0:T(8,128)}, u32[]{:S(2)}, u32[]{:S(2)}) collective-permute-start(f32[96,512]{1,0:T(8,128)} %late_kernel.1.refs_0_), channel_id=1, source_target_pairs={{0,96},{32,64},{64,32},{96,0},{128,224},{160,192},{192,160},{224,1... | collective-permute-start | bytes 589832 | tf_op jit(solution)/shard_map/ppermute | solution.py:326
  138.5 28.8 %collective-permute-start.15 = (f32[96,512]{1,0:T(8,128)}, f32[96,512]{1,0:T(8,128)}, u32[]{:S(2)}, u32[]{:S(2)}) collective-permute-start(f32[96,512]{1,0:T(8,128)} %late_kernel.1.refs_0_), channel_id=1, source_target_pairs={{0,224},{32,192},{64,160},{96,128},{128,96},{160,64},{192,32},{224... | collective-permute-start | bytes 589832 | tf_op jit(solution)/shard_map/ppermute | solution.py:326
  138.5 28.8 %collective-permute-start.16 = (f32[96,512]{1,0:T(8,128)}, f32[96,512]{1,0:T(8,128)}, u32[]{:S(2)}, u32[]{:S(2)}) collective-permute-start(f32[96,512]{1,0:T(8,128)} %late_kernel.1.refs_0_), channel_id=1, source_target_pairs={{0,128},{32,160},{64,192},{96,224},{128,0},{160,32},{192,64},{224,... | collective-permute-start | bytes 589832 | tf_op jit(solution)/shard_map/ppermute | solution.py:326
  143.9 23.4 %collective-permute-start.17 = (f32[96,512]{1,0:T(8,128)}, f32[96,512]{1,0:T(8,128)}, u32[]{:S(2)}, u32[]{:S(2)}) collective-permute-start(f32[96,512]{1,0:T(8,128)} %late_kernel.1.refs_0_), channel_id=1, source_target_pairs={{0,160},{32,128},{64,224},{96,192},{128,32},{160,0},{192,96},{224,... | collective-permute-start | bytes 589832 | tf_op jit(solution)/shard_map/ppermute | solution.py:326

commit v4 on v3

--- a/solution.py
+++ b/solution.py
@@ -315,8 +315,8 @@
     n_wells = receiver_wells.shape[1]
     rows = probes * count
     me = lax.axis_index("shot").reshape(1).astype(jnp.int32)
-    params = pltpu.CompilerParams(vmem_limit_bytes=48 * 1024 * 1024)
-    gather_params = pltpu.CompilerParams(vmem_limit_bytes=40 * 1024 * 1024)
+    params = pltpu.CompilerParams(vmem_limit_bytes=49 * 1024 * 1024)
+    gather_params = pltpu.CompilerParams(vmem_limit_bytes=30 * 1024 * 1024)
     image_params = pltpu.CompilerParams(vmem_limit_bytes=67043328)
 
     rounds = strips // 2
@@ -448,7 +448,7 @@
 
 
 NEAR = (1, 2, 6)
-FAR = (3, 7, 4, 5)
+FAR = (4, 5, 3, 7)
 
 
 def solution(mesh):

time: 178 us -> 175 us (0.983)
  the two profiles are of different devices: /device:TPU:22 before, /device:TPU:30 now
where the time goes in v4:
time: 175 us
  starting transfers between devices  62.6 us (36%)
  waiting for transfers between devices  58.5 us (33%)
  Pallas kernels  42.6 us (24%)
  local copies, waits for them, and re-layouts  7.01 us (4%)
  between operations  2.12 us (1%)
  other arithmetic  1.87 us (1%)
    ppermute x15, waiting for transfers between devices, sent(): return lax.ppermute(value, 'shot', pairs)  45 us
    ppermute x15, starting transfers between devices, sent(): return lax.ppermute(value, 'shot', pairs)  30.7 us
    pallas_call x3, Pallas kernels, image(): pl.pallas_call(functools.partial(image_kernel, count, probes, flips, scal...  22.6 us
    ppermute x3, starting transfers between devices, spread(): lax.ppermute(low_layers, axis, backward)  21.1 us
    pallas_call x3, Pallas kernels, gather(): pl.pallas_call(functools.partial(gather_kernel, count, probes, rounds, pl...  13.5 us
    ppermute x3, waiting for transfers between devices, spread(): lax.ppermute(low_layers, axis, backward)  8.73 us
    ppermute x3, starting transfers between devices, spread(): lax.ppermute(high_layers, axis, forward)  6.06 us
    unnamed x20, local copies, waits for them, and re-layouts  4.85 us
  transfers between devices with their start and end apart: 22, of which 11 were waited for; matrix products, arithmetic and copies ran while one was open for 2% of the time, Pallas kernels for 15%

profile of v4, /device:TPU:30, one launch (start us, length us, event | category | flops | bytes accessed | tf_op | source)
XLA Modules:
  0.0 174.7 jit_solution(2470167636985962032)
XLA Ops:
  0.0 1.1 slice_bitcast_fusion.2
  1.1 1.9 %collective-permute-start = (f32[4,128,128]{2,1,0:T(8,128)S(1)}, f32[4,128,128]{2,1,0:T(8,128)S(1)}, u32[]{:S(2)}, u32[]{:S(2)}) collective-permute-start(f32[4,128,128]{2,1,0:T(8,128)S(1)} %get-tuple-element.38), channel_id=1, source_target_pairs={{0,1},{1,2},{2,3},{3,4},{4,5},{5,6},{6,7},{7,8},{8,9},{9,10},{10,1... | collective-permute-start | bytes 786440 | tf_op jit(solution)/shard_map/ppermute | solution.py:308
  3.0 7.9 %collective-permute-start.1 = (f32[4,128,128]{2,1,0:T(8,128)S(1)}, f32[4,128,128]{2,1,0:T(8,128)S(1)}, u32[]{:S(2)}, u32[]{:S(2)}) collective-permute-start(f32[4,128,128]{2,1,0:T(8,128)S(1)} %get-tuple-element.37), channel_id=1, source_target_pairs={{1,0},{2,1},{3,2},{4,3},{5,4},{6,5},{7,6},{8,7},{9,8},{10,9},{11,1... | collective-permute-start | bytes 786440 | tf_op jit(solution)/shard_map/ppermute | solution.py:308
  12.9 0.8 collective-permute-done.low_ref
  13.6 4.0 %collective-permute-done.1.high_ref = f32[4,128,128]{2,1,0:T(8,128)S(1)} collective-permute-done((f32[4,128,128]{2,1,0:T(8,128)S(1)}, f32[4,128,128]{2,1,0:T(8,128)S(1)}, u32[]{:S(2)}, u32[]{:S(2)}) %collective-permute-start.1) | collective-permute-done | bytes 262176 | tf_op jit(solution)/shard_map/ppermute | solution.py:308
  17.6 3.0 %step_kernel.1 = (f32[16,128,128]{2,1,0:T(8,128)S(1)}, f32[16,128,128]{2,1,0:T(8,128)S(1)}, f32[16,128,128]{2,1,0:T(8,128)S(1)}, f32[4,128,128]{2,1,0:T(8,128)S(1)}, f32[4,128,128]{2,1,0:T(8,128)S(1)}) custom-call(s32[1]{0:T(128)} %bitcast.1.slab_ref, s32[1]{0:T(128)S(6)} %copy.9.depth_ref, s32[1]{0:T(128)S(6)} %copy.10.column_ref, f32[1]{0:T(128)S(6)} %copy.11.strength_ref, ...), custom_call_target="tpu_custom_call" | custom-call | tf_op jit(solution)/shard_map/step_kernel/pallas_call | solution.py:343
  20.6 2.1 %collective-permute-start.2 = (f32[4,128,128]{2,1,0:T(8,128)S(1)}, f32[4,128,128]{2,1,0:T(8,128)S(1)}, u32[]{:S(2)}, u32[]{:S(2)}) collective-permute-start(f32[4,128,128]{2,1,0:T(8,128)S(1)} %get-tuple-element.22), channel_id=1, source_target_pairs={{0,1},{1,2},{2,3},{3,4},{4,5},{5,6},{6,7},{7,8},{8,9},{9,10},{10,1... | collective-permute-start | bytes 786440 | tf_op jit(solution)/shard_map/ppermute | solution.py:308
  22.8 6.6 %collective-permute-start.3 = (f32[4,128,128]{2,1,0:T(8,128)S(1)}, f32[4,128,128]{2,1,0:T(8,128)S(1)}, u32[]{:S(2)}, u32[]{:S(2)}) collective-permute-start(f32[4,128,128]{2,1,0:T(8,128)S(1)} %get-tuple-element.23), channel_id=1, source_target_pairs={{1,0},{2,1},{3,2},{4,3},{5,4},{6,5},{7,6},{8,7},{9,8},{10,9},{11,1... | collective-permute-start | bytes 786440 | tf_op jit(solution)/shard_map/ppermute | solution.py:308
  29.4 3.4 %collective-permute-done.2.low_ref = f32[4,128,128]{2,1,0:T(8,128)S(1)} collective-permute-done((f32[4,128,128]{2,1,0:T(8,128)S(1)}, f32[4,128,128]{2,1,0:T(8,128)S(1)}, u32[]{:S(2)}, u32[]{:S(2)}) %collective-permute-start.2) | collective-permute-done | bytes 262176 | tf_op jit(solution)/shard_map/ppermute | solution.py:308
  32.8 1.8 %collective-permute-done.3.high_ref = f32[4,128,128]{2,1,0:T(8,128)S(1)} collective-permute-done((f32[4,128,128]{2,1,0:T(8,128)S(1)}, f32[4,128,128]{2,1,0:T(8,128)S(1)}, u32[]{:S(2)}, u32[]{:S(2)}) %collective-permute-start.3) | collective-permute-done | bytes 262176 | tf_op jit(solution)/shard_map/ppermute | solution.py:308
  34.6 2.5 %second_kernel.1.buf_ref = f32[8,520,128]{2,1,0:T(8,128)} custom-call(s32[1,512]{1,0:T(1,128)S(1)} %copy-done.9, f32[16,128,128]{2,1,0:T(8,128)S(1)} %get-tuple-element.21.next_ref, f32[4,128,128]{2,1,0:T(8,128)S(1)} %collective-permute-done.2.low_ref, f32[4,128,128]{2,1,0:T(8,128)S(1)} %collective-permute-done.3.high_ref, ...), custom_call_target="tpu_custom_call" | custom-call | tf_op jit(solution)/shard_map/second_kernel/pallas_call | solution.py:354
  37.1 4.7 %all-to-all-start = ((f32[8,520,128]{2,1,0:T(8,128)}), f32[8,520,128]{2,1,0:T(8,128)}, u32[]{:S(2)}, u32[]{:S(2)}) async-start(f32[8,520,128]{2,1,0:T(8,128)} %second_kernel.1.buf_ref), calls=%async_computation | async-start | bytes 4259840 | tf_op jit(solution)/shard_map/all_to_all | solution.py:362
  41.8 1.5 collective-permute-start.4
  43.3 1.1 fusion
  44.4 0.6 collective-permute-start.8
  45.0 2.4 %collective-permute-start.9 = (f32[4,16,8,128]{3,2,1,0:T(8,128)S(1)}, f32[4,16,8,128]{3,2,1,0:T(8,128)S(1)}, u32[]{:S(2)}, u32[]{:S(2)}) collective-permute-start(f32[4,16,8,128]{3,2,1,0:T(8,128)S(1)} %get-tuple-element.39), channel_id=1, source_target_pairs={{0,128},{32,160},{64,192},{96,224},{128,0},{160,32},{192,64},{224,... | collective-permute-start | bytes 786440 | tf_op jit(solution)/shard_map/ppermute | solution.py:326
  47.4 24.1 %collective-permute-done.8 = f32[4,16,8,128]{3,2,1,0:T(8,128)S(1)} collective-permute-done((f32[4,16,8,128]{3,2,1,0:T(8,128)S(1)}, f32[4,16,8,128]{3,2,1,0:T(8,128)S(1)}, u32[]{:S(2)}, u32[]{:S(2)}) %collective-permute-start.8) | collective-permute-done | bytes 262176 | tf_op jit(solution)/shard_map/ppermute | solution.py:326
  71.5 0.6 collective-permute-done.9
  72.1 6.4 %collective-permute-done.10 = f32[4,16,8,128]{3,2,1,0:T(8,128)S(1)} collective-permute-done((f32[4,16,8,128]{3,2,1,0:T(8,128)S(1)}, f32[4,16,8,128]{3,2,1,0:T(8,128)S(1)}, u32[]{:S(2)}, u32[]{:S(2)}) %collective-permute-start.10) | collective-permute-done | bytes 262176 | tf_op jit(solution)/shard_map/ppermute | solution.py:326
  78.5 1.0 pad_maximum_fusion
  79.5 0.5 collective-permute-start.11
  80.1 0.8 copy-done.3
  80.9 0.8 pad_maximum_fusion.1
  81.8 2.3 %collective-permute-start.7 = (f32[2,4,16,8,128]{4,3,2,1,0:T(8,128)}, f32[2,4,16,8,128]{4,3,2,1,0:T(8,128)}, u32[]{:S(2)}, u32[]{:S(2)}) collective-permute-start(f32[2,4,16,8,128]{4,3,2,1,0:T(8,128)} %pad_maximum_fusion.1), channel_id=1, source_target_pairs={{0,64},{32,96},{64,128},{96,160},{128,192},{160,224},{192,0},{224,... | collective-permute-start | bytes 1572872 | tf_op jit(solution)/shard_map/ppermute | solution.py:326
  84.0 1.8 %collective-permute-start.5 = (f32[2,4,16,8,128]{4,3,2,1,0:T(8,128)}, f32[2,4,16,8,128]{4,3,2,1,0:T(8,128)}, u32[]{:S(2)}, u32[]{:S(2)}) collective-permute-start(f32[2,4,16,8,128]{4,3,2,1,0:T(8,128)} %pad_maximum_fusion.1), channel_id=1, source_target_pairs={{0,128},{32,160},{64,192},{96,224},{128,0},{160,32},{192,64},{224,... | collective-permute-start | bytes 1572872 | tf_op jit(solution)/shard_map/ppermute | solution.py:326
  85.9 0.3 collective-permute-start.6
  86.1 1.0 copy-done.2
  87.2 1.0 copy-done.4
  88.2 0.9 copy-done.6
  89.2 0.9 copy-done.8
  90.1 3.9 %shard_map.82 = (f32[64,512]{1,0:T(8,128)S(1)}, f32[64,512]{1,0:T(8,128)S(1)}, f32[16,512]{1,0:T(8,128)S(1)}) custom-call(s32[1]{0:T(128)} %bitcast.me_ref, s32[1,512]{1,0:T(1,128)S(1)} %copy-done.9, f32[2048,128]{1,0:T(8,128)S(1)} %bitcast.27, f32[8,520,128]{2,1,0:T(8,128)S(1)} %copy-done, f32[1,1024,128]{2,1,0:T(8,128)S(1)} %bitcast.33, ...), custom_call_target="tpu_custom_call" | custom-call | tf_op jit(solution)/shard_map/pallas_call | solution.py:374
  94.0 5.4 %collective-permute-done.11 = f32[3,4,16,8,128]{4,3,2,1,0:T(8,128)} collective-permute-done((f32[3,4,16,8,128]{4,3,2,1,0:T(8,128)}, f32[3,4,16,8,128]{4,3,2,1,0:T(8,128)}, u32[]{:S(2)}, u32[]{:S(2)}) %collective-permute-start.11) | collective-permute-done | bytes 786464 | tf_op jit(solution)/shard_map/ppermute | solution.py:326
  99.4 8.5 %collective-permute-done.7 = f32[2,4,16,8,128]{4,3,2,1,0:T(8,128)} collective-permute-done((f32[2,4,16,8,128]{4,3,2,1,0:T(8,128)}, f32[2,4,16,8,128]{4,3,2,1,0:T(8,128)}, u32[]{:S(2)}, u32[]{:S(2)}) %collective-permute-start.7) | collective-permute-done | bytes 524320 | tf_op jit(solution)/shard_map/ppermute | solution.py:326
  107.9 5.2 %shard_map.83 = (f32[64,512]{1,0:T(8,128)S(1)}, f32[64,512]{1,0:T(8,128)S(1)}, f32[16,512]{1,0:T(8,128)S(1)}) custom-call(s32[1]{0:T(128)} %bitcast.me_ref, s32[1,512]{1,0:T(1,128)S(1)} %copy-done.9, f32[2048,128]{1,0:T(8,128)S(1)} %bitcast.28, f32[8,520,128]{2,1,0:T(8,128)S(1)} %copy-done, f32[2,512,128]{2,1,0:T(8,128)} %bitcast.12.refs_0_, ...), custom_call_target="tpu_custom_call" | custom-call | tf_op jit(solution)/shard_map/pallas_call | solution.py:374
  113.1 4.4 %shard_map.84 = (f32[64,512]{1,0:T(8,128)S(1)}, f32[64,512]{1,0:T(8,128)S(1)}, f32[16,512]{1,0:T(8,128)S(1)}, f32[56,512]{1,0:T(8,128)S(1)}, f32[56,512]{1,0:T(8,128)S(1)}) custom-call(s32[1]{0:T(128)} %bitcast.me_ref, s32[1,512]{1,0:T(1,128)S(1)} %copy-done.9, f32[2048,128]{1,0:T(8,128)S(1)} %bitcast.29, f32[8,520,128]{2,1,0:T(8,128)S(1)} %copy-done, ...), custom_call_target="tpu_custom_call" | custom-call | tf_op jit(solution)/shard_map/pallas_call | solution.py:374
  117.5 2.0 %collective-permute-start.12 = (f32[56,512]{1,0:T(8,128)S(1)}, f32[56,512]{1,0:T(8,128)S(1)}, u32[]{:S(2)}, u32[]{:S(2)}) collective-permute-start(f32[56,512]{1,0:T(8,128)S(1)} %get-tuple-element.35), channel_id=1, source_target_pairs={{0,1},{1,2},{2,3},{3,4},{4,5},{5,6},{6,7},{7,8},{8,9},{9,10},{10,1... | collective-permute-start | bytes 344072 | tf_op jit(solution)/shard_map/ppermute | solution.py:308
  119.5 6.6 %collective-permute-start.13 = (f32[56,512]{1,0:T(8,128)S(1)}, f32[56,512]{1,0:T(8,128)S(1)}, u32[]{:S(2)}, u32[]{:S(2)}) collective-permute-start(f32[56,512]{1,0:T(8,128)S(1)} %get-tuple-element.36), channel_id=1, source_target_pairs={{1,0},{2,1},{3,2},{4,3},{5,4},{6,5},{7,6},{8,7},{9,8},{10,9},{11,1... | collective-permute-start | bytes 344072 | tf_op jit(solution)/shard_map/ppermute | solution.py:308
  126.1 0.6 collective-permute-done.12.low_ref
  126.7 2.9 %collective-permute-done.13.high_ref = f32[56,512]{1,0:T(8,128)S(1)} collective-permute-done((f32[56,512]{1,0:T(8,128)S(1)}, f32[56,512]{1,0:T(8,128)S(1)}, u32[]{:S(2)}, u32[]{:S(2)}) %collective-permute-start.13) | collective-permute-done | bytes 114720 | tf_op jit(solution)/shard_map/ppermute | solution.py:308
  129.7 1.0 late_kernel.1.refs_0_
  130.6 3.7 %collective-permute-start.20 = (f32[96,512]{1,0:T(8,128)}, f32[96,512]{1,0:T(8,128)}, u32[]{:S(2)}, u32[]{:S(2)}) collective-permute-start(f32[96,512]{1,0:T(8,128)} %late_kernel.1.refs_0_), channel_id=1, source_target_pairs={{0,192},{32,224},{64,128},{96,160},{128,64},{160,96},{192,0},{224,... | collective-permute-start | bytes 589832 | tf_op jit(solution)/shard_map/ppermute | solution.py:326
  134.3 1.5 collective-permute-start.14
  135.8 3.5 %collective-permute-start.15 = (f32[96,512]{1,0:T(8,128)}, f32[96,512]{1,0:T(8,128)}, u32[]{:S(2)}, u32[]{:S(2)}) collective-permute-start(f32[96,512]{1,0:T(8,128)} %late_kernel.1.refs_0_), channel_id=1, source_target_pairs={{0,160},{32,128},{64,224},{96,192},{128,32},{160,0},{192,96},{224,... | collective-permute-start | bytes 589832 | tf_op jit(solution)/shard_map/ppermute | solution.py:326
  139.3 0.9 collective-permute-start.16
  140.2 11.9 %collective-permute-start.17 = (f32[96,512]{1,0:T(8,128)}, f32[96,512]{1,0:T(8,128)}, u32[]{:S(2)}, u32[]{:S(2)}) collective-permute-start(f32[96,512]{1,0:T(8,128)} %late_kernel.1.refs_0_), channel_id=1, source_target_pairs={{0,224},{32,192},{64,160},{96,128},{128,96},{160,64},{192,32},{224... | collective-permute-start | bytes 589832 | tf_op jit(solution)/shard_map/ppermute | solution.py:326
  152.0 3.9 %shard_map.85.refs_3_ = f32[1024,128]{1,0:T(8,128)} custom-call(s32[1]{0:T(128)} %bitcast.me_ref, f32[8,520,128]{2,1,0:T(8,128)} %second_kernel.1.buf_ref, f32[1024,128]{1,0:T(8,128)} %bitcast.30, f32[96,512]{1,0:T(8,128)} %late_kernel.1.refs_0_), custom_call_target="tpu_custom_call" | custom-call | tf_op jit(solution)/shard_map/pallas_call | solution.py:423
  156.0 8.3 %shard_map.86.refs_4_ = f32[1024,128]{1,0:T(8,128)} custom-call(s32[1]{0:T(128)} %bitcast.me_ref, f32[8,520,128]{2,1,0:T(8,128)} %all-to-all-done.buf_ref, f32[1024,128]{1,0:T(8,128)} %bitcast.31, f32[96,512]{1,0:T(8,128)} %collective-permute-done.18.refs_0_, f32[96,512]{1,0:T(8,128)} %collective-permute-done.19.refs_1_, ...), custom_call_target="tpu_custom_call" | custom-call | tf_op jit(solution)/shard_map/pallas_call | solution.py:423
  164.3 10.4 %shard_map.87 = f32[1024,128]{1,0:T(8,128)} custom-call(s32[1]{0:T(128)} %bitcast.me_ref, f32[8,520,128]{2,1,0:T(8,128)} %all-to-all-done.buf_ref, f32[1024,128]{1,0:T(8,128)} %bitcast.32, f32[96,512]{1,0:T(8,128)} %collective-permute-done.14.refs_0_, f32[96,512]{1,0:T(8,128)} %collective-permute-done.15.refs_1_, f32[96,512]{1,0:T(8,128)} %collective-permute-done.16.refs_2_, ...), custom_call_target="tpu_custom_call" | custom-call | tf_op jit(solution)/shard_map/pallas_call | solution.py:423
  (30 shorter events, 0.1 us)
Async XLA Ops:
  0.0 34.6 %copy-start.9 = (s32[1,512]{1,0:T(1,128)S(1)}, s32[1,512]{1,0:T(1,128)}, u32[]{:S(2)}) copy-start(s32[1,512]{1,0:T(1,128)} %wells_ref.7) | copy-start | bytes 6148
  1.1 12.6 %collective-permute-start = (f32[4,128,128]{2,1,0:T(8,128)S(1)}, f32[4,128,128]{2,1,0:T(8,128)S(1)}, u32[]{:S(2)}, u32[]{:S(2)}) collective-permute-start(f32[4,128,128]{2,1,0:T(8,128)S(1)} %get-tuple-element.38), channel_id=1, source_target_pairs={{0,1},{1,2},{2,3},{3,4},{4,5},{5,6},{6,7},{7,8},{8,9},{9,10},{10,1... | collective-permute-start | bytes 786440 | tf_op jit(solution)/shard_map/ppermute | solution.py:308
  3.0 14.6 %collective-permute-start.1 = (f32[4,128,128]{2,1,0:T(8,128)S(1)}, f32[4,128,128]{2,1,0:T(8,128)S(1)}, u32[]{:S(2)}, u32[]{:S(2)}) collective-permute-start(f32[4,128,128]{2,1,0:T(8,128)S(1)} %get-tuple-element.37), channel_id=1, source_target_pairs={{1,0},{2,1},{3,2},{4,3},{5,4},{6,5},{7,6},{8,7},{9,8},{10,9},{11,1... | collective-permute-start | bytes 786440 | tf_op jit(solution)/shard_map/ppermute | solution.py:308
  20.6 12.1 %collective-permute-start.2 = (f32[4,128,128]{2,1,0:T(8,128)S(1)}, f32[4,128,128]{2,1,0:T(8,128)S(1)}, u32[]{:S(2)}, u32[]{:S(2)}) collective-permute-start(f32[4,128,128]{2,1,0:T(8,128)S(1)} %get-tuple-element.22), channel_id=1, source_target_pairs={{0,1},{1,2},{2,3},{3,4},{4,5},{5,6},{6,7},{7,8},{8,9},{9,10},{10,1... | collective-permute-start | bytes 786440 | tf_op jit(solution)/shard_map/ppermute | solution.py:308
  22.8 11.8 %collective-permute-start.3 = (f32[4,128,128]{2,1,0:T(8,128)S(1)}, f32[4,128,128]{2,1,0:T(8,128)S(1)}, u32[]{:S(2)}, u32[]{:S(2)}) collective-permute-start(f32[4,128,128]{2,1,0:T(8,128)S(1)} %get-tuple-element.23), channel_id=1, source_target_pairs={{1,0},{2,1},{3,2},{4,3},{5,4},{6,5},{7,6},{8,7},{9,8},{10,9},{11,1... | collective-permute-start | bytes 786440 | tf_op jit(solution)/shard_map/ppermute | solution.py:308
  37.1 118.8 %all-to-all-start = ((f32[8,520,128]{2,1,0:T(8,128)}), f32[8,520,128]{2,1,0:T(8,128)}, u32[]{:S(2)}, u32[]{:S(2)}) async-start(f32[8,520,128]{2,1,0:T(8,128)} %second_kernel.1.buf_ref), calls=%async_computation | async-start | bytes 4259840 | tf_op jit(solution)/shard_map/all_to_all | solution.py:362
  41.8 44.3 %copy-start = (f32[8,520,128]{2,1,0:T(8,128)S(1)}, f32[8,520,128]{2,1,0:T(8,128)}, u32[]{:S(2)}) copy-start(f32[8,520,128]{2,1,0:T(8,128)} %second_kernel.1.buf_ref) | copy-start | bytes 6389764
  41.8 44.3 %copy-start.1 = (f32[16,128,128]{2,1,0:T(8,128)S(1)}, f32[16,128,128]{2,1,0:T(8,128)}, u32[]{:S(2)}) copy-start(f32[16,128,128]{2,1,0:T(8,128)} %vel_ref.1) | copy-start | bytes 3145732
  41.8 38.2 %collective-permute-start.4 = (f32[4,16,16,128]{3,2,1,0:T(8,128)}, f32[4,16,16,128]{3,2,1,0:T(8,128)S(1)}, u32[]{:S(2)}, u32[]{:S(2)}) collective-permute-start(f32[4,16,16,128]{3,2,1,0:T(8,128)} %param.11), channel_id=1, source_target_pairs={{0,32},{32,0},{64,96},{96,64},{128,160},{160,128},{192,224},{224,1... | collective-permute-start | bytes 1572872 | tf_op jit(solution)/shard_map/ppermute | solution.py:326
  44.4 27.1 %collective-permute-start.8 = (f32[4,16,8,128]{3,2,1,0:T(8,128)S(1)}, f32[4,16,8,128]{3,2,1,0:T(8,128)S(1)}, u32[]{:S(2)}, u32[]{:S(2)}) collective-permute-start(f32[4,16,8,128]{3,2,1,0:T(8,128)S(1)} %get-tuple-element.39), channel_id=1, source_target_pairs={{0,64},{32,96},{64,128},{96,160},{128,192},{160,224},{192,0},{224,... | collective-permute-start | bytes 786440 | tf_op jit(solution)/shard_map/ppermute | solution.py:326
  45.0 27.1 %collective-permute-start.9 = (f32[4,16,8,128]{3,2,1,0:T(8,128)S(1)}, f32[4,16,8,128]{3,2,1,0:T(8,128)S(1)}, u32[]{:S(2)}, u32[]{:S(2)}) collective-permute-start(f32[4,16,8,128]{3,2,1,0:T(8,128)S(1)} %get-tuple-element.39), channel_id=1, source_target_pairs={{0,128},{32,160},{64,192},{96,224},{128,0},{160,32},{192,64},{224,... | collective-permute-start | bytes 786440 | tf_op jit(solution)/shard_map/ppermute | solution.py:326
  47.4 31.1 %collective-permute-start.10 = (f32[4,16,8,128]{3,2,1,0:T(8,128)S(1)}, f32[4,16,8,128]{3,2,1,0:T(8,128)S(1)}, u32[]{:S(2)}, u32[]{:S(2)}) collective-permute-start(f32[4,16,8,128]{3,2,1,0:T(8,128)S(1)} %get-tuple-element.39), channel_id=1, source_target_pairs={{0,192},{32,224},{64,0},{96,32},{128,64},{160,96},{192,128},{224,1... | collective-permute-start | bytes 786440 | tf_op jit(solution)/shard_map/ppermute | solution.py:326
  72.1 8.0 %copy-start.5 = (f32[4,16,8,128]{3,2,1,0:T(8,128)}, f32[4,16,8,128]{3,2,1,0:T(8,128)S(1)}, u32[]{:S(2)}) copy-start(f32[4,16,8,128]{3,2,1,0:T(8,128)S(1)} %collective-permute-done.9) | copy-start | bytes 786436
  78.5 2.4 %copy-start.7 = (f32[4,16,8,128]{3,2,1,0:T(8,128)}, f32[4,16,8,128]{3,2,1,0:T(8,128)S(1)}, u32[]{:S(2)}) copy-start(f32[4,16,8,128]{3,2,1,0:T(8,128)S(1)} %collective-permute-done.10) | copy-start | bytes 786436
  79.5 19.9 %collective-permute-start.11 = (f32[3,4,16,8,128]{4,3,2,1,0:T(8,128)}, f32[3,4,16,8,128]{4,3,2,1,0:T(8,128)}, u32[]{:S(2)}, u32[]{:S(2)}) collective-permute-start(f32[3,4,16,8,128]{4,3,2,1,0:T(8,128)} %pad_maximum_fusion), channel_id=1, source_target_pairs={{0,32},{32,0},{64,96},{96,64},{128,160},{160,128},{192,224},{224,1... | collective-permute-start | bytes 2359304 | tf_op jit(solution)/shard_map/ppermute | solution.py:326
  80.1 0.9 copy-start.3
  81.8 26.1 %collective-permute-start.7 = (f32[2,4,16,8,128]{4,3,2,1,0:T(8,128)}, f32[2,4,16,8,128]{4,3,2,1,0:T(8,128)}, u32[]{:S(2)}, u32[]{:S(2)}) collective-permute-start(f32[2,4,16,8,128]{4,3,2,1,0:T(8,128)} %pad_maximum_fusion.1), channel_id=1, source_target_pairs={{0,64},{32,96},{64,128},{96,160},{128,192},{160,224},{192,0},{224,... | collective-permute-start | bytes 1572872 | tf_op jit(solution)/shard_map/ppermute | solution.py:326
  84.0 29.1 %collective-permute-start.5 = (f32[2,4,16,8,128]{4,3,2,1,0:T(8,128)}, f32[2,4,16,8,128]{4,3,2,1,0:T(8,128)}, u32[]{:S(2)}, u32[]{:S(2)}) collective-permute-start(f32[2,4,16,8,128]{4,3,2,1,0:T(8,128)} %pad_maximum_fusion.1), channel_id=1, source_target_pairs={{0,128},{32,160},{64,192},{96,224},{128,0},{160,32},{192,64},{224,... | collective-permute-start | bytes 1572872 | tf_op jit(solution)/shard_map/ppermute | solution.py:326
  85.9 27.3 %collective-permute-start.6 = (f32[2,4,16,8,128]{4,3,2,1,0:T(8,128)}, f32[2,4,16,8,128]{4,3,2,1,0:T(8,128)}, u32[]{:S(2)}, u32[]{:S(2)}) collective-permute-start(f32[2,4,16,8,128]{4,3,2,1,0:T(8,128)} %pad_maximum_fusion.1), channel_id=1, source_target_pairs={{0,192},{32,224},{64,0},{96,32},{128,64},{160,96},{192,128},{224,1... | collective-permute-start | bytes 1572872 | tf_op jit(solution)/shard_map/ppermute | solution.py:326
  86.1 1.0 copy-start.2
  87.2 1.0 copy-start.4
  88.2 0.9 copy-start.6
  89.1 0.9 copy-start.8
  117.5 9.2 %collective-permute-start.12 = (f32[56,512]{1,0:T(8,128)S(1)}, f32[56,512]{1,0:T(8,128)S(1)}, u32[]{:S(2)}, u32[]{:S(2)}) collective-permute-start(f32[56,512]{1,0:T(8,128)S(1)} %get-tuple-element.35), channel_id=1, source_target_pairs={{0,1},{1,2},{2,3},{3,4},{4,5},{5,6},{6,7},{7,8},{8,9},{9,10},{10,1... | collective-permute-start | bytes 344072 | tf_op jit(solution)/shard_map/ppermute | solution.py:308
  119.5 10.1 %collective-permute-start.13 = (f32[56,512]{1,0:T(8,128)S(1)}, f32[56,512]{1,0:T(8,128)S(1)}, u32[]{:S(2)}, u32[]{:S(2)}) collective-permute-start(f32[56,512]{1,0:T(8,128)S(1)} %get-tuple-element.36), channel_id=1, source_target_pairs={{1,0},{2,1},{3,2},{4,3},{5,4},{6,5},{7,6},{8,7},{9,8},{10,9},{11,1... | collective-permute-start | bytes 344072 | tf_op jit(solution)/shard_map/ppermute | solution.py:308
  130.6 8.7 %collective-permute-start.18 = (f32[96,512]{1,0:T(8,128)}, f32[96,512]{1,0:T(8,128)}, u32[]{:S(2)}, u32[]{:S(2)}) collective-permute-start(f32[96,512]{1,0:T(8,128)} %late_kernel.1.refs_0_), channel_id=1, source_target_pairs={{0,32},{32,0},{64,96},{96,64},{128,160},{160,128},{192,224},{224,1... | collective-permute-start | bytes 589832 | tf_op jit(solution)/shard_map/ppermute | solution.py:326
  130.6 9.6 %collective-permute-start.19 = (f32[96,512]{1,0:T(8,128)}, f32[96,512]{1,0:T(8,128)}, u32[]{:S(2)}, u32[]{:S(2)}) collective-permute-start(f32[96,512]{1,0:T(8,128)} %late_kernel.1.refs_0_), channel_id=1, source_target_pairs={{0,64},{32,96},{64,0},{96,32},{128,192},{160,224},{192,128},{224,1... | collective-permute-start | bytes 589832 | tf_op jit(solution)/shard_map/ppermute | solution.py:326
  130.6 25.4 %collective-permute-start.20 = (f32[96,512]{1,0:T(8,128)}, f32[96,512]{1,0:T(8,128)}, u32[]{:S(2)}, u32[]{:S(2)}) collective-permute-start(f32[96,512]{1,0:T(8,128)} %late_kernel.1.refs_0_), channel_id=1, source_target_pairs={{0,192},{32,224},{64,128},{96,160},{128,64},{160,96},{192,0},{224,... | collective-permute-start | bytes 589832 | tf_op jit(solution)/shard_map/ppermute | solution.py:326
  134.3 30.0 %collective-permute-start.14 = (f32[96,512]{1,0:T(8,128)}, f32[96,512]{1,0:T(8,128)}, u32[]{:S(2)}, u32[]{:S(2)}) collective-permute-start(f32[96,512]{1,0:T(8,128)} %late_kernel.1.refs_0_), channel_id=1, source_target_pairs={{0,128},{32,160},{64,192},{96,224},{128,0},{160,32},{192,64},{224,... | collective-permute-start | bytes 589832 | tf_op jit(solution)/shard_map/ppermute | solution.py:326
  135.8 28.5 %collective-permute-start.15 = (f32[96,512]{1,0:T(8,128)}, f32[96,512]{1,0:T(8,128)}, u32[]{:S(2)}, u32[]{:S(2)}) collective-permute-start(f32[96,512]{1,0:T(8,128)} %late_kernel.1.refs_0_), channel_id=1, source_target_pairs={{0,160},{32,128},{64,224},{96,192},{128,32},{160,0},{192,96},{224,... | collective-permute-start | bytes 589832 | tf_op jit(solution)/shard_map/ppermute | solution.py:326
  139.3 25.0 %collective-permute-start.16 = (f32[96,512]{1,0:T(8,128)}, f32[96,512]{1,0:T(8,128)}, u32[]{:S(2)}, u32[]{:S(2)}) collective-permute-start(f32[96,512]{1,0:T(8,128)} %late_kernel.1.refs_0_), channel_id=1, source_target_pairs={{0,96},{32,64},{64,32},{96,0},{128,224},{160,192},{192,160},{224,1... | collective-permute-start | bytes 589832 | tf_op jit(solution)/shard_map/ppermute | solution.py:326
  140.2 24.1 %collective-permute-start.17 = (f32[96,512]{1,0:T(8,128)}, f32[96,512]{1,0:T(8,128)}, u32[]{:S(2)}, u32[]{:S(2)}) collective-permute-start(f32[96,512]{1,0:T(8,128)} %late_kernel.1.refs_0_), channel_id=1, source_target_pairs={{0,224},{32,192},{64,160},{96,128},{128,96},{160,64},{192,32},{224... | collective-permute-start | bytes 589832 | tf_op jit(solution)/shard_map/ppermute | solution.py:326
